TPU v7x, 32 devices: a whole 2x2x4 slice. The times are simulated.
32 devices in a mesh: table: 8 (over z, y), batch: 4 (over x, core).
Axes of the slice: x: 2, y: 2, z: 4, core: 2. Of those that a mesh axis runs over, the one named last changes fastest.
Arguments:
- tokens: bfloat16 [96, 512, 768], P(('table', 'batch')), may hold values from -6 to 6
- row_blocks: int32 [96], P(('table', 'batch')), may hold values from 8 to 64, as said below
- block_fill: int32 [96, 64], P(('table', 'batch')), may hold values from 4 to 8
- row_table: int32 [96], P('table'), may hold values from 0 to 3
- class_count: int32 [32], P(('table', 'batch')), may hold values from 2 to 128, as said below
- merge_w: bfloat16 [768, 768], P(('table', 'batch')), may hold values from -0.21875 to 0.21875
- qkv_w: bfloat16 [768, 2304], P(('table', 'batch')), may hold values from -0.21875 to 0.21875
- query_bias: bfloat16 [768], P(('table', 'batch')), may hold values from -3 to 3
- value_bias: bfloat16 [768], P(('table', 'batch')), may hold values from -3 to 3
- out_w: bfloat16 [768, 768], P(('table', 'batch')), may hold values from -2.5 to 2.5
- out_bias: bfloat16 [768], P(('table', 'batch')), may hold values from -3 to 3
- gain_one: bfloat16 [768], P(('table', 'batch')), may hold values from 0.5 to 1.5
- shift_one: bfloat16 [768], P(('table', 'batch')), may hold values from -3 to 3
- up_w: bfloat16 [768, 3072], P(('table', 'batch')), may hold values from -0.21875 to 0.21875
- up_bias: bfloat16 [3072], P(('table', 'batch')), may hold values from -3 to 3
- down_w: bfloat16 [3072, 768], P(('table', 'batch')), may hold values from -0.109375 to 0.109375
- down_bias: bfloat16 [768], P(('table', 'batch')), may hold values from -3 to 3
- gain_two: bfloat16 [768], P(('table', 'batch')), may hold values from 0.5 to 1.5
- shift_two: bfloat16 [768], P(('table', 'batch')), may hold values from -3 to 3
- head_w: bfloat16 [32, 768, 128], P(('table', 'batch')), may hold values from -0.21875 to 0.21875
- cotangent: bfloat16 [96, 512, 768], P(('table', 'batch')), may hold values from -6 to 6
- logit_cotangent: float32 [96, 128], P(('table', 'batch')), may hold values from -6 to 6
Outputs:
- layer_out: bfloat16 [96, 512, 768], P(('table', 'batch'))
- logits: float32 [96, 128], P(('table', 'batch'))
- grad_input: bfloat16 [96, 512, 768], P(('table', 'batch'))
- grad_merge_w: float32 [768, 768], P(('table', 'batch'))
- grad_qkv_w: float32 [768, 2304], P(('table', 'batch'))
- grad_query_bias: float32 [768], P(('table', 'batch'))
- grad_value_bias: float32 [768], P(('table', 'batch'))
- grad_out_w: float32 [768, 768], P(('table', 'batch'))
- grad_out_bias: float32 [768], P(('table', 'batch'))
- grad_gain_one: float32 [768], P(('table', 'batch'))
- grad_shift_one: float32 [768], P(('table', 'batch'))
- grad_up_w: float32 [768, 3072], P(('table', 'batch'))
- grad_up_bias: float32 [3072], P(('table', 'batch'))
- grad_down_w: float32 [3072, 768], P(('table', 'batch'))
- grad_down_bias: float32 [768], P(('table', 'batch'))
- grad_gain_two: float32 [768], P(('table', 'batch'))
- grad_shift_two: float32 [768], P(('table', 'batch'))
- grad_head_w: float32 [32, 768, 128], P(('table', 'batch'))
- root_squares: float32 [5], replicated
Inputs may be any that keep to these rules, and one draw needn't show every extreme that they name: A row's live positions lie in its first row_blocks word groups; some row has 64 and some 8. Head of a row is its table group's index times the batch axis's size plus row_table. `class_count`: some table has 128 classes and some 2.
All inputs are finite; a program needn't handle non-finite values.
Results may differ from a plain program's by a relative error of at most 0.018.
The roundings to bfloat16 on the way count: a program that leaves them out, or rounds other values in their place, can miss the bound.
Values may be sent and summed in bfloat16 or wider, within the bound.
A program may use at most 256 MiB of HBM per device.

v0:
```python
import jax
import jax.numpy as jnp
from jax import lax
from jax.sharding import PartitionSpec as P

HEADS = 12
BLOCK = 8


NORM_EPS = 1e-05
MASKED = -1000000000.0
PRECISE = lax.Precision.HIGHEST


def product(left, right):
    return jnp.dot(left, right, preferred_element_type=jnp.float32)


def inner_rows(left, right, precision=None):
    return lax.dot_general(
        left,
        right,
        (((0,), (0,)), ((), ())),
        precision=precision,
        preferred_element_type=jnp.float32,
    )


def outer_cols(left, right, precision=None):
    return lax.dot_general(
        left,
        right,
        (((1,), (1,)), ((), ())),
        precision=precision,
        preferred_element_type=jnp.float32,
    )


def valid_tokens(row_blocks, block_fill, seq_len):
    position = jnp.arange(seq_len, dtype=jnp.int32)
    fill_tok = jnp.repeat(block_fill, BLOCK, axis=1)
    live_mask = ((position // BLOCK)[None, :] < row_blocks[:, None]) & (
        (position % BLOCK)[None, :] < fill_tok
    )
    return live_mask.astype(jnp.float32)


def norm_forward(hidden, norm_gain, norm_shift):
    average = jnp.mean(hidden, axis=-1, keepdims=True)
    centered = hidden - average
    variance = jnp.mean(centered * centered, axis=-1, keepdims=True)
    inv_std = lax.rsqrt(variance + NORM_EPS)
    standard = centered * inv_std
    return (standard * norm_gain + norm_shift, standard, inv_std)


def norm_backward(grad_norm, standard, inv_std, norm_gain):
    scaled = grad_norm * norm_gain
    grad_hidden = inv_std * (
        scaled
        - jnp.mean(scaled, axis=-1, keepdims=True)
        - standard * jnp.mean(scaled * standard, axis=-1, keepdims=True)
    )
    return (grad_hidden, jnp.sum(grad_norm * standard, axis=0), jnp.sum(grad_norm, axis=0))


def gelu_slope(values):
    cumulative = 0.5 * (1.0 + lax.erf(values * 0.7071067811865476))
    density = jnp.exp(-0.5 * values * values) * 0.3989422804014327
    return cumulative + values * density


def body(
    tokens,
    row_blocks,
    block_fill,
    row_table,
    class_count,
    merge_w,
    qkv_w,
    query_bias,
    value_bias,
    out_w,
    out_bias,
    gain_one,
    shift_one,
    up_w,
    up_bias,
    down_w,
    down_bias,
    gain_two,
    shift_two,
    head_w,
    cotangent,
    logit_cotangent,
):
    count_rows, seq_len, width = tokens.shape
    token_count = count_rows * seq_len
    head_size = width // HEADS
    block_count = seq_len // BLOCK
    gathered = (
        lax.all_gather(merge_w, ("table", "batch"), axis=0, tiled=True),
        lax.all_gather(qkv_w, ("table", "batch"), axis=0, tiled=True),
        lax.all_gather(query_bias, ("table", "batch"), axis=0, tiled=True),
        lax.all_gather(value_bias, ("table", "batch"), axis=0, tiled=True),
        lax.all_gather(out_w, ("table", "batch"), axis=0, tiled=True),
        lax.all_gather(out_bias, ("table", "batch"), axis=0, tiled=True),
        lax.all_gather(gain_one, ("table", "batch"), axis=0, tiled=True),
        lax.all_gather(shift_one, ("table", "batch"), axis=0, tiled=True),
        lax.all_gather(up_w, ("table", "batch"), axis=0, tiled=True),
        lax.all_gather(up_bias, ("table", "batch"), axis=0, tiled=True),
        lax.all_gather(down_w, ("table", "batch"), axis=0, tiled=True),
        lax.all_gather(down_bias, ("table", "batch"), axis=0, tiled=True),
        lax.all_gather(gain_two, ("table", "batch"), axis=0, tiled=True),
        lax.all_gather(shift_two, ("table", "batch"), axis=0, tiled=True),
    )
    merge_full, qkv_full, out_full, up_full, down_full = (
        gathered[0],
        gathered[1],
        gathered[4],
        gathered[8],
        gathered[10],
    )
    query_vec = gathered[2].astype(jnp.float32)
    value_vec = gathered[3].astype(jnp.float32)
    out_bias_vec = gathered[5].astype(jnp.float32)
    gain_one_vec = gathered[6].astype(jnp.float32)
    shift_one_vec = gathered[7].astype(jnp.float32)
    up_bias_vec = gathered[9].astype(jnp.float32)
    down_bias_vec = gathered[11].astype(jnp.float32)
    gain_two_vec = gathered[12].astype(jnp.float32)
    shift_two_vec = gathered[13].astype(jnp.float32)
    live_mask = valid_tokens(row_blocks, block_fill, seq_len)
    live_flat = live_mask.reshape(-1, 1)
    tok_flat = tokens.reshape(token_count, width)
    tok_wide = tok_flat.astype(jnp.float32)
    blocks_x = tokens.reshape(count_rows, block_count, BLOCK, width)
    live_blk = live_mask.reshape(count_rows, block_count, 1, BLOCK)
    merge_scale = width ** (-0.5)
    merge_query = product(tok_flat, merge_full).astype(jnp.bfloat16)
    blocks_q = merge_query.reshape(count_rows, block_count, BLOCK, width)
    merge_scores = (
        jnp.einsum("rbid,rbjd->rbij", blocks_q, blocks_x, preferred_element_type=jnp.float32)
        * merge_scale
    )
    merge_probs = jax.nn.softmax(jnp.where(live_blk > 0, merge_scores, MASKED), axis=-1)
    merge_low = merge_probs.astype(jnp.bfloat16)
    merged_out = (
        jnp.einsum(
            "rbij,rbjd->rbid", merge_low, blocks_x, preferred_element_type=jnp.float32
        ).reshape(token_count, width)
        * live_flat
    )
    hidden_one = tok_wide + merged_out
    attn_in = hidden_one.astype(jnp.bfloat16)
    qkv_bias = jnp.concatenate([query_vec, jnp.zeros_like(query_vec), value_vec])
    packed_qkv = (product(attn_in, qkv_full) + qkv_bias).astype(jnp.bfloat16)
    queries = packed_qkv[:, :width].reshape(count_rows, seq_len, HEADS, head_size)
    keys_part = packed_qkv[:, width : 2 * width].reshape(count_rows, seq_len, HEADS, head_size)
    values = packed_qkv[:, 2 * width :].reshape(count_rows, seq_len, HEADS, head_size)
    score_scale = head_size ** (-0.5)
    key_live = live_mask[:, None, None, :] > 0
    masked = jnp.where(
        key_live,
        jnp.einsum("rqhe,rkhe->rhqk", queries, keys_part, preferred_element_type=jnp.float32)
        * score_scale,
        MASKED,
    )
    row_top = jnp.max(masked, axis=-1, keepdims=True)
    exp_terms = jnp.exp(masked - row_top)
    totals = jnp.sum(exp_terms, axis=-1, keepdims=True)
    attn_probs = exp_terms / totals
    log_total = row_top + jnp.log(totals)
    probs_low = attn_probs.astype(jnp.bfloat16)
    context = (
        jnp.einsum("rhqk,rkhe->rqhe", probs_low, values, preferred_element_type=jnp.float32)
        .astype(jnp.bfloat16)
        .reshape(token_count, width)
    )
    attn_branch = product(context, out_full) + out_bias_vec
    norm_one, standard_one, inv_one = norm_forward(
        hidden_one + attn_branch, gain_one_vec, shift_one_vec
    )
    ffn_in = norm_one.astype(jnp.bfloat16)
    up_pre = product(ffn_in, up_full) + up_bias_vec
    activated = jax.nn.gelu(up_pre, approximate=False).astype(jnp.bfloat16)
    down_branch = product(activated, down_full) + down_bias_vec
    normed_two, standard_two, inv_two = norm_forward(
        norm_one + down_branch, gain_two_vec, shift_two_vec
    )
    layer_out = (normed_two * live_flat).astype(jnp.bfloat16)
    cls_rows = layer_out.reshape(count_rows, seq_len, width)[:, 0, :]
    group_cls = lax.all_gather(cls_rows, "batch", axis=0, tiled=True)
    owner_mask = (row_table == lax.axis_index("batch")).astype(jnp.float32)[:, None]
    class_live = (jnp.arange(head_w.shape[2], dtype=jnp.int32) < class_count[0]).astype(
        jnp.float32
    )[None, :]
    route_mask = owner_mask * class_live
    head_low = head_w[0]
    group_logits = product(group_cls, head_low) * route_mask
    logits = lax.psum_scatter(group_logits, "batch", scatter_dimension=0, tiled=True)
    out_wide = layer_out.astype(jnp.float32)
    square_sums = jnp.stack(
        [
            jnp.sum(live_flat * field * field)
            for field in (tok_wide, merged_out, attn_branch, down_branch, out_wide)
        ]
    )
    total_squares, total_live = lax.psum((square_sums, jnp.sum(live_mask)), ("table", "batch"))
    root_squares = jnp.sqrt(total_squares / (total_live * width))
    group_dlog = lax.all_gather(logit_cotangent, "batch", axis=0, tiled=True) * route_mask
    grad_head = inner_rows(group_cls.astype(jnp.float32), group_dlog, PRECISE)[None]
    cls_terms = outer_cols(group_dlog, head_low.astype(jnp.float32), PRECISE)
    cls_grad = lax.psum_scatter(
        cls_terms.astype(jnp.bfloat16), "batch", scatter_dimension=0, tiled=True
    ).astype(jnp.float32)
    grad_y = cotangent.astype(jnp.float32).at[:, 0, :].add(cls_grad).reshape(token_count, width)
    merge_back, qkv_back, out_back, up_back, down_back = (
        lax.all_gather(merge_w, ("table", "batch"), axis=0, tiled=True),
        lax.all_gather(qkv_w, ("table", "batch"), axis=0, tiled=True),
        lax.all_gather(out_w, ("table", "batch"), axis=0, tiled=True),
        lax.all_gather(up_w, ("table", "batch"), axis=0, tiled=True),
        lax.all_gather(down_w, ("table", "batch"), axis=0, tiled=True),
    )
    grad_three, grad_gain_two, grad_shift_two = norm_backward(
        grad_y * live_flat, standard_two, inv_two, gain_two_vec
    )
    grad_down = grad_three.astype(jnp.bfloat16)
    grad_down_w = inner_rows(activated, grad_down)
    grad_down_bias = jnp.sum(grad_down.astype(jnp.float32), axis=0)
    grad_up = (outer_cols(grad_down, down_back) * gelu_slope(up_pre)).astype(jnp.bfloat16)
    grad_up_w = inner_rows(ffn_in, grad_up)
    grad_up_bias = jnp.sum(grad_up.astype(jnp.float32), axis=0)
    grad_norm_one = grad_three + outer_cols(grad_up, up_back)
    grad_two, grad_gain_one, grad_shift_one = norm_backward(
        grad_norm_one, standard_one, inv_one, gain_one_vec
    )
    grad_attn = grad_two.astype(jnp.bfloat16)
    grad_out_w = inner_rows(context, grad_attn)
    grad_out_bias = jnp.sum(grad_attn.astype(jnp.float32), axis=0)
    grad_context = (
        outer_cols(grad_attn, out_back)
        .astype(jnp.bfloat16)
        .reshape(count_rows, seq_len, HEADS, head_size)
    )
    masked_again = jnp.where(
        key_live,
        jnp.einsum("rqhe,rkhe->rhqk", queries, keys_part, preferred_element_type=jnp.float32)
        * score_scale,
        MASKED,
    )
    probs_again = jnp.exp(masked_again - log_total)
    grad_values = jnp.einsum(
        "rhqk,rqhe->rkhe",
        probs_again.astype(jnp.bfloat16),
        grad_context,
        preferred_element_type=jnp.float32,
    )
    grad_probs = jnp.einsum(
        "rqhe,rkhe->rhqk", grad_context, values, preferred_element_type=jnp.float32
    )
    grad_scores = (
        probs_again * (grad_probs - jnp.sum(probs_again * grad_probs, axis=-1, keepdims=True))
    ).astype(jnp.bfloat16)
    grad_queries = (
        jnp.einsum("rhqk,rkhe->rqhe", grad_scores, keys_part, preferred_element_type=jnp.float32)
        * score_scale
    )
    grad_keys = (
        jnp.einsum("rhqk,rqhe->rkhe", grad_scores, queries, preferred_element_type=jnp.float32)
        * score_scale
    )
    grad_packed = jnp.concatenate(
        [
            grad_queries.reshape(token_count, width),
            grad_keys.reshape(token_count, width),
            grad_values.reshape(token_count, width),
        ],
        axis=1,
    ).astype(jnp.bfloat16)
    grad_qkv_w = inner_rows(attn_in, grad_packed)
    grad_query_bias = jnp.sum(grad_packed[:, :width].astype(jnp.float32), axis=0)
    grad_value_bias = jnp.sum(grad_packed[:, 2 * width :].astype(jnp.float32), axis=0)
    grad_one = grad_two + outer_cols(grad_packed, qkv_back)
    grad_merged = (
        (grad_one * live_flat).astype(jnp.bfloat16).reshape(count_rows, block_count, BLOCK, width)
    )
    grad_blocks = jnp.einsum(
        "rbij,rbid->rbjd", merge_low, grad_merged, preferred_element_type=jnp.float32
    )
    grad_merge_probs = jnp.einsum(
        "rbid,rbjd->rbij", grad_merged, blocks_x, preferred_element_type=jnp.float32
    )
    grad_merge_scores = jnp.where(
        live_blk > 0,
        merge_probs
        * (grad_merge_probs - jnp.sum(merge_probs * grad_merge_probs, axis=-1, keepdims=True)),
        0.0,
    ).astype(jnp.bfloat16)
    grad_merge_query = (
        (
            jnp.einsum(
                "rbij,rbjd->rbid", grad_merge_scores, blocks_x, preferred_element_type=jnp.float32
            )
            * merge_scale
        )
        .astype(jnp.bfloat16)
        .reshape(token_count, width)
    )
    grad_blocks = (
        grad_blocks
        + jnp.einsum(
            "rbij,rbid->rbjd", grad_merge_scores, blocks_q, preferred_element_type=jnp.float32
        )
        * merge_scale
    )
    grad_merge_w = inner_rows(tok_flat, grad_merge_query)
    grad_input = (
        (
            grad_one
            + grad_blocks.reshape(token_count, width)
            + outer_cols(grad_merge_query, merge_back)
        )
        .astype(jnp.bfloat16)
        .reshape(count_rows, seq_len, width)
    )
    owned = (
        lax.psum_scatter(grad_merge_w, ("table", "batch"), scatter_dimension=0, tiled=True),
        lax.psum_scatter(grad_qkv_w, ("table", "batch"), scatter_dimension=0, tiled=True),
        lax.psum_scatter(grad_query_bias, ("table", "batch"), scatter_dimension=0, tiled=True),
        lax.psum_scatter(grad_value_bias, ("table", "batch"), scatter_dimension=0, tiled=True),
        lax.psum_scatter(grad_out_w, ("table", "batch"), scatter_dimension=0, tiled=True),
        lax.psum_scatter(grad_out_bias, ("table", "batch"), scatter_dimension=0, tiled=True),
        lax.psum_scatter(grad_gain_one, ("table", "batch"), scatter_dimension=0, tiled=True),
        lax.psum_scatter(grad_shift_one, ("table", "batch"), scatter_dimension=0, tiled=True),
        lax.psum_scatter(grad_up_w, ("table", "batch"), scatter_dimension=0, tiled=True),
        lax.psum_scatter(grad_up_bias, ("table", "batch"), scatter_dimension=0, tiled=True),
        lax.psum_scatter(grad_down_w, ("table", "batch"), scatter_dimension=0, tiled=True),
        lax.psum_scatter(grad_down_bias, ("table", "batch"), scatter_dimension=0, tiled=True),
        lax.psum_scatter(grad_gain_two, ("table", "batch"), scatter_dimension=0, tiled=True),
        lax.psum_scatter(grad_shift_two, ("table", "batch"), scatter_dimension=0, tiled=True),
    )
    return (
        layer_out.reshape(count_rows, seq_len, width),
        logits,
        grad_input,
        owned[0],
        owned[1],
        owned[2],
        owned[3],
        owned[4],
        owned[5],
        owned[6],
        owned[7],
        owned[8],
        owned[9],
        owned[10],
        owned[11],
        owned[12],
        owned[13],
        grad_head,
        root_squares,
    )


def solution(mesh):
    placed = (
        P(("table", "batch"), None, None),
        P(("table", "batch")),
        P(("table", "batch"), None),
        P("table"),
        P(("table", "batch")),
        P(("table", "batch"), None),
        P(("table", "batch"), None),
        P(("table", "batch")),
        P(("table", "batch")),
        P(("table", "batch"), None),
        P(("table", "batch")),
        P(("table", "batch")),
        P(("table", "batch")),
        P(("table", "batch"), None),
        P(("table", "batch")),
        P(("table", "batch"), None),
        P(("table", "batch")),
        P(("table", "batch")),
        P(("table", "batch")),
        P(("table", "batch"), None, None),
        P(("table", "batch"), None, None),
        P(("table", "batch"), None),
    )
    return jax.shard_map(
        body,
        mesh=mesh,
        in_specs=placed,
        out_specs=(
            P(("table", "batch"), None, None),
            P(("table", "batch"), None),
            P(("table", "batch"), None, None),
            P(("table", "batch"), None),
            P(("table", "batch"), None),
            P(("table", "batch")),
            P(("table", "batch")),
            P(("table", "batch"), None),
            P(("table", "batch")),
            P(("table", "batch")),
            P(("table", "batch")),
            P(("table", "batch"), None),
            P(("table", "batch")),
            P(("table", "batch"), None),
            P(("table", "batch")),
            P(("table", "batch")),
            P(("table", "batch")),
            P(("table", "batch"), None, None),
            P(),
        ),
        check_vma=False,
    )
```

profile of v0, /device:TPU:0, one launch (start us, length us, event | category | flops | bytes accessed | tf_op | source)
XLA Modules:
  0.0 1115.7 jit_solution(6391904415945860554)
XLA Ops:
  20.0 42.4 %all-reduce.21 = (bf16[768]{0:T(1024)(128)(2,1)S(1)}, bf16[768]{0:T(1024)(128)(2,1)S(1)}, bf16[768]{0:T(1024)(128)(2,1)S(1)}, bf16[768]{0:T(1024)(128)(2,1)S(1)}...) all-reduce(bf16[768]{0:T(1024)(128)(2,1)S(1)} %dynamic-update-slice, ...), channel_id=1, replica_groups=mesh['table'=8,'batch'=4] {'table','batch'}, use_global_device_ids=true, to_apply=%add.1 | all-reduce | flops 9216 | bytes 36864
  64.7 5.6 all-gather.1
  72.0 12.8 %all-reduce.10 = bf16[12,768]{1,0:T(8,128)(2,1)S(1)} all-reduce(bf16[12,768]{1,0:T(8,128)(2,1)S(1)} %convolution_convert_fusion.2), channel_id=4, replica_groups=mesh['table'=8,'batch'=4] {'batch'}, use_global_device_ids=true, to_apply=%region_9.10.clone | all-reduce | flops 9216 | bytes 36864
  85.5 4.2 convert_element_type.179
  93.4 4.4 multiply_reduce_fusion.8
  106.5 3.8 fusion.26
  110.3 4.7 fusion.35
  115.0 14.5 %all-gather.10.cloned.1.call-done = bf16[768,2304]{1,0:T(8,128)(2,1)} async-done(((bf16[24,2304]{1,0:T(8,128)(2,1)}), bf16[768,2304]{1,0:T(8,128)(2,1)}) %all-gather.10.cloned.1.call-update) | async-done | bytes 3538960 | tf_op jit(solution)/shard_map/all_gather | solution.py:103
  129.5 8.2 add_convert_fusion
  140.9 8.2 reshape.440
  149.0 7.3 copy.148
  156.3 8.2 reshape.439
  164.5 7.4 copy.147
  171.9 8.2 reshape.438
  180.1 7.8 copy.149
  187.8 18.4 %fusion.24 = (f32[3,12,512]{2,1,0:T(8,128)S(1)}, f32[3,12,512,512]{2,3,1,0:T(8,128)}) fusion(pred[3,512]{1,0:T(4,128)(4,1)S(1)} %get-tuple-element.169, bf16[3,512,12,64]{1,3,2,0:T(8,128)(2,1)} %copy.147, bf16[3,512,12,64]{1,3,2,0:T(8,128)(2,1)} %copy.148), kind=kOutput, calls=%fused_computation.40 | convolution fusion | flops 1236252672 | bytes 42542592 | tf_op jit(solution)/shard_map/rqhe,rkhe->rhqk/dot_general | solution.py:165
  206.3 16.1 %fusion.2 = f32[3,12,512]{2,1,0:T(8,128)S(1)} fusion(f32[3,12,512]{2,1,0:T(8,128)S(1)} %get-tuple-element.179, f32[3,12,512,512]{2,3,1,0:T(8,128)} %get-tuple-element.180, pred[3,512]{1,0:T(4,128)(4,1)S(1)} %get-tuple-element.169), kind=kLoop, calls=%fused_computation.8 | loop fusion | flops 37730304 | bytes 37897728 | tf_op jit(solution)/shard_map/reduce_sum | solution.py:171
  223.1 19.3 %convert_bitcast_fusion.1 = bf16[3,512,12,64]{1,3,2,0:T(8,128)(2,1)} fusion(bf16[3,512,12,64]{1,3,2,0:T(8,128)(2,1)} %copy.149, f32[3,12,512]{2,1,0:T(8,128)S(1)} %fusion.2, f32[3,12,512]{2,1,0:T(8,128)S(1)} %get-tuple-element.179, f32[3,12,512,512]{2,3,1,0:T(8,128)} %get-tuple-element.180, pred[3,512]{1,0:T(4,128)(4,1)S(1)} %get-tuple-element.169), kind=kOutput, calls=%fused_computation.102 | convolution fusion | flops 1256325120 | bytes 42616320 | tf_op jit(solution)/shard_map/rhqk,rkhe->rqhe/dot_general | solution.py:176
  248.3 8.4 fusion.114
  259.7 53.2 %fusion.6 = (bf16[1536,3072]{1,0:T(8,128)(2,1)}, f32[1536,3072]{1,0:T(8,128)}) fusion(f32[3072]{0:T(1024)S(1)} %copy-done.49, bf16[768,3072]{1,0:T(8,128)(2,1)} %all-gather.14.cloned.1.call-done, f32[1536,768]{1,0:T(8,128)} %copy-done.3, f32[768]{0:T(1024)S(1)} %copy-done.55, f32[768]{0:T(1024)S(1)} %copy-done.45, f32[1536]{0:T(1024)S(1)} %add_rsqrt_fusion.1, ...), kind=kOutput, calls=%fused_computation.14 | convolution fusion | flops 7565082624 | bytes 37779456 | tf_op jit(solution)/shard_map/dot_general | solution.py:16
  315.2 13.3 %fusion.113 = (f32[1536]{0:T(1024)S(1)}, f32[1536,768]{1,0:T(8,128)S(1)}, f32[1536,768]{1,0:T(8,128)S(1)}) fusion(f32[768]{0:T(1024)S(1)} %copy-done.46, f32[768]{0:T(1024)S(1)} %copy-done.55, f32[768]{0:T(1024)S(1)} %copy-done.45, f32[1536]{0:T(1024)S(1)} %add_rsqrt_fusion.1, f32[1536,768]{1,0:T(8,128)} %copy-done.3, ...), kind=kOutput, calls=%fused_computation.197 | convolution fusion | flops 7256013312 | bytes 28339200 | tf_op jit(solution)/shard_map/dot_general | solution.py:16
  329.3 6.5 fusion.29
  338.3 20.6 %convert_reduce_fusion = (f32[3072]{0:T(1024)}, bf16[1536,3072]{1,0:T(8,128)(2,1)}) fusion(f32[1536,3072]{1,0:T(8,128)} %get-tuple-element.183, f32[3072]{0:T(1024)S(1)} %copy-done.49, bf16[3072,768]{1,0:T(8,128)(2,1)} %all-gather.16.cloned.1.call-done, f32[1536,768]{1,0:T(8,128)S(1)} %get-tuple-element.161), kind=kOutput, calls=%fused_computation.22 | convolution fusion | flops 7310275584 | bytes 37773312 | tf_op jit(solution)/shard_map/dot_general | solution.py:30
  358.9 14.0 %multiply_reduce_fusion.2 = (f32[768]{0:T(1024)}, f32[1536]{0:T(1024)S(1)}, f32[1536]{0:T(1024)S(1)}, f32[768]{0:T(1024)}, f32[1536,768]{1,0:T(8,128)S(1)}) fusion(f32[1536,768]{1,0:T(8,128)S(1)} %bitcast.151, f32[1536]{0:T(1024)S(1)} %add_rsqrt_fusion.1, f32[1536]{0:T(1024)S(1)} %broadcast_multiply_fusion.5, f32[768]{0:T(1024)S(1)} %copy-done.45, ...), kind=kOutput, calls=%fused_computation.60 | convolution fusion | flops 7259548672 | bytes 28345344 | tf_op jit(solution)/shard_map/dot_general | solution.py:30
  380.8 4.7 convolution_convert_fusion
  385.5 6.0 reshape.441
  391.5 6.3 copy.155
  397.9 16.6 %convert_bitcast_fusion = bf16[3,512,12,64]{1,3,2,0:T(8,128)(2,1)} fusion(bf16[3,512,12,64]{1,3,2,0:T(8,128)(2,1)S(1)} %copy.155, f32[3,12,512]{2,1,0:T(8,128)S(1)} %copy-done.23, f32[3,12,512,512]{2,3,1,0:T(8,128)} %get-tuple-element.180, pred[3,512]{1,0:T(4,128)(4,1)S(1)} %copy-done.34), kind=kOutput, calls=%fused_computation.101 | convolution fusion | flops 1246887936 | bytes 42542592 | tf_op jit(solution)/shard_map/rhqk,rqhe->rkhe/dot_general | solution.py:253
  414.5 30.9 %multiply_reduce_fusion = (f32[3,12,512]{2,1,0:T(8,128)S(1)}, f32[3,12,512,512]{2,3,1,0:T(8,128)}) fusion(f32[3,12,512]{2,1,0:T(8,128)S(1)} %copy-done.23, f32[3,12,512,512]{2,3,1,0:T(8,128)} %get-tuple-element.180, pred[3,512]{1,0:T(4,128)(4,1)S(1)} %copy-done.34, bf16[3,512,12,64]{1,3,2,0:T(8,128)(2,1)S(1)} %copy.155, ...), kind=kOutput, calls=%fused_computation.3 | convolution fusion | flops 1255127040 | bytes 80365056 | tf_op jit(solution)/shard_map/rqhe,rkhe->rhqk/dot_general | solution.py:259
  445.4 31.5 %multiply_convert_fusion = bf16[3,12,512,512]{2,3,1,0:T(8,128)(2,1)} fusion(f32[3,12,512,512]{2,3,1,0:T(8,128)} %get-tuple-element.187, f32[3,12,512]{2,1,0:T(8,128)S(1)} %get-tuple-element.186, f32[3,12,512]{2,1,0:T(8,128)S(1)} %copy-done.23, f32[3,12,512,512]{2,3,1,0:T(8,128)} %get-tuple-element.180, pred[3,512]{1,0:T(4,128)(4,1)S(1)} %copy-done.34), kind=kLoop, calls=%fused_computation.2 | loop fusion | flops 56623104 | bytes 94520832 | tf_op jit(solution)/shard_map/convert_element_type | solution.py:264
  477.0 11.4 %fusion.37 = bf16[3,512,12,64]{1,3,2,0:T(8,128)(2,1)} fusion(bf16[3,512,12,64]{1,3,2,0:T(8,128)(2,1)S(1)} %copy-done.5, bf16[3,12,512,512]{2,3,1,0:T(8,128)(2,1)} %multiply_convert_fusion), kind=kOutput, calls=%fused_computation.92 | convolution fusion | flops 1210318848 | bytes 23592960 | tf_op jit(solution)/shard_map/rhqk,rqhe->rkhe/dot_general | solution.py:270
  488.3 9.5 fusion.36
  511.9 8.2 multiply_convert_fusion.2
  523.7 4.5 multiply_convert_fusion.1
  528.2 5.2 convolution_bitcast_fusion
  536.7 10.9 fusion.117
  548.3 14.8 %fusion.109 = f32[768,3072]{1,0:T(8,128)} fusion(bf16[1536,3072]{1,0:T(8,128)(2,1)} %get-tuple-element.191, f32[1536,768]{1,0:T(8,128)} %copy-done.3, f32[768]{0:T(1024)S(1)} %copy-done.56, f32[768]{0:T(1024)S(1)} %copy-done.45, f32[1536]{0:T(1024)S(1)} %add_rsqrt_fusion.1, f32[1536]{0:T(1024)S(1)} %broadcast_multiply_fusion.5), kind=kOutput, calls=%fused_computation.195 | convolution fusion | flops 7253655552 | bytes 23611392 | tf_op jit(solution)/shard_map/dot_general | solution.py:20
  563.1 13.9 %fusion.102 = f32[3072,768]{1,0:T(8,128)} fusion(bf16[1536,3072]{1,0:T(8,128)(2,1)} %get-tuple-element.182, f32[1536,768]{1,0:T(8,128)} %copy-done.18), kind=kOutput, calls=%fused_computation.188 | convolution fusion | flops 7248936960 | bytes 23592960 | tf_op jit(solution)/shard_map/dot_general | solution.py:20
  586.0 40.5 %all-reduce.20 = (f32[768]{0:T(1024)}, f32[768]{0:T(1024)}, f32[768]{0:T(1024)}, f32[768]{0:T(1024)}, f32[768]{0:T(1024)}, /*index=5*/f32[3072]{0:T(1024)S(1)}, ...) all-reduce(f32[768]{0:T(1024)S(1)} %convert_reduce_fusion.4, ...), channel_id=7, replica_groups=mesh['table'=8,'batch'=4] {'table','batch'}, use_global_device_ids=true, to_apply=%region_19.20.clone | all-reduce | flops 9222 | bytes 73776
  636.6 5.5 all-gather
  642.9 7.9 all-reduce.9
  654.3 4.5 fusion.72
  658.9 6.5 multiply_add_fusion
  665.4 8.4 fusion.31
  673.8 26.6 %reduce-scatter.16.cloned.1.call-done = f32[24,768]{1,0:T(8,128)} async-done(((f32[768,768]{1,0:T(8,128)}), f32[24,768]{1,0:T(8,128)}) %reduce-scatter.16.cloned.1.call-update) | async-done | bytes 73744
  700.4 124.9 %reduce-scatter.8.cloned.1.call-done = f32[24,2304]{1,0:T(8,128)} async-done(((f32[768,2304]{1,0:T(8,128)}), f32[24,2304]{1,0:T(8,128)}) %reduce-scatter.8.cloned.1.call-update) | async-done | bytes 221200 | tf_op jit(solution)/shard_map/reduce_scatter | solution.py:329
  825.3 141.6 %reduce-scatter.12.cloned.1.call-done = f32[24,3072]{1,0:T(8,128)} async-done(((f32[768,3072]{1,0:T(8,128)}), f32[24,3072]{1,0:T(8,128)}) %reduce-scatter.12.cloned.1.call-update) | async-done | bytes 294928 | tf_op jit(solution)/shard_map/reduce_scatter | solution.py:336
  966.9 141.8 %reduce-scatter.14.cloned.1.call-done = f32[96,768]{1,0:T(8,128)} async-done(((f32[3072,768]{1,0:T(8,128)}), f32[96,768]{1,0:T(8,128)}) %reduce-scatter.14.cloned.1.call-update) | async-done | bytes 294928 | tf_op jit(solution)/shard_map/reduce_scatter | solution.py:338
  (265 shorter events, 98.4 us)
Async XLA Ops:
  7.2 64.5 %copy-start = (bf16[1,768,128]{2,1,0:T(8,128)(2,1)S(1)}, bf16[1,768,128]{2,1,0:T(8,128)(2,1)}, u32[]{:S(2)}) copy-start(bf16[1,768,128]{2,1,0:T(8,128)(2,1)} %param.43) | copy-start | bytes 589828
  7.2 82.5 %copy-start.60 = (u32[32]{0:T(128)S(1)}, u32[32]{0:T(128)}, u32[]{:S(2)}) copy-start(u32[32]{0:T(128)} %constant.220) | copy-start | bytes 388
  7.2 86.2 %copy-start.1 = (bf16[3,512,768]{2,1,0:T(8,128)(2,1)S(1)}, bf16[3,512,768]{2,1,0:T(8,128)(2,1)}, u32[]{:S(2)}) copy-start(bf16[3,512,768]{2,1,0:T(8,128)(2,1)} %param.24) | copy-start | bytes 7077892
  7.2 92.0 %all-gather.8.cloned.1.call-start = ((), (), s32[]{:S(2)}) async-start(), calls=%async_computation.5 | async-start | bytes 1216512 | tf_op jit(solution)/shard_map/all_gather | solution.py:102
  8.0 121.6 %all-gather.10.cloned.1.call-start = ((), (), s32[]{:S(2)}) async-start(), calls=%async_computation.6 | async-start | bytes 3649536 | tf_op jit(solution)/shard_map/all_gather | solution.py:103
  8.7 239.6 %all-gather.12.cloned.1.call-start = ((), (), s32[]{:S(2)}) async-start(), calls=%async_computation.7 | async-start | bytes 1216512 | tf_op jit(solution)/shard_map/all_gather | solution.py:106
  9.4 250.2 %all-gather.14.cloned.1.call-start = ((), (), s32[]{:S(2)}) async-start(), calls=%async_computation.8 | async-start | bytes 4866048 | tf_op jit(solution)/shard_map/all_gather | solution.py:110
  10.0 305.2 %all-gather.16.cloned.1.call-start = ((), (), s32[]{:S(2)}) async-start(), calls=%async_computation.9 | async-start | bytes 4866048 | tf_op jit(solution)/shard_map/all_gather | solution.py:112
  10.6 663.2 %reduce-scatter.10.cloned.1.call-start = ((), (), s32[]{:S(2)}) async-start(), calls=%async_computation.11 | async-start | bytes 2433024 | tf_op jit(solution)/shard_map/reduce_scatter | solution.py:332
  10.7 87.7 %copy-start.25 = (s32[64,8]{1,0:T(8,128)}, s32[64,8]{1,0:T(8,128)S(1)}, u32[]{:S(2)}) copy-start(s32[64,8]{1,0:T(8,128)S(1)} %get-tuple-element.196) | copy-start | bytes 6148
  10.7 87.7 %copy-start.27 = (s32[64,8]{1,0:T(8,128)}, s32[64,8]{1,0:T(8,128)S(1)}, u32[]{:S(2)}) copy-start(s32[64,8]{1,0:T(8,128)S(1)} %get-tuple-element.197) | copy-start | bytes 6148
  12.4 72.3 %copy-start.57 = (f32[128]{0:T(128)}, f32[128]{0:T(128)S(1)}, u32[]{:S(2)}) copy-start(f32[128]{0:T(128)S(1)} %compare_convert_fusion) | copy-start | bytes 1540
  63.6 34.3 %copy-start.37 = (f32[768]{0:T(1024)}, f32[768]{0:T(1024)S(1)}, u32[]{:S(2)}) copy-start(f32[768]{0:T(1024)S(1)} %convert_element_type.174) | copy-start | bytes 9220
  70.4 27.4 %copy-start.35 = (f32[12,128]{1,0:T(8,128)}, f32[12,128]{1,0:T(8,128)S(1)}, u32[]{:S(2)}) copy-start(f32[12,128]{1,0:T(8,128)S(1)} %reshape.433) | copy-start | bytes 18436
  71.7 13.1 %copy-start.58 = (f32[12]{0:T(128)}, f32[12]{0:T(128)S(1)}, u32[]{:S(2)}) copy-start(f32[12]{0:T(128)S(1)} %compare_convert_fusion.1) | copy-start | bytes 148
  85.5 137.6 %copy-start.33 = (pred[3,512]{1,0:T(4,128)(4,1)}, pred[3,512]{1,0:T(4,128)(4,1)S(1)}, u32[]{:S(2)}) copy-start(pred[3,512]{1,0:T(4,128)(4,1)S(1)} %get-tuple-element.169) | copy-start | bytes 4612
  89.6 8.8 copy-start.40
  89.7 8.8 copy-start.52
  99.2 236.6 %copy-start.31 = (f32[1536]{0:T(1024)}, f32[1536]{0:T(1024)S(1)}, u32[]{:S(2)}) copy-start(f32[1536]{0:T(1024)S(1)} %and_convert_fusion.2) | copy-start | bytes 18436
  106.5 8.5 copy-start.21
  110.3 19.2 %copy-start.50 = (f32[2304]{0:T(1024)S(1)}, f32[2304]{0:T(1024)}, u32[]{:S(2)}) copy-start(f32[2304]{0:T(1024)} %pad_maximum_fusion) | copy-start | bytes 27652
  259.6 55.6 %copy-start.46 = (f32[768]{0:T(1024)S(1)}, f32[768]{0:T(1024)}, u32[]{:S(2)}) copy-start(f32[768]{0:T(1024)} %convert_element_type.173) | copy-start | bytes 9220
  315.2 14.0 %slice-start = ((s8[4718592]{0:T(1024)(128)(4,1)}), s8[4194304]{0:T(1024)(128)(4,1)S(1)}, s32[]{:S(2)}) async-start(s8[4718592]{0:T(1024)(128)(4,1)} %bitcast.148), calls=%async_computation.15 | async-start | bytes 8388608
  315.2 14.0 %slice-start.4 = ((s8[4718592]{0:T(1024)(128)(4,1)}), s8[4194304]{0:T(1024)(128)(4,1)S(1)}, s32[]{:S(2)}) async-start(s8[4718592]{0:T(1024)(128)(4,1)} %bitcast.156), calls=%async_computation.19 | async-start | bytes 8388608
  315.2 14.0 %slice-start.1 = ((s8[4718592]{0:T(1024)(128)(4,1)}), s8[524288]{0:T(1024)(128)(4,1)S(1)}, s32[]{:S(2)}) async-start(s8[4718592]{0:T(1024)(128)(4,1)} %bitcast.148), calls=%async_computation.16 | async-start | bytes 1048576
  315.2 14.1 %slice-start.5 = ((s8[4718592]{0:T(1024)(128)(4,1)}), s8[524288]{0:T(1024)(128)(4,1)S(1)}, s32[]{:S(2)}) async-start(s8[4718592]{0:T(1024)(128)(4,1)} %bitcast.156), calls=%async_computation.20 | async-start | bytes 1048576
  335.8 23.1 %slice-start.2 = ((s8[4718592]{0:T(1024)(128)(4,1)}), s8[4194304]{0:T(1024)(128)(4,1)S(1)}, s32[]{:S(2)}) async-start(s8[4718592]{0:T(1024)(128)(4,1)} %bitcast.150), calls=%async_computation.17 | async-start | bytes 8388608
  338.3 20.6 %copy-start.18 = (f32[1536,768]{1,0:T(8,128)}, f32[1536,768]{1,0:T(8,128)S(1)}, u32[]{:S(2)}) copy-start(f32[1536,768]{1,0:T(8,128)S(1)} %get-tuple-element.161) | copy-start | bytes 14155780
  338.3 20.6 %slice-start.3 = ((s8[4718592]{0:T(1024)(128)(4,1)}), s8[524288]{0:T(1024)(128)(4,1)S(1)}, s32[]{:S(2)}) async-start(s8[4718592]{0:T(1024)(128)(4,1)} %bitcast.150), calls=%async_computation.18 | async-start | bytes 1048576
  397.9 16.6 %copy-start.9 = (bf16[3,512,12,64]{1,3,2,0:T(8,128)(2,1)S(1)}, bf16[3,512,12,64]{1,3,2,0:T(8,128)(2,1)}, u32[]{:S(2)}) copy-start(bf16[3,512,12,64]{1,3,2,0:T(8,128)(2,1)} %copy.149) | copy-start | bytes 7077892
  445.4 31.6 %copy-start.5 = (bf16[3,512,12,64]{1,3,2,0:T(8,128)(2,1)S(1)}, bf16[3,512,12,64]{1,3,2,0:T(8,128)(2,1)}, u32[]{:S(2)}) copy-start(bf16[3,512,12,64]{1,3,2,0:T(8,128)(2,1)} %copy.147) | copy-start | bytes 7077892
  476.9 11.4 %copy-start.4 = (bf16[3,512,12,64]{1,3,2,0:T(8,128)(2,1)S(1)}, bf16[3,512,12,64]{1,3,2,0:T(8,128)(2,1)}, u32[]{:S(2)}) copy-start(bf16[3,512,12,64]{1,3,2,0:T(8,128)(2,1)} %copy.148) | copy-start | bytes 7077892
  497.9 202.5 %reduce-scatter.16.cloned.1.call-start = ((), (), s32[]{:S(2)}) async-start(), calls=%async_computation.14 | async-start | bytes 2433024
  511.9 8.2 copy-start.24
  511.9 9.6 copy-start.2
  536.6 288.7 %reduce-scatter.8.cloned.1.call-start = ((), (), s32[]{:S(2)}) async-start(), calls=%async_computation.10 | async-start | bytes 7299072 | tf_op jit(solution)/shard_map/reduce_scatter | solution.py:329
  547.6 419.3 %reduce-scatter.12.cloned.1.call-start = ((), (), s32[]{:S(2)}) async-start(), calls=%async_computation.12 | async-start | bytes 9732096 | tf_op jit(solution)/shard_map/reduce_scatter | solution.py:336
  563.1 545.6 %reduce-scatter.14.cloned.1.call-start = ((), (), s32[]{:S(2)}) async-start(), calls=%async_computation.13 | async-start | bytes 9732096 | tf_op jit(solution)/shard_map/reduce_scatter | solution.py:338
  577.0 8.9 copy-start.42
  577.1 8.9 copy-start.43
  577.1 8.9 copy-start.44
  577.1 74.3 %copy-start.36 = (f32[12,128]{1,0:T(8,128)S(1)}, f32[12,128]{1,0:T(8,128)}, u32[]{:S(2)}) copy-start(f32[12,128]{1,0:T(8,128)} %copy-done.35) | copy-start | bytes 18436
  577.1 77.2 %copy-start.16 = (f32[3,64,8,8]{2,3,1,0:T(8,128)S(1)}, f32[3,64,8,8]{2,3,1,0:T(8,128)}, u32[]{:S(2)}) copy-start(f32[3,64,8,8]{2,3,1,0:T(8,128)} %copy-done.15) | copy-start | bytes 147460
  579.4 6.6 copy-start.48
  579.4 6.6 copy-start.51
  579.4 6.6 copy-start.53
  579.4 6.6 copy-start.54
  585.9 72.9 %copy-start.13 = (bf16[1536,768]{1,0:T(8,128)(2,1)S(1)}, bf16[1536,768]{1,0:T(8,128)(2,1)}, u32[]{:S(2)}) copy-start(bf16[1536,768]{1,0:T(8,128)(2,1)} %copy-done.12) | copy-start | bytes 7077892
  (31 other events, 95.2 us)
Sparse Core Ops, SparseCore 0:
  10.9 56.6 all-gather.7
  70.5 58.9 all-gather.9
  132.4 52.7 all-gather.11
  188.0 62.4 all-gather.13
  253.2 61.9 all-gather.15
  498.0 97.8 reduce-scatter.9
  601.7 98.6 reduce-scatter.15
  706.6 118.6 reduce-scatter.7
  831.8 135.0 reduce-scatter.11
  973.2 135.3 reduce-scatter.13
where the time goes:
time: 1120 us
  waiting for transfers between devices  455 us (41%)
  matrix products  322 us (29%)
  local copies, waits for them, and re-layouts  119 us (11%)
  blocking collectives  115 us (10%)
  other arithmetic  86.7 us (8%)
  between operations  17.2 us (2%)
    reduce_scatter x1, waiting for transfers between devices, body(): lax.psum_scatter(grad_down_w, ('table', 'batch'), scatter_dimension=0, ti...  142 us
    reduce_scatter x1, waiting for transfers between devices, body(): lax.psum_scatter(grad_up_w, ('table', 'batch'), scatter_dimension=0, tile...  142 us
    reduce_scatter x1, waiting for transfers between devices, body(): lax.psum_scatter(grad_qkv_w, ('table', 'batch'), scatter_dimension=0, til...  125 us
    unnamed x4, blocking collectives  104 us
    dot_general x6, matrix products, product(): return jnp.dot(left, right, preferred_element_type=jnp.float32)  87.3 us
    dot_general x6, matrix products, outer_cols(): lax.dot_general(left, right, (((1,), (1,)), ((), ())), precision=precisio...  56.2 us
    dot_general x6, matrix products, inner_rows(): lax.dot_general(left, right, (((0,), (0,)), ((), ())), precision=precisio...  50 us
    unnamed x175, local copies, waits for them, and re-layouts  37.8 us
  transfers between devices with their start and end apart: 10, of which 6 were waited for; matrix products, arithmetic and copies ran while one was open for 30% of the time, Pallas kernels for 0%

commit v1 on v0

v1 whole, which is shorter than its diff:
```python
import functools

import jax
import jax.numpy as jnp
from jax import lax
from jax.experimental import pallas as pl
from jax.experimental.pallas import tpu as pltpu
from jax.sharding import PartitionSpec as P

HEADS = 12
BLOCK = 8
NORM_EPS = 1e-05
MASKED = -1000000000.0
FAR = -3e38
PRECISE = lax.Precision.HIGHEST
TILE = 256
VMEM_BYTES = 64_000_000
BOTH = ("table", "batch")
F32 = jnp.float32
BF16 = jnp.bfloat16


def mm(left, right):
    return jnp.dot(left, right, preferred_element_type=F32)


def mm_t(left, right):
    return lax.dot_general(left, right, (((1,), (1,)), ((), ())), preferred_element_type=F32)


def t_mm(left, right):
    return lax.dot_general(left, right, (((0,), (0,)), ((), ())), preferred_element_type=F32)


def rowsum(values):
    return jnp.sum(values, axis=0, keepdims=True)


def norm_forward(hidden, gain, shift):
    average = jnp.mean(hidden, axis=-1, keepdims=True)
    centered = hidden - average
    variance = jnp.mean(centered * centered, axis=-1, keepdims=True)
    inv_std = lax.rsqrt(variance + NORM_EPS)
    standard = centered * inv_std
    return standard * gain + shift, standard, inv_std


def norm_backward(grad_norm, standard, inv_std, gain):
    scaled = grad_norm * gain
    return inv_std * (
        scaled
        - jnp.mean(scaled, axis=-1, keepdims=True)
        - standard * jnp.mean(scaled * standard, axis=-1, keepdims=True)
    )


def group_probs(query, tok, live_row, scale):
    size = tok.shape[0]
    row = lax.broadcasted_iota(jnp.int32, (size, size), 0) // BLOCK
    col = lax.broadcasted_iota(jnp.int32, (size, size), 1) // BLOCK
    scores = jnp.where(live_row > 0, mm_t(query, tok) * scale, MASKED)
    scores = jnp.where(row == col, scores, FAR)
    terms = jnp.exp(scores - jnp.max(scores, axis=-1, keepdims=True))
    return terms / jnp.sum(terms, axis=-1, keepdims=True), row == col


def merge_kernel(tok, live_row, live_col, merge_w, qkv_w, qkv_bias, query_out, hidden_out, attn_out, packed_out, squares):
    step = pl.program_id(0)
    scale = tok.shape[1] ** -0.5
    x = tok[...]
    live = live_col[...]
    query = mm(x, merge_w[...]).astype(BF16)
    query_out[...] = query
    probs, _ = group_probs(query, x, live_row[0], scale)
    merged = mm(probs.astype(BF16), x) * live
    wide = x.astype(F32)
    hidden = wide + merged
    hidden_out[...] = hidden
    attn_in = hidden.astype(BF16)
    attn_out[...] = attn_in
    packed_out[...] = (mm(attn_in, qkv_w[...]) + qkv_bias[...]).astype(BF16)

    @pl.when(step == 0)
    def _():
        squares[...] = jnp.zeros_like(squares)

    squares[0:1, :] += rowsum(live * wide * wide)
    squares[1:2, :] += rowsum(merged * merged)


def lane_mask(values, low, high):
    lane = lax.broadcasted_iota(jnp.int32, values.shape, 1)
    return jnp.where((lane >= low) & (lane < high), values, jnp.zeros_like(values))


def attn_kernel(scale, q_ref, k_ref, v_ref, bias_ref, ctx_ref, lse_ref):
    seq, lanes = q_ref.shape[1:]
    head = lanes // 2
    q = q_ref[0] * jnp.asarray(scale, BF16)
    k = k_ref[0]
    v_t = v_ref[0].T
    bias = bias_ref[0]
    for c in range(seq // TILE):
        rows = slice(c * TILE, (c + 1) * TILE)
        parts = []
        for h in range(2):
            scores = mm_t(k, lane_mask(q[rows], h * head, (h + 1) * head)) + bias
            top = jnp.max(scores, axis=0, keepdims=True)
            terms = jnp.exp(scores - top)
            total = jnp.sum(terms, axis=0, keepdims=True)
            probs = (terms * (1.0 / total)).astype(BF16)
            lse_ref[0, 0, h : h + 1, rows] = top + jnp.log(total)
            parts.append(mm(v_t[h * head : (h + 1) * head], probs))
        ctx_ref[0, rows, :] = jnp.concatenate(parts, axis=0).T.astype(BF16)


def attn_back_kernel(scale, q_ref, k_ref, v_ref, bias_ref, lse_ref, grad_ref, dq_ref, dk_ref, dv_ref):
    seq, lanes = q_ref.shape[1:]
    head = lanes // 2
    q = q_ref[0] * jnp.asarray(scale, BF16)
    k = k_ref[0]
    v = v_ref[0]
    k_t = k.T
    bias = bias_ref[0]
    grad_k = jnp.zeros((seq, lanes), F32)
    grad_v = jnp.zeros((seq, lanes), F32)
    for c in range(seq // TILE):
        rows = slice(c * TILE, (c + 1) * TILE)
        parts = []
        for h in range(2):
            q_part = lane_mask(q[rows], h * head, (h + 1) * head)
            g_part = lane_mask(grad_ref[0, rows, :], h * head, (h + 1) * head)
            scores = mm_t(k, q_part) + bias
            probs = jnp.exp(scores - lse_ref[0, 0, h : h + 1, rows])
            grad_v += mm(probs.astype(BF16), g_part)
            grad_p = mm_t(v, g_part)
            grad_s = (probs * (grad_p - jnp.sum(probs * grad_p, axis=0, keepdims=True))).astype(BF16)
            grad_k += mm(grad_s, q_part)
            parts.append(mm(k_t[h * head : (h + 1) * head], grad_s))
        dq_ref[0, rows, :] = (jnp.concatenate(parts, axis=0).T * scale).astype(BF16)
    dk_ref[0] = grad_k.astype(BF16)
    dv_ref[0] = grad_v.astype(BF16)


def ffn_kernel(
    per_row,
    ctx,
    hidden,
    cot,
    cls_grad,
    live_col,
    out_w,
    up_w,
    down_w,
    vecs,
    layer_out,
    activated,
    grad_up,
    ffn_in_out,
    grad_down_out,
    grad_attn_out,
    grad_two_out,
    grad_ctx_out,
    sums,
    up_sums,
    slope,
):
    step = pl.program_id(0)
    width = hidden.shape[1]
    chunks = up_w.shape[1] // width

    @pl.when(step == 0)
    def _():
        sums[...] = jnp.zeros_like(sums)
        up_sums[...] = jnp.zeros_like(up_sums)

    live = live_col[...]
    out_bias, gain_one, shift_one, down_bias, gain_two, shift_two = (vecs[i : i + 1, :width] for i in range(6))
    branch = mm(ctx[...], out_w[...]) + out_bias
    norm_one, standard_one, inv_one = norm_forward(hidden[...] + branch, gain_one, shift_one)
    ffn_in = norm_one.astype(BF16)
    ffn_in_out[...] = ffn_in
    down = jnp.zeros_like(norm_one)
    for j in range(chunks):
        cols = slice(j * width, (j + 1) * width)
        pre = mm(ffn_in, up_w[:, cols]) + vecs[6:7, cols]
        cumulative = 0.5 * (1.0 + lax.erf(pre * 0.7071067811865476))
        act = (pre * cumulative).astype(BF16)
        slope[:, cols] = cumulative + pre * (jnp.exp(-0.5 * pre * pre) * 0.3989422804014327)
        activated[:, cols] = act
        down += mm(act, down_w[cols, :])
    down += down_bias
    normed, standard_two, inv_two = norm_forward(norm_one + down, gain_two, shift_two)
    result = (normed * live).astype(BF16)
    layer_out[...] = result
    wide = result.astype(F32)
    sums[5:6, :] += rowsum(live * branch * branch)
    sums[6:7, :] += rowsum(live * down * down)
    sums[7:8, :] += rowsum(wide * wide)
    first = (lax.broadcasted_iota(jnp.int32, (hidden.shape[0], 1), 0) == 0) & (step % per_row == 0)
    grad = live * (cot[...].astype(F32) + jnp.where(first, cls_grad[0], 0.0))
    sums[0:1, :] += rowsum(grad * standard_two)
    sums[1:2, :] += rowsum(grad)
    grad_three = norm_backward(grad, standard_two, inv_two, gain_two)
    grad_down = grad_three.astype(BF16)
    grad_down_out[...] = grad_down
    sums[2:3, :] += rowsum(grad_down.astype(F32))
    total = grad_three
    for j in range(chunks):
        cols = slice(j * width, (j + 1) * width)
        piece = (mm_t(grad_down, down_w[cols, :]) * slope[:, cols]).astype(BF16)
        grad_up[:, cols] = piece
        up_sums[0:1, cols] += rowsum(piece.astype(F32))
        total += mm_t(piece, up_w[:, cols])
    sums[3:4, :] += rowsum(total * standard_one)
    sums[4:5, :] += rowsum(total)
    grad_two = norm_backward(total, standard_one, inv_one, gain_one)
    grad_two_out[...] = grad_two
    grad_attn = grad_two.astype(BF16)
    grad_attn_out[...] = grad_attn
    sums[8:9, :] += rowsum(grad_attn.astype(F32))
    grad_ctx_out[...] = mm_t(grad_attn, out_w[...]).astype(BF16)


def input_kernel(
    dq, dk, dv, grad_two, tok, query, live_row, live_col, merge_w, qkv_w, grad_input, grad_query_out, packed_out, sums
):
    step = pl.program_id(0)
    width = tok.shape[1]
    scale = width**-0.5

    @pl.when(step == 0)
    def _():
        sums[...] = jnp.zeros_like(sums)

    x = tok[...]
    grad_q, grad_v = dq[...], dv[...]
    grad_one = grad_two[...]
    for i, piece in enumerate((grad_q, dk[...], grad_v)):
        cols = slice(i * width, (i + 1) * width)
        packed_out[:, cols] = piece
        grad_one += mm_t(piece, qkv_w[:, cols])
    sums[0:1, :] += rowsum(grad_q.astype(F32))
    sums[1:2, :] += rowsum(grad_v.astype(F32))
    grad_merged = (grad_one * live_col[...]).astype(BF16)
    mq = query[...]
    probs, same = group_probs(mq, x, live_row[0], scale)
    grad_probs = mm_t(grad_merged, x)
    grad_scores = probs * (grad_probs - jnp.sum(probs * grad_probs, axis=-1, keepdims=True))
    grad_scores = jnp.where(same & (live_row[0] > 0), grad_scores, 0.0)
    grad_query = (mm(grad_scores.astype(BF16), x) * scale).astype(BF16)
    grad_query_out[...] = grad_query
    blocks = mm(probs.T.astype(BF16), grad_merged) + mm(grad_scores.T.astype(BF16), mq) * scale
    blocks += mm_t(grad_query, merge_w[...])
    grad_input[...] = (grad_one + blocks).astype(BF16)


def params(**kw):
    return pltpu.CompilerParams(vmem_limit_bytes=VMEM_BYTES, **kw)


def fixed(shape):
    zeros = (0,) * len(shape)
    return pl.BlockSpec(shape, lambda *_: zeros, pipeline_mode=pl.Buffered(1))


def tiled(size, width):
    return pl.BlockSpec((size, width), lambda i: (i, 0))


def body(
    tokens,
    row_blocks,
    block_fill,
    row_table,
    class_count,
    merge_w,
    qkv_w,
    query_bias,
    value_bias,
    out_w,
    out_bias,
    gain_one,
    shift_one,
    up_w,
    up_bias,
    down_w,
    down_bias,
    gain_two,
    shift_two,
    head_w,
    cotangent,
    logit_cotangent,
):
    rows, seq, width = tokens.shape
    count = rows * seq
    ff = up_w.shape[1]
    head = width // HEADS
    per_row = seq // TILE
    tiles = count // TILE
    share = merge_w.shape[0]
    devices = width // share
    wide_ff = ff // width

    def cut(mat, n):
        return [mat[:, i * width : (i + 1) * width] for i in range(n)]

    vec_list = (out_bias, gain_one, shift_one, down_bias, gain_two, shift_two, query_bias, value_bias)
    vec_row = jnp.concatenate([*vec_list, up_bias])
    used = vec_row.shape[0]
    vec_row = jnp.pad(vec_row, (0, 8 * width - used)).reshape(8, width)
    mine = jnp.concatenate([merge_w, out_w, *cut(qkv_w, 3), *cut(up_w, wide_ff), down_w, vec_row], axis=0)
    gathered = lax.all_gather(mine, BOTH, axis=0)

    def unit(start, n):
        part = gathered[:, start : start + n * share]
        part = part.reshape(devices, n, share, width).transpose(0, 2, 1, 3)
        return part.reshape(width, n * width)

    merge_full = unit(0, 1)
    out_full = unit(share, 1)
    qkv_full = unit(2 * share, 3)
    up_full = unit(5 * share, wide_ff)
    base = (5 + wide_ff) * share
    down_full = gathered[:, base : base + wide_ff * share].reshape(ff, width)
    vec_rows = gathered[:, base + wide_ff * share].astype(F32)
    vectors = [vec_rows[:, i * share : (i + 1) * share].reshape(1, width) for i in range(8)]
    up_bias_full = vec_rows[:, 8 * share : 8 * share + wide_ff * share].reshape(1, ff)
    query_vec, value_vec = vectors[6], vectors[7]
    qkv_bias = jnp.concatenate([query_vec, jnp.zeros_like(query_vec), value_vec], axis=1)
    vecs = jnp.concatenate(
        [jnp.pad(jnp.concatenate(vectors[:6], axis=0), ((0, 0), (0, ff - width))), up_bias_full, jnp.zeros((1, ff), F32)],
        axis=0,
    )

    position = jnp.arange(seq, dtype=jnp.int32)
    fill_tok = jnp.repeat(block_fill, BLOCK, axis=1)
    live = ((position // BLOCK)[None, :] < row_blocks[:, None]) & ((position % BLOCK)[None, :] < fill_tok)
    live_mask = live.astype(F32)
    live_col = live_mask.reshape(count, 1)
    live_row = live_mask.reshape(tiles, 1, TILE)
    key_bias = jnp.where(live, 0.0, MASKED).astype(F32).reshape(rows, seq, 1)

    batch = lax.axis_size("batch")
    group_rows = rows * batch
    heads = lax.all_gather(head_w[0], "batch", axis=0)
    counts = lax.all_gather(class_count, "batch", axis=0, tiled=True)
    group_dlog_raw = lax.all_gather(logit_cotangent, "batch", axis=0, tiled=True)
    classes = head_w.shape[2]
    own = lax.axis_index("batch")
    my_table = lax.dynamic_slice(row_table, (own * rows,), (rows,))
    class_ids = jnp.arange(classes, dtype=jnp.int32)
    my_select = (my_table[:, None] == jnp.arange(batch, dtype=jnp.int32)[None, :]).astype(F32)
    my_class = (class_ids[None, :] < (my_select * counts[None, :].astype(F32)).sum(1, keepdims=True)).astype(F32)
    my_dlog = logit_cotangent * my_class
    picked = (my_select[:, :, None] * my_dlog[:, None, :]).transpose(1, 0, 2)
    cls_grad = jnp.sum(
        lax.dot_general(picked, heads.astype(F32), (((2,), (2,)), ((0,), (0,))), precision=PRECISE), axis=0
    )

    tok_flat = tokens.reshape(count, width)
    cot_flat = cotangent.reshape(count, width)
    merge_query, hidden, attn_in, packed, squares = pl.pallas_call(
        merge_kernel,
        grid=(tiles,),
        in_specs=[
            tiled(TILE, width),
            pl.BlockSpec((1, 1, TILE), lambda i: (i, 0, 0)),
            tiled(TILE, 1),
            fixed((width, width)),
            fixed((width, 3 * width)),
            fixed((1, 3 * width)),
        ],
        out_specs=[
            tiled(TILE, width),
            tiled(TILE, width),
            tiled(TILE, width),
            tiled(TILE, 3 * width),
            fixed((8, width)),
        ],
        out_shape=[
            jax.ShapeDtypeStruct((count, width), BF16),
            jax.ShapeDtypeStruct((count, width), F32),
            jax.ShapeDtypeStruct((count, width), BF16),
            jax.ShapeDtypeStruct((count, 3 * width), BF16),
            jax.ShapeDtypeStruct((8, width), F32),
        ],
        compiler_params=params(),
        name="merge_qkv",
    )(tok_flat, live_row, live_col, merge_full, qkv_full, qkv_bias)

    packed_rows = packed.reshape(rows, seq, 3 * width)
    pairs = HEADS // 2
    lanes = 2 * head

    def head_block(offset):
        return pl.BlockSpec((1, seq, lanes), lambda r, p: (r, 0, p + offset))

    bias_block = pl.BlockSpec((1, seq, 1), lambda r, p: (r, 0, 0))
    lse_block = pl.BlockSpec((1, 1, 2, seq), lambda r, p: (r, p, 0, 0))
    context, lse = pl.pallas_call(
        functools.partial(attn_kernel, head**-0.5),
        grid=(rows, pairs),
        in_specs=[head_block(0), head_block(pairs), head_block(2 * pairs), bias_block],
        out_specs=[head_block(0), lse_block],
        out_shape=[
            jax.ShapeDtypeStruct((rows, seq, width), BF16),
            jax.ShapeDtypeStruct((rows, pairs, 2, seq), F32),
        ],
        compiler_params=params(),
        name="attention",
    )(packed_rows, packed_rows, packed_rows, key_bias)

    context = context.reshape(count, width)
    (layer_out, activated, grad_up, ffn_in, grad_down, grad_attn, grad_two, grad_ctx, sums, up_sums) = pl.pallas_call(
        functools.partial(ffn_kernel, per_row),
        grid=(tiles,),
        in_specs=[
            tiled(TILE, width),
            tiled(TILE, width),
            tiled(TILE, width),
            pl.BlockSpec((1, 1, width), lambda i: (i // per_row, 0, 0)),
            tiled(TILE, 1),
            fixed((width, width)),
            fixed((width, ff)),
            fixed((ff, width)),
            fixed((8, ff)),
        ],
        out_specs=[
            tiled(TILE, width),
            tiled(TILE, ff),
            tiled(TILE, ff),
            tiled(TILE, width),
            tiled(TILE, width),
            tiled(TILE, width),
            tiled(TILE, width),
            tiled(TILE, width),
            fixed((16, width)),
            fixed((8, ff)),
        ],
        out_shape=[
            jax.ShapeDtypeStruct((count, width), BF16),
            jax.ShapeDtypeStruct((count, ff), BF16),
            jax.ShapeDtypeStruct((count, ff), BF16),
            jax.ShapeDtypeStruct((count, width), BF16),
            jax.ShapeDtypeStruct((count, width), BF16),
            jax.ShapeDtypeStruct((count, width), BF16),
            jax.ShapeDtypeStruct((count, width), F32),
            jax.ShapeDtypeStruct((count, width), BF16),
            jax.ShapeDtypeStruct((16, width), F32),
            jax.ShapeDtypeStruct((8, ff), F32),
        ],
        scratch_shapes=[pltpu.VMEM((TILE, ff), F32)],
        compiler_params=params(),
        name="ffn",
    )(context, hidden, cot_flat, cls_grad.reshape(rows, 1, width), live_col, out_full, up_full, down_full, vecs)

    grad_rows = grad_ctx.reshape(rows, seq, width)
    grad_q, grad_k, grad_v = pl.pallas_call(
        functools.partial(attn_back_kernel, head**-0.5),
        grid=(rows, pairs),
        in_specs=[head_block(0), head_block(pairs), head_block(2 * pairs), bias_block, lse_block, head_block(0)],
        out_specs=[head_block(0)] * 3,
        out_shape=[jax.ShapeDtypeStruct((rows, seq, width), BF16)] * 3,
        compiler_params=params(),
        name="attention_back",
    )(packed_rows, packed_rows, packed_rows, key_bias, lse, grad_rows)

    grad_input, grad_query, grad_packed, bias_sums = pl.pallas_call(
        input_kernel,
        grid=(tiles,),
        in_specs=[
            tiled(TILE, width),
            tiled(TILE, width),
            tiled(TILE, width),
            tiled(TILE, width),
            tiled(TILE, width),
            tiled(TILE, width),
            pl.BlockSpec((1, 1, TILE), lambda i: (i, 0, 0)),
            tiled(TILE, 1),
            fixed((width, width)),
            fixed((width, 3 * width)),
        ],
        out_specs=[tiled(TILE, width), tiled(TILE, width), tiled(TILE, 3 * width), fixed((8, width))],
        out_shape=[
            jax.ShapeDtypeStruct((count, width), BF16),
            jax.ShapeDtypeStruct((count, width), BF16),
            jax.ShapeDtypeStruct((count, 3 * width), BF16),
            jax.ShapeDtypeStruct((8, width), F32),
        ],
        compiler_params=params(),
        name="merge_back",
    )(
        grad_q.reshape(count, width),
        grad_k.reshape(count, width),
        grad_v.reshape(count, width),
        grad_two,
        tok_flat,
        merge_query,
        live_row,
        live_col,
        merge_full,
        qkv_full,
    )

    grad_merge_w = t_mm(tok_flat, grad_query).astype(BF16)
    grad_qkv_w = t_mm(attn_in, grad_packed).astype(BF16)
    grad_out_w = t_mm(context, grad_attn).astype(BF16)
    grad_up_w = t_mm(ffn_in, grad_up).astype(BF16)
    grad_down_w = t_mm(activated, grad_down).astype(BF16)

    def owners(mat, n):
        return mat.reshape(devices, share, n, width).transpose(0, 2, 1, 3).reshape(devices, n * share, width)

    vec_grads = (sums[8], sums[3], sums[4], sums[2], sums[0], sums[1], bias_sums[0], bias_sums[1])
    vec_block = jnp.concatenate(
        [v.reshape(devices, share) for v in vec_grads] + [up_sums[0].reshape(devices, wide_ff * share)], axis=1
    )
    vec_block = jnp.pad(vec_block, ((0, 0), (0, 8 * width - used))).astype(BF16).reshape(devices, 8, width)
    all_grads = jnp.concatenate(
        [
            owners(grad_merge_w, 1),
            owners(grad_out_w, 1),
            owners(grad_qkv_w, 3),
            owners(grad_up_w, wide_ff),
            grad_down_w.reshape(devices, wide_ff * share, width),
            vec_block,
        ],
        axis=1,
    )
    owned = lax.psum_scatter(all_grads, BOTH, scatter_dimension=0, tiled=True)[0].astype(F32)

    def joined(start, n):
        return jnp.concatenate([owned[start + i * share : start + (i + 1) * share] for i in range(n)], axis=1)

    own_vec = owned[base + wide_ff * share]
    own_vecs = [own_vec[i * share : (i + 1) * share] for i in range(8)]
    own_up_bias = own_vec[8 * share : 8 * share + wide_ff * share]

    layer_rows = layer_out.reshape(rows, seq, width)
    cls_rows = layer_rows[:, 0, :]
    my_logits = jnp.sum(
        my_select[:, :, None] * jnp.einsum("rd,kdc->rkc", cls_rows, heads, preferred_element_type=F32), axis=1
    )
    logits = my_logits * my_class
    group_cls = lax.all_gather(cls_rows, "batch", axis=0, tiled=True)
    owner_mask = (row_table == own).astype(F32)[:, None]
    class_live = (class_ids < class_count[0]).astype(F32)[None, :]
    group_dlog = group_dlog_raw * (owner_mask * class_live)
    grad_head = lax.dot_general(
        group_cls.astype(F32), group_dlog, (((0,), (0,)), ((), ())), precision=PRECISE, preferred_element_type=F32
    )[None]
    partial = jnp.stack(
        [
            jnp.sum(squares[0]),
            jnp.sum(squares[1]),
            jnp.sum(sums[5]),
            jnp.sum(sums[6]),
            jnp.sum(sums[7]),
            jnp.sum(live_mask),
        ]
    )
    totals = lax.psum(partial, BOTH)
    root_squares = jnp.sqrt(totals[:5] / (totals[5] * width))
    return (
        layer_rows,
        logits,
        grad_input.reshape(rows, seq, width),
        joined(0, 1),
        joined(2 * share, 3),
        own_vecs[6],
        own_vecs[7],
        joined(share, 1),
        own_vecs[0],
        own_vecs[1],
        own_vecs[2],
        joined(5 * share, wide_ff),
        own_up_bias,
        owned[base : base + wide_ff * share],
        own_vecs[3],
        own_vecs[4],
        own_vecs[5],
        grad_head,
        root_squares,
    )


def solution(mesh):
    three = P(BOTH, None, None)
    two = P(BOTH, None)
    one = P(BOTH)
    placed = (
        three, one, two, P("table"), one, two, two, one, one, two, one, one, one, two, one, two, one, one, one, three,
        three, two,
    )
    results = (
        three, two, three, two, two, one, one, two, one, one, one, two, one, two, one, one, one, three, P(),
    )
    return jax.shard_map(body, mesh=mesh, in_specs=placed, out_specs=results, check_vma=False)
```

time: 1120 us -> 617 us (0.55)
  matrix products: 322 us -> 41.3 us
  waiting for transfers between devices: 455 us -> 190 us
  Pallas kernels: 0 us -> 174 us
  other arithmetic: 86.7 us -> 15 us
  blocking collectives: 115 us -> 63.8 us
  local copies, waits for them, and re-layouts: 119 us -> 106 us
    reduce_scatter x4 -> x1, waiting for transfers between devices: 408 us -> 107 us  [body(): lax.psum_scatter(all_grads, BOTH, scatter_dimension=0, tiled=True)[0]]
    dot_general x30 -> x8, matrix products: 322 us -> 41.3 us  [the longest x5 39.2 us: t_mm(): lax.dot_general(left, right, (((0,), (0,)), ((), ())), preferred_element_...]
    pallas_call x0 -> x5, Pallas kernels: none -> 174 us  [the longest x1 54.1 us: body(): pl.pallas_call(functools.partial(ffn_kernel, per_row), grid=(tiles,), in_...]
    unnamed x4 -> x1, blocking collectives: 104 us -> 6.38 us
    all_gather x5 -> x1, waiting for transfers between devices: 16.8 us -> 83.3 us  [body(): gathered = lax.all_gather(mine, BOTH, axis=0)]
    convert_element_type x16 -> x10, other arithmetic: 44.1 us -> 3.9 us  [the longest x2 1.67 us: body(): live_mask = live.astype(F32)]
    psum x0 -> x1, blocking collectives: none -> 38.4 us  [body(): totals = lax.psum(partial, BOTH)]
    reduce_sum x9 -> x3, other arithmetic: 35.6 us -> 2.98 us  [the longest x1 1.47 us: body(): jnp.sum(sums[7])]
  transfers between devices with their start and end apart: 10 -> 2, of which waited for: 6 -> 2; matrix products, arithmetic and copies ran while one was open for 30% -> 4% of each run, Pallas kernels for 0% -> 0%
where the time goes in v1:
time: 617 us; the launch traced here: 607 us
  waiting for transfers between devices  190 us (31%)
  Pallas kernels  174 us (28%)
  local copies, waits for them, and re-layouts  106 us (17%)
  blocking collectives  63.8 us (10%)
  matrix products  41.3 us (7%)
  between operations  16.4 us (3%)
  other arithmetic  15 us (2%)
    reduce_scatter x1, waiting for transfers between devices, body(): lax.psum_scatter(all_grads, BOTH, scatter_dimension=0, tiled=True)[0]  107 us
    all_gather x1, waiting for transfers between devices, body(): gathered = lax.all_gather(mine, BOTH, axis=0)  83.3 us
    pallas_call x1, Pallas kernels, body(): pl.pallas_call(functools.partial(ffn_kernel, per_row), grid=(tiles,), in_...  54.1 us
    pallas_call x1, Pallas kernels, body(): pl.pallas_call(functools.partial(attn_kernel, head ** (-0.5)), grid=(rows...  41.4 us
    dot_general x5, matrix products, t_mm(): lax.dot_general(left, right, (((0,), (0,)), ((), ())), preferred_element_...  39.2 us
    pallas_call x1, Pallas kernels, body(): pl.pallas_call(functools.partial(attn_back_kernel, head ** (-0.5)), grid=...  38.8 us
    psum x1, blocking collectives, body(): totals = lax.psum(partial, BOTH)  38.4 us
    unnamed x99, local copies, waits for them, and re-layouts  29 us
  transfers between devices with their start and end apart: 2, of which 2 were waited for; matrix products, arithmetic and copies ran while one was open for 4% of the time, Pallas kernels for 0%

profile of v1, /device:TPU:0, one launch (start us, length us, event | category | flops | bytes accessed | tf_op | source)
XLA Modules:
  0.0 607.1 jit_solution(10440687231471519233)
XLA Ops:
  7.3 6.1 %concatenate.28 = bf16[288]{0:T(512)(128)(2,1)S(1)} concatenate(bf16[24]{0:T(256)(128)(2,1)} %param.32, bf16[24]{0:T(256)(128)(2,1)} %param.33, bf16[24]{0:T(256)(128)(2,1)} %param.34, bf16[24]{0:T(256)(128)(2,1)} %param.38, bf16[24]{0:T(256)(128)(2,1)} %param.39, bf16[24]{0:T(256)(128)(2,1)} %param.40, bf16[24]{0:T(256)(128)(2,1)} %param.29, bf16[24]{0:T(256)(128)(2,1)} %param.30, ...), dimensions={0} | concatenate | bytes 1152 | tf_op jit(solution)/shard_map/concatenate | solution.py:309
  22.8 1.2 dynamic-slice
  24.8 6.4 %all-reduce.3 = s32[4]{0:T(128)S(1)} all-reduce(s32[4]{0:T(128)S(1)} %dynamic-update-slice), channel_id=1, replica_groups=mesh['table'=8,'batch'=4] {'batch'}, use_global_device_ids=true, to_apply=%add.3 | all-reduce | flops 4 | bytes 32
  38.1 8.2 %all_gather.21 = bf16[4,768,128]{2,1,0:T(8,128)(2,1)S(1)} all-gather(bf16[1,768,128]{2,1,0:T(8,128)(2,1)} %param.41), channel_id=1, replica_groups=mesh['table'=8,'batch'=4] {'batch'}, dimensions={0}, use_global_device_ids=true | all-gather | bytes 983040 | tf_op jit(solution)/shard_map/all_gather | solution.py:346
  49.2 1.1 and_select_fusion.bias_ref
  51.3 83.3 %all-gather.5.cloned.1.call-done = bf16[10240,768]{1,0:T(8,128)(2,1)} async-done(((bf16[320,768]{1,0:T(8,128)(2,1)}), bf16[10240,768]{1,0:T(8,128)(2,1)}) %all-gather.5.cloned.1.call-update) | async-done | bytes 15728656 | tf_op jit(solution)/shard_map/all_gather | solution.py:313
  137.0 3.2 fusion.31
  140.2 2.2 slice.328
  142.5 7.9 %fusion.30 = (bf16[32,96,768]{2,1,0:T(8,128)(2,1)}, bf16[32,96,768]{2,1,0:T(8,128)(2,1)}) fusion(bf16[32,320,768]{2,1,0:T(8,128)(2,1)} %bitcast.146), kind=kLoop, calls=%fused_computation.123 | loop fusion | bytes 18874368 | tf_op jit(solution)/shard_map/slice | solution.py:325
  150.4 1.4 reshape.465
  151.8 1.4 reshape.464
  153.2 1.4 reshape.463
  154.6 1.4 reshape.462
  156.0 1.4 reshape.461
  157.4 1.4 reshape.460
  158.7 1.4 reshape.459
  160.1 1.4 reshape.450
  162.2 4.7 copy.91
  166.9 3.2 copy.103
  170.1 2.3 copy.89
  172.4 2.7 copy.102
  175.7 19.0 %merge_qkv.1 = (bf16[1536,768]{1,0:T(8,128)(2,1)}, f32[1536,768]{1,0:T(8,128)}, bf16[1536,768]{1,0:T(8,128)(2,1)}, bf16[1536,2304]{1,0:T(8,128)(2,1)}, f32[8,768]{1,0:T(8,128)}) custom-call(bf16[1536,768]{1,0:T(8,128)(2,1)} %bitcast.151, f32[6,1,256]{2,1,0:T(1,128)} %and_convert_fusion.live_row, f32[1536,1]{1,0:T(8,128)} %fusion.1.live_col, ...), custom_call_target="tpu_custom_call" | custom-call | tf_op jit(solution)/shard_map/merge_qkv/pallas_call | solution.py:363
  194.8 41.4 %attention.1 = (bf16[3,512,768]{2,1,0:T(8,128)(2,1)}, f32[3,6,2,512]{3,2,1,0:T(2,128)}) custom-call(bf16[3,512,2304]{2,1,0:T(8,128)(2,1)} %bitcast.127, bf16[3,512,2304]{2,1,0:T(8,128)(2,1)} %bitcast.128, bf16[3,512,2304]{2,1,0:T(8,128)(2,1)} %bitcast.129, f32[3,512,1]{2,1,0:T(8,128)} %and_select_fusion.bias_ref), custom_call_target="tpu_custom_call" | custom-call | tf_op jit(solution)/shard_map/attention/pallas_call | solution.py:401
  237.0 54.1 %ffn.1 = (bf16[1536,768]{1,0:T(8,128)(2,1)}, bf16[1536,3072]{1,0:T(8,128)(2,1)}, bf16[1536,3072]{1,0:T(8,128)(2,1)}, bf16[1536,768]{1,0:T(8,128)(2,1)}, bf16[153...) custom-call(bf16[1536,768]{1,0:T(8,128)(2,1)} %bitcast.157, ...), custom_call_target="tpu_custom_call" | custom-call | tf_op jit(solution)/shard_map/ffn/pallas_call | solution.py:415
  291.1 4.8 convolution_convert_fusion.3
  297.6 38.8 %attention_back.1 = (bf16[3,512,768]{2,1,0:T(8,128)(2,1)}, bf16[3,512,768]{2,1,0:T(8,128)(2,1)}, bf16[3,512,768]{2,1,0:T(8,128)(2,1)}) custom-call(bf16[3,512,2304]{2,1,0:T(8,128)(2,1)} %bitcast.130, bf16[3,512,2304]{2,1,0:T(8,128)(2,1)} %bitcast.131, bf16[3,512,2304]{2,1,0:T(8,128)(2,1)} %bitcast.132, f32[3,512,1]{2,1,0:T(8,128)} %and_select_fusion.bias_ref, ...), custom_call_target="tpu_custom_call" | custom-call | tf_op jit(solution)/shard_map/attention_back/pallas_call | solution.py:459
  336.3 20.6 %merge_back.1 = (bf16[1536,768]{1,0:T(8,128)(2,1)}, bf16[1536,768]{1,0:T(8,128)(2,1)}, bf16[1536,2304]{1,0:T(8,128)(2,1)}, f32[8,768]{1,0:T(8,128)}) custom-call(bf16[1536,768]{1,0:T(8,128)(2,1)} %bitcast.159, bf16[1536,768]{1,0:T(8,128)(2,1)} %bitcast.160, bf16[1536,768]{1,0:T(8,128)(2,1)} %bitcast.161, f32[1536,768]{1,0:T(8,128)} %get-tuple-element.52.grad_two, ...), custom_call_target="tpu_custom_call" | custom-call | tf_op jit(solution)/shard_map/merge_back/pallas_call | solution.py:469
  358.9 5.3 convolution_convert_fusion.4
  364.2 6.0 convolution_convert_fusion.1
  370.2 5.7 reshape.472
  376.0 3.1 copy.93
  379.1 12.8 %convolution_convert_fusion.2 = bf16[768,3072]{1,0:T(8,128)(2,1)} fusion(bf16[1536,768]{1,0:T(8,128)(2,1)S(1)} %copy-done.32, bf16[1536,3072]{1,0:T(8,128)(2,1)} %get-tuple-element.60), kind=kOutput, calls=%fused_computation.2 | convolution fusion | flops 7250116608 | bytes 16515072 | tf_op jit(solution)/shard_map/dot_general | solution.py:32
  391.9 9.7 %reshape.474 = bf16[32,24,4,768]{3,2,1,0:T(4,128)(2,1)} reshape(bf16[768,3072]{1,0:T(8,128)(2,1)} %convolution_convert_fusion.2) | data formatting | bytes 9437184 | tf_op jit(solution)/shard_map/reshape | solution.py:513
  401.7 3.4 copy.94
  406.2 10.3 %convolution_convert_fusion = bf16[3072,768]{1,0:T(8,128)(2,1)S(1)} fusion(bf16[1536,3072]{1,0:T(8,128)(2,1)} %get-tuple-element.61, bf16[1536,768]{1,0:T(8,128)(2,1)S(1)} %copy-done.31), kind=kOutput, calls=%fused_computation | convolution fusion | flops 7250116608 | bytes 16515072 | tf_op jit(solution)/shard_map/dot_general | solution.py:32
  416.5 1.1 constant_dynamic-update-slice_fusion.15
  417.6 2.0 constant_dynamic-update-slice_fusion.14
  419.6 2.5 constant_dynamic-update-slice_fusion.13
  422.1 2.5 constant_dynamic-update-slice_fusion.12
  426.1 5.2 all-gather.2
  432.0 1.4 slice_reduce_fusion.11
  433.5 1.5 slice_reduce_fusion.8
  434.9 4.0 stack.27
  438.9 38.4 %psum.7 = f32[6]{0:T(128)S(1)} all-reduce(f32[6]{0:T(128)S(1)} %stack.27), channel_id=1, replica_groups=mesh['table'=8,'batch'=4] {'table','batch'}, use_global_device_ids=true, to_apply=%region_9.10 | all-reduce | flops 6 | bytes 48 | tf_op jit(solution)/shard_map/psum | solution.py:563
  479.4 5.7 all-gather.1
  485.0 1.1 convolution_bitcast_fusion
  487.6 107.0 %reduce-scatter.2.cloned.1.call-done = bf16[1,320,768]{2,1,0:T(8,128)(2,1)} async-done(((bf16[32,320,768]{2,1,0:T(8,128)(2,1)}), bf16[1,320,768]{2,1,0:T(8,128)(2,1)}) %reduce-scatter.2.cloned.1.call-update) | async-done | bytes 491536 | tf_op jit(solution)/shard_map/reduce_scatter | solution.py:531
  594.6 1.2 convert_bitcast_fusion
  (169 shorter events, 38.5 us)
Async XLA Ops:
  7.2 42.0 %copy-start.19 = (s32[3]{0:T(128)S(1)}, s32[3]{0:T(128)}, u32[]{:S(2)}) copy-start(s32[3]{0:T(128)} %param.23) | copy-start | bytes 40
  7.2 127.3 %all-gather.5.cloned.1.call-start = ((), (), s32[]{:S(2)}) async-start(), calls=%async_computation.2 | async-start | bytes 16220160 | tf_op jit(solution)/shard_map/all_gather | solution.py:313
  21.3 0.8 copy-start.7
  22.1 572.5 %reduce-scatter.2.cloned.1.call-start = ((), (), s32[]{:S(2)}) async-start(), calls=%async_computation.1 | async-start | bytes 16220160 | tf_op jit(solution)/shard_map/reduce_scatter | solution.py:531
  36.8 0.5 copy-start.27
  36.9 100.1 %copy-start.23 = (f32[128]{0:T(128)}, f32[128]{0:T(128)S(1)}, u32[]{:S(2)}) copy-start(f32[128]{0:T(128)S(1)} %iota_convert_fusion) | copy-start | bytes 1540
  37.4 99.6 %copy-start.25 = (f32[3]{0:T(128)}, f32[3]{0:T(128)S(1)}, u32[]{:S(2)}) copy-start(f32[3]{0:T(128)S(1)} %select_reduce_fusion) | copy-start | bytes 40
  46.3 0.9 copy-start.1
  172.4 2.7 copy-start.10
  172.4 2.7 copy-start.11
  172.4 2.7 copy-start.12
  194.7 41.5 %copy-start.13 = (f32[1,768]{1,0:T(1,128)S(1)}, f32[1,768]{1,0:T(1,128)}, u32[]{:S(2)}) copy-start(f32[1,768]{1,0:T(1,128)} %reshape.464) | copy-start | bytes 9220
  194.7 41.4 %copy-start.14 = (f32[1,768]{1,0:T(1,128)S(1)}, f32[1,768]{1,0:T(1,128)}, u32[]{:S(2)}) copy-start(f32[1,768]{1,0:T(1,128)} %reshape.463) | copy-start | bytes 9220
  194.7 41.4 %copy-start.15 = (f32[1,768]{1,0:T(1,128)S(1)}, f32[1,768]{1,0:T(1,128)}, u32[]{:S(2)}) copy-start(f32[1,768]{1,0:T(1,128)} %reshape.462) | copy-start | bytes 9220
  194.7 41.4 %copy-start.16 = (f32[1,768]{1,0:T(1,128)S(1)}, f32[1,768]{1,0:T(1,128)}, u32[]{:S(2)}) copy-start(f32[1,768]{1,0:T(1,128)} %reshape.461) | copy-start | bytes 9220
  194.7 41.4 %copy-start.17 = (f32[1,768]{1,0:T(1,128)S(1)}, f32[1,768]{1,0:T(1,128)}, u32[]{:S(2)}) copy-start(f32[1,768]{1,0:T(1,128)} %reshape.460) | copy-start | bytes 9220
  194.8 41.4 %copy-start.18 = (f32[1,768]{1,0:T(1,128)S(1)}, f32[1,768]{1,0:T(1,128)}, u32[]{:S(2)}) copy-start(f32[1,768]{1,0:T(1,128)} %reshape.459) | copy-start | bytes 9220
  194.8 41.5 %copy-start.9 = (f32[1,3072]{1,0:T(1,128)S(1)}, f32[1,3072]{1,0:T(1,128)}, u32[]{:S(2)}) copy-start(f32[1,3072]{1,0:T(1,128)} %reshape.465) | copy-start | bytes 36868
  194.8 41.5 %copy-start.29 = (f32[8]{0:T(128)S(1)}, f32[8]{0:T(128)}, u32[]{:S(2)}) copy-start(f32[8]{0:T(128)} %pad.25.clone) | copy-start | bytes 100
  237.0 54.1 %copy-start.3 = (bf16[3,512,768]{2,1,0:T(8,128)(2,1)S(1)}, bf16[3,512,768]{2,1,0:T(8,128)(2,1)}, u32[]{:S(2)}) copy-start(bf16[3,512,768]{2,1,0:T(8,128)(2,1)} %get-tuple-element.44) | copy-start | bytes 7077892
  291.1 4.8 copy-start.8
  336.3 22.5 %copy-start = (bf16[3,512,768]{2,1,0:T(8,128)(2,1)S(1)}, bf16[3,512,768]{2,1,0:T(8,128)(2,1)}, u32[]{:S(2)}) copy-start(bf16[3,512,768]{2,1,0:T(8,128)(2,1)} %param.22) | copy-start | bytes 7077892
  358.0 6.2 %slice-start = ((s8[7077888]{0:T(1024)(128)(4,1)}), s8[4194304]{0:T(1024)(128)(4,1)S(1)}, s32[]{:S(2)}) async-start(s8[7077888]{0:T(1024)(128)(4,1)} %bitcast.174), calls=%async_computation.3 | async-start | bytes 8388608
  358.9 5.4 slice-start.1
  358.9 5.4 copy-start.30
  376.0 3.1 copy-start.32
  401.7 3.4 copy-start.6
  401.7 4.5 copy-start.31
  406.2 10.3 %copy-start.5 = (bf16[768,768]{1,0:T(8,128)(2,1)S(1)}, bf16[768,768]{1,0:T(8,128)(2,1)}, u32[]{:S(2)}) copy-start(bf16[768,768]{1,0:T(8,128)(2,1)} %convolution_convert_fusion.3) | copy-start | bytes 3538948
  422.1 2.5 copy-start.4
  425.4 0.7 copy-start.22
  425.4 5.9 copy-start.20
  425.4 5.9 copy-start.21
  425.4 6.6 %copy-start.33 = (s32[12]{0:T(128)S(1)}, s32[12]{0:T(128)}, u32[]{:S(2)}) copy-start(s32[12]{0:T(128)} %param.25) | copy-start | bytes 148
  425.4 6.6 %copy-start.28 = (s32[3]{0:T(128)S(1)}, s32[3]{0:T(128)}, u32[]{:S(2)}) copy-start(s32[3]{0:T(128)} %copy-done.27) | copy-start | bytes 40
  425.4 60.7 %copy-start.2 = (bf16[4,768,128]{2,1,0:T(8,128)(2,1)S(1)}, bf16[4,768,128]{2,1,0:T(8,128)(2,1)}, u32[]{:S(2)}) copy-start(bf16[4,768,128]{2,1,0:T(8,128)(2,1)} %copy-done.1) | copy-start | bytes 2359300
  425.4 61.5 %copy-start.24 = (f32[128]{0:T(128)S(1)}, f32[128]{0:T(128)}, u32[]{:S(2)}) copy-start(f32[128]{0:T(128)} %copy-done.23) | copy-start | bytes 1540
  425.4 61.5 %copy-start.26 = (f32[3]{0:T(128)S(1)}, f32[3]{0:T(128)}, u32[]{:S(2)}) copy-start(f32[3]{0:T(128)} %copy-done.25) | copy-start | bytes 40
Sparse Core Ops, SparseCore 0:
  22.2 112.2 all-gather.4
  425.6 168.9 reduce-scatter.1

commit v2 on v1

--- a/solution.py
+++ b/solution.py
@@ -268,6 +268,260 @@
     return pl.BlockSpec((size, width), lambda i: (i, 0))
 
 
+MESH = pl.DeviceIdType.MESH
+TABLE_MAJOR = 4
+CORES = 2
+
+
+def here(dims):
+    table, batch = lax.axis_index("table"), lax.axis_index("batch")
+    return [table // dims[1], lax.rem(table, dims[1]), batch // CORES, lax.rem(batch, CORES)]
+
+
+def peer(dims, spot, axis, offset):
+    other = list(spot)
+    other[axis] = lax.rem(spot[axis] + offset, dims[axis])
+    return (other[0] * dims[1] + other[1], other[2] * CORES + other[3]), other[axis]
+
+
+def greet(dims, spot):
+    barrier = pltpu.get_barrier_semaphore()
+    total = 0
+    for axis in range(4):
+        for offset in range(1, dims[axis]):
+            target, _ = peer(dims, spot, axis, offset)
+            pl.semaphore_signal(barrier, inc=1, device_id=target, device_id_type=MESH)
+            total += 1
+    pl.semaphore_wait(barrier, total)
+
+
+def gather_kernel(dims, orders, *refs):
+    count = len(orders)
+    shards, fulls = refs[:count], refs[count : 2 * count]
+    local_sem, send_sem, recv_sem = refs[2 * count :]
+    spot = here(dims)
+    greet(dims, spot)
+    sent = {}
+
+    def start(item, stage):
+        axis = orders[item][stage]
+        done = orders[item][:stage]
+        where = tuple(slice(None) if a in done else spot[a] for a in range(4))
+        source = fulls[item].at[where] if stage else shards[item]
+        for offset in range(1, dims[axis]):
+            copy = pltpu.make_async_remote_copy(
+                src_ref=source,
+                dst_ref=fulls[item].at[where],
+                send_sem=send_sem.at[item, stage, offset],
+                recv_sem=recv_sem.at[item, stage, offset],
+                device_id=peer(dims, spot, axis, offset)[0],
+                device_id_type=MESH,
+            )
+            copy.start()
+            sent[item, stage, offset] = copy
+
+    def finish(item, stage):
+        for offset in range(1, dims[orders[item][stage]]):
+            sent[item, stage, offset].wait_recv()
+
+    kept = []
+    for item in range(count):
+        copy = pltpu.make_async_copy(shards[item], fulls[item].at[tuple(spot)], local_sem.at[item])
+        copy.start()
+        kept.append(copy)
+        start(item, 0)
+    pairs = (count + 1) // 2
+    for slot in range(pairs + 3):
+        for stage in (3, 2, 1, 0):
+            pair = slot - stage
+            for item in range(2 * pair, min(2 * pair + 2, count)) if 0 <= pair < pairs else ():
+                finish(item, stage)
+                if stage == 0:
+                    kept[item].wait()
+                if stage < 3:
+                    start(item, stage + 1)
+    for copy in sent.values():
+        copy.wait_send()
+
+
+def scatter_kernel(dims, items, arrays, *refs):
+    count = len(items)
+    grads, square, outs, total_out = refs[:arrays], refs[arrays], refs[arrays + 1 : 2 * arrays + 1], refs[2 * arrays + 1]
+    refs = refs[2 * arrays + 2 :]
+    buffers = [refs[i * 7 : (i + 1) * 7] for i in range(count)]
+    square_sum, square_got, local_sem, send_sem, recv_sem = refs[7 * count :]
+    spot = here(dims)
+    greet(dims, spot)
+    sent = {}
+
+    def send(key, index, source, landing, axis, offset):
+        copy = pltpu.make_async_remote_copy(
+            src_ref=source,
+            dst_ref=landing,
+            send_sem=send_sem.at[index],
+            recv_sem=recv_sem.at[index],
+            device_id=peer(dims, spot, axis, offset)[0],
+            device_id_type=MESH,
+        )
+        copy.start()
+        sent.setdefault(key, []).append(copy)
+
+    def slot_of(item, stage, offset):
+        return item, stage, offset
+
+    def square_start(stage):
+        axis = 3 - stage
+        for offset in range(1, dims[axis]):
+            send(("square", stage), (count, stage, offset), square_sum.at[stage], square_got.at[stage, offset - 1], axis, offset)
+
+    def square_finish(stage):
+        for copy in sent["square", stage]:
+            copy.wait_recv()
+        value = square_sum[stage]
+        for offset in range(1, dims[3 - stage]):
+            value = value + square_got[stage, offset - 1]
+        square_sum[stage + 1] = value
+
+    def start(item, stage):
+        array, low, size, order = items[item]
+        own, first, second, got_core, got_first, got_second, got_last = buffers[item]
+        axis = order[stage]
+        for offset in range(1, dims[axis]):
+            _, other = peer(dims, spot, axis, offset)
+            index = slot_of(item, stage, offset)
+            if stage == 0:
+                source, landing = grads[array].at[:, :, :, other, :, pl.ds(low, size)], got_core
+            elif stage == 1:
+                source = own.at[:, :, other] if axis == 2 else own.at[:, other]
+                landing = got_first.at[offset - 1]
+            elif stage == 2:
+                source, landing = first.at[:, other], got_second.at[offset - 1]
+            else:
+                source, landing = second.at[other], got_last.at[offset - 1]
+            send((item, stage), index, source, landing, axis, offset)
+
+    def finish(item, stage):
+        array, low, size, order = items[item]
+        own, first, second, got_core, got_first, got_second, got_last = buffers[item]
+        axis = order[stage]
+        others = range(dims[axis] - 1)
+        mine = spot[axis]
+        for copy in sent[item, stage]:
+            copy.wait_recv()
+        if stage == 0:
+            loads[item].wait()
+
+            @pl.loop(0, dims[0] * dims[1] * dims[2])
+            def _(i):
+                at = (i // (dims[1] * dims[2]), lax.rem(i // dims[2], dims[1]), lax.rem(i, dims[2]))
+                own[at] = (own[at].astype(F32) + got_core[at].astype(F32)).astype(BF16)
+        elif stage == 1:
+            inner = first.shape[1]
+
+            @pl.loop(0, dims[0] * inner)
+            def _(i):
+                at = (i // inner, lax.rem(i, inner))
+                value = own[(*at, mine) if axis == 2 else (at[0], mine, at[1])].astype(F32)
+                for k in others:
+                    value += got_first[(k, *at)].astype(F32)
+                first[at] = value.astype(BF16)
+        elif stage == 2:
+
+            @pl.loop(0, dims[0])
+            def _(i):
+                value = first[i, mine].astype(F32)
+                for k in others:
+                    value += got_second[k, i].astype(F32)
+                second[i] = value.astype(BF16)
+        else:
+            value = second[mine].astype(F32)
+            for k in others:
+                value += got_last[k].astype(F32)
+            outs[array][:, low : low + size] = value
+
+    square_sum[0] = square[...]
+    loads = []
+    for item, (array, low, size, _) in enumerate(items):
+        copy = pltpu.make_async_copy(
+            grads[array].at[:, :, :, spot[3], :, pl.ds(low, size)], buffers[item][0], local_sem.at[item]
+        )
+        copy.start()
+        loads.append(copy)
+        start(item, 0)
+    square_start(0)
+    pairs = (count + 1) // 2
+    for slot in range(pairs + 3):
+        for stage in (3, 2, 1, 0):
+            pair = slot - stage
+            for item in range(2 * pair, min(2 * pair + 2, count)) if 0 <= pair < pairs else ():
+                finish(item, stage)
+                if stage < 3:
+                    start(item, stage + 1)
+        if slot < 4:
+            square_finish(slot)
+            if slot < 3:
+                square_start(slot + 1)
+    total_out[...] = square_sum[4]
+    for group in sent.values():
+        for copy in group:
+            copy.wait_send()
+
+
+def gather_all(dims, shards, orders):
+    anywhere = pl.BlockSpec(memory_space=pl.ANY)
+    most = max(dims)
+    count = len(shards)
+    return pl.pallas_call(
+        functools.partial(gather_kernel, dims, orders),
+        in_specs=[pl.BlockSpec(memory_space=pltpu.VMEM)] * count,
+        out_specs=[anywhere] * count,
+        out_shape=[jax.ShapeDtypeStruct((*dims, *a.shape), a.dtype) for a in shards],
+        scratch_shapes=[
+            pltpu.SemaphoreType.DMA((count,)),
+            pltpu.SemaphoreType.DMA((count, 4, most)),
+            pltpu.SemaphoreType.DMA((count, 4, most)),
+        ],
+        compiler_params=params(collective_id=0, has_side_effects=True),
+        name="gather_weights",
+    )(*shards)
+
+
+def scatter_all(dims, grads, square, items):
+    most = max(dims)
+    count = len(items)
+    scratch = []
+    for array, _, size, order in items:
+        tail = (grads[array].shape[4], size)
+        inner = dims[order[2]]
+        for shape in (
+            dims[:3],
+            (dims[0], inner),
+            (dims[0],),
+            dims[:3],
+            (dims[order[1]] - 1, dims[0], inner),
+            (inner - 1, dims[0]),
+            (dims[0] - 1,),
+        ):
+            scratch.append(pltpu.VMEM((*shape, *tail), BF16))
+    vmem = pl.BlockSpec(memory_space=pltpu.VMEM)
+    scratch += [
+        pltpu.VMEM((5, *square.shape), F32),
+        pltpu.VMEM((4, most - 1, *square.shape), F32),
+        pltpu.SemaphoreType.DMA((count,)),
+        pltpu.SemaphoreType.DMA((count + 1, 4, most)),
+        pltpu.SemaphoreType.DMA((count + 1, 4, most)),
+    ]
+    return pl.pallas_call(
+        functools.partial(scatter_kernel, dims, items, len(grads)),
+        in_specs=[pl.BlockSpec(memory_space=pl.ANY)] * len(grads) + [vmem],
+        out_specs=[vmem] * (len(grads) + 1),
+        out_shape=[jax.ShapeDtypeStruct(g.shape[4:], F32) for g in grads] + [jax.ShapeDtypeStruct(square.shape, F32)],
+        scratch_shapes=scratch,
+        compiler_params=params(collective_id=1, has_side_effects=True),
+        name="scatter_grads",
+    )(*grads, square)
+
+
 def body(
     tokens,
     row_blocks,
@@ -305,25 +559,42 @@
     def cut(mat, n):
         return [mat[:, i * width : (i + 1) * width] for i in range(n)]
 
+    table_size, batch_size = lax.axis_size("table"), lax.axis_size("batch")
+    dims = (TABLE_MAJOR, table_size // TABLE_MAJOR, batch_size // CORES, CORES)
+    direct = share % BLOCK == 0
     vec_list = (out_bias, gain_one, shift_one, down_bias, gain_two, shift_two, query_bias, value_bias)
     vec_row = jnp.concatenate([*vec_list, up_bias])
     used = vec_row.shape[0]
     vec_row = jnp.pad(vec_row, (0, 8 * width - used)).reshape(8, width)
-    mine = jnp.concatenate([merge_w, out_w, *cut(qkv_w, 3), *cut(up_w, wide_ff), down_w, vec_row], axis=0)
-    gathered = lax.all_gather(mine, BOTH, axis=0)
-
-    def unit(start, n):
-        part = gathered[:, start : start + n * share]
-        part = part.reshape(devices, n, share, width).transpose(0, 2, 1, 3)
-        return part.reshape(width, n * width)
-
-    merge_full = unit(0, 1)
-    out_full = unit(share, 1)
-    qkv_full = unit(2 * share, 3)
-    up_full = unit(5 * share, wide_ff)
     base = (5 + wide_ff) * share
-    down_full = gathered[:, base : base + wide_ff * share].reshape(ff, width)
-    vec_rows = gathered[:, base + wide_ff * share].astype(F32)
+    if direct:
+        y_first, x_first = (0, 1, 2, 3), (0, 2, 1, 3)
+        qkv_full, down_full, merge_full, up_full, out_full, vec_full = gather_all(
+            dims,
+            (qkv_w, down_w, merge_w, up_w, out_w, vec_row),
+            (y_first, x_first, y_first, y_first, x_first, x_first),
+        )
+        qkv_full = qkv_full.reshape(width, 3 * width)
+        down_full = down_full.reshape(ff, width)
+        merge_full = merge_full.reshape(width, width)
+        up_full = up_full.reshape(width, ff)
+        out_full = out_full.reshape(width, width)
+        vec_rows = vec_full.reshape(devices, 8, width)[:, 0].astype(F32)
+    else:
+        mine = jnp.concatenate([merge_w, out_w, *cut(qkv_w, 3), *cut(up_w, wide_ff), down_w, vec_row], axis=0)
+        gathered = lax.all_gather(mine, BOTH, axis=0)
+
+        def unit(start, n):
+            part = gathered[:, start : start + n * share]
+            part = part.reshape(devices, n, share, width).transpose(0, 2, 1, 3)
+            return part.reshape(width, n * width)
+
+        merge_full = unit(0, 1)
+        out_full = unit(share, 1)
+        qkv_full = unit(2 * share, 3)
+        up_full = unit(5 * share, wide_ff)
+        down_full = gathered[:, base : base + wide_ff * share].reshape(ff, width)
+        vec_rows = gathered[:, base + wide_ff * share].astype(F32)
     vectors = [vec_rows[:, i * share : (i + 1) * share].reshape(1, width) for i in range(8)]
     up_bias_full = vec_rows[:, 8 * share : 8 * share + wide_ff * share].reshape(1, ff)
     query_vec, value_vec = vectors[6], vectors[7]
@@ -509,31 +780,72 @@
     grad_up_w = t_mm(ffn_in, grad_up).astype(BF16)
     grad_down_w = t_mm(activated, grad_down).astype(BF16)
 
-    def owners(mat, n):
-        return mat.reshape(devices, share, n, width).transpose(0, 2, 1, 3).reshape(devices, n * share, width)
-
     vec_grads = (sums[8], sums[3], sums[4], sums[2], sums[0], sums[1], bias_sums[0], bias_sums[1])
     vec_block = jnp.concatenate(
         [v.reshape(devices, share) for v in vec_grads] + [up_sums[0].reshape(devices, wide_ff * share)], axis=1
     )
     vec_block = jnp.pad(vec_block, ((0, 0), (0, 8 * width - used))).astype(BF16).reshape(devices, 8, width)
-    all_grads = jnp.concatenate(
+    partial = jnp.stack(
         [
-            owners(grad_merge_w, 1),
-            owners(grad_out_w, 1),
-            owners(grad_qkv_w, 3),
-            owners(grad_up_w, wide_ff),
-            grad_down_w.reshape(devices, wide_ff * share, width),
-            vec_block,
-        ],
-        axis=1,
+            jnp.sum(squares[0]),
+            jnp.sum(squares[1]),
+            jnp.sum(sums[5]),
+            jnp.sum(sums[6]),
+            jnp.sum(sums[7]),
+            jnp.sum(live_mask),
+        ]
     )
-    owned = lax.psum_scatter(all_grads, BOTH, scatter_dimension=0, tiled=True)[0].astype(F32)
-
-    def joined(start, n):
-        return jnp.concatenate([owned[start + i * share : start + (i + 1) * share] for i in range(n)], axis=1)
-
-    own_vec = owned[base + wide_ff * share]
+    if direct:
+        y_first, x_first = (3, 1, 2, 0), (3, 2, 1, 0)
+        half_ff, half_qkv, half = ff // 2, 3 * width // 2, width // 2
+        items = (
+            (0, 0, half_ff, x_first),
+            (1, 0, half, y_first),
+            (0, half_ff, half_ff, x_first),
+            (1, half, half, y_first),
+            (2, 0, half_qkv, x_first),
+            (2, half_qkv, half_qkv, y_first),
+            (3, 0, width, x_first),
+            (4, 0, width, y_first),
+            (5, 0, width, x_first),
+        )
+        square = jnp.broadcast_to(jnp.pad(partial, (0, 2))[:, None], (8, 128))
+        own_up, own_down, own_qkv, own_merge, own_out, own_vec, square = scatter_all(
+            dims,
+            [
+                g.reshape(*dims, -1, g.shape[-1])
+                for g in (grad_up_w, grad_down_w, grad_qkv_w, grad_merge_w, grad_out_w, vec_block)
+            ],
+            square,
+            items,
+        )
+        own_vec = own_vec[0]
+        totals = square[:6, 0]
+    else:
+        def owners(mat, n):
+            return mat.reshape(devices, share, n, width).transpose(0, 2, 1, 3).reshape(devices, n * share, width)
+
+
+        all_grads = jnp.concatenate(
+            [
+                owners(grad_merge_w, 1),
+                owners(grad_out_w, 1),
+                owners(grad_qkv_w, 3),
+                owners(grad_up_w, wide_ff),
+                grad_down_w.reshape(devices, wide_ff * share, width),
+                vec_block,
+            ],
+            axis=1,
+        )
+        owned = lax.psum_scatter(all_grads, BOTH, scatter_dimension=0, tiled=True)[0].astype(F32)
+
+        def joined(start, n):
+            return jnp.concatenate([owned[start + i * share : start + (i + 1) * share] for i in range(n)], axis=1)
+
+        own_vec = owned[base + wide_ff * share]
+        own_merge, own_qkv, own_out, own_up = joined(0, 1), joined(2 * share, 3), joined(share, 1), joined(5 * share, wide_ff)
+        own_down = owned[base : base + wide_ff * share]
+        totals = lax.psum(partial, BOTH)
     own_vecs = [own_vec[i * share : (i + 1) * share] for i in range(8)]
     own_up_bias = own_vec[8 * share : 8 * share + wide_ff * share]
 
@@ -550,33 +862,22 @@
     grad_head = lax.dot_general(
         group_cls.astype(F32), group_dlog, (((0,), (0,)), ((), ())), precision=PRECISE, preferred_element_type=F32
     )[None]
-    partial = jnp.stack(
-        [
-            jnp.sum(squares[0]),
-            jnp.sum(squares[1]),
-            jnp.sum(sums[5]),
-            jnp.sum(sums[6]),
-            jnp.sum(sums[7]),
-            jnp.sum(live_mask),
-        ]
-    )
-    totals = lax.psum(partial, BOTH)
     root_squares = jnp.sqrt(totals[:5] / (totals[5] * width))
     return (
         layer_rows,
         logits,
         grad_input.reshape(rows, seq, width),
-        joined(0, 1),
-        joined(2 * share, 3),
+        own_merge,
+        own_qkv,
         own_vecs[6],
         own_vecs[7],
-        joined(share, 1),
+        own_out,
         own_vecs[0],
         own_vecs[1],
         own_vecs[2],
-        joined(5 * share, wide_ff),
+        own_up,
         own_up_bias,
-        owned[base : base + wide_ff * share],
+        own_down,
         own_vecs[3],
         own_vecs[4],
         own_vecs[5],

time: 617 us -> 514 us (0.83); the launches traced: 607 us -> 512 us
  Pallas kernels: 174 us -> 396 us
  waiting for transfers between devices: 190 us -> 0 us
  local copies, waits for them, and re-layouts: 106 us -> 35.4 us
  blocking collectives: 63.8 us -> 25.6 us
  between operations: 16.4 us -> 2.35 us
    pallas_call x0 -> x2, Pallas kernels: none -> 222 us  [the longest x1 126 us: gather_all(): pl.pallas_call(functools.partial(gather_kernel, dims, orders), in_specs=[...]
    reduce_scatter x1 -> x0, waiting for transfers between devices: 107 us -> none  [body(): lax.psum_scatter(all_grads, BOTH, scatter_dimension=0, tiled=True)[0]]
    all_gather x1 -> x0, waiting for transfers between devices: 83.3 us -> none  [body(): gathered = lax.all_gather(mine, BOTH, axis=0)]
    psum x1 -> x0, blocking collectives: 38.4 us -> none  [body(): totals = lax.psum(partial, BOTH)]
    reshape x3 -> x0, local copies, waits for them, and re-layouts: 20.1 us -> none  [the longest x2 15.5 us: owners(): mat.reshape(devices, share, n, width).transpose(0, 2, 1, 3)]
    unnamed x99 -> x40, local copies, waits for them, and re-layouts: 29 us -> 11.3 us
    slice x5 -> x1, local copies, waits for them, and re-layouts: 14.8 us -> 1.05 us  [body(): vec_rows = vec_full.reshape(devices, 8, width)[:, 0].astype(F32)]
    reshape x8, local copies, waits for them, and re-layouts: 10.4 us -> 0.7 us  [body(): vec_rows[:, i * share:(i + 1) * share].reshape(1, width)]
  transfers between devices with their start and end apart: 2 -> 0, of which waited for: 2 -> 0; matrix products, arithmetic and copies ran while one was open for 4% -> 0% of each run, Pallas kernels for 0% -> 0%
where the time goes in v2:
time: 514 us; the launch traced here: 512 us
  Pallas kernels  396 us (77%)
  matrix products  41 us (8%)
  local copies, waits for them, and re-layouts  35.4 us (7%)
  blocking collectives  25.6 us (5%)
  other arithmetic  12.6 us (2%)
    pallas_call x1, Pallas kernels, gather_all(): pl.pallas_call(functools.partial(gather_kernel, dims, orders), in_specs=[...  126 us
    pallas_call x1, Pallas kernels, scatter_all(): pl.pallas_call(functools.partial(scatter_kernel, dims, items, len(grads))...  96.6 us
    pallas_call x1, Pallas kernels, body(): pl.pallas_call(functools.partial(ffn_kernel, per_row), grid=(tiles,), in_...  53.9 us
    pallas_call x1, Pallas kernels, body(): pl.pallas_call(functools.partial(attn_kernel, head ** (-0.5)), grid=(rows...  41.3 us
    dot_general x5, matrix products, t_mm(): lax.dot_general(left, right, (((0,), (0,)), ((), ())), preferred_element_...  38.9 us
    pallas_call x1, Pallas kernels, body(): pl.pallas_call(functools.partial(attn_back_kernel, head ** (-0.5)), grid=...  38.7 us
    pallas_call x1, Pallas kernels, body(): pl.pallas_call(input_kernel, grid=(tiles,), in_specs=[tiled(TILE, width),...  20.5 us
    pallas_call x1, Pallas kernels, body(): pl.pallas_call(merge_kernel, grid=(tiles,), in_specs=[tiled(TILE, width),...  19 us

profile of v2, /device:TPU:0, one launch (start us, length us, event | category | flops | bytes accessed | tf_op | source)
XLA Modules:
  0.0 512.5 jit_solution(18015665484502440822)
XLA Ops:
  1.3 0.7 dynamic_slice.3
  2.7 1.2 dynamic-slice
  4.0 0.8 dynamic-update-slice
  4.7 6.4 %all-reduce.4 = s32[4]{0:T(128)S(1)} all-reduce(s32[4]{0:T(128)S(1)} %dynamic-update-slice), channel_id=1, replica_groups=mesh['table'=8,'batch'=4] {'batch'}, use_global_device_ids=true, to_apply=%add.4 | all-reduce | flops 4 | bytes 32
  11.3 6.1 %concatenate.16 = bf16[288]{0:T(512)(128)(2,1)S(1)} concatenate(bf16[24]{0:T(256)(128)(2,1)} %param.32, bf16[24]{0:T(256)(128)(2,1)} %param.33, bf16[24]{0:T(256)(128)(2,1)} %param.34, bf16[24]{0:T(256)(128)(2,1)} %param.38, bf16[24]{0:T(256)(128)(2,1)} %param.39, bf16[24]{0:T(256)(128)(2,1)} %param.40, bf16[24]{0:T(256)(128)(2,1)} %param.29, bf16[24]{0:T(256)(128)(2,1)} %param.30, ...), dimensions={0} | concatenate | bytes 1152 | tf_op jit(solution)/shard_map/concatenate | solution.py:566
  17.4 0.8 compare_select_fusion.1
  18.1 0.7 lt.148
  19.1 0.7 compare_bitcast_fusion
  19.9 5.3 %all-gather.1 = f32[4,3,128]{2,1,0:T(4,128)S(1)} all-gather(f32[1,3,128]{2,1,0:T(4,128)} %bitcast.130), channel_id=1, replica_groups=mesh['table'=8,'batch'=4] {'batch'}, dimensions={0}, use_global_device_ids=true | all-gather | bytes 7680 | tf_op jit(solution)/shard_map/all_gather | solution.py:619
  25.9 1.4 convert_reduce_fusion
  27.3 0.8 broadcast_in_dim.18
  28.3 0.7 and_convert_fusion.live_row
  29.7 1.0 fusion.1.live_col
  31.0 1.1 and_select_fusion.bias_ref
  32.1 8.7 %all_gather.13 = bf16[4,768,128]{2,1,0:T(8,128)(2,1)S(1)} all-gather(bf16[1,768,128]{2,1,0:T(8,128)(2,1)S(1)} %copy-done.1), channel_id=1, replica_groups=mesh['table'=8,'batch'=4] {'batch'}, dimensions={0}, use_global_device_ids=true | all-gather | bytes 983040 | tf_op jit(solution)/shard_map/all_gather | solution.py:617
  40.8 0.7 convolution_bitcast_fusion.1
  42.1 125.5 %gather_weights.1 = (bf16[4,2,2,2,24,2304]{5,4,3,2,1,0:T(8,128)(2,1)}, bf16[4,2,2,2,96,768]{5,4,3,2,1,0:T(8,128)(2,1)}, bf16[4,2,2,2,24,768]{5,4,3,2,1,0:T(8,128...) custom-call(bf16[24,2304]{1,0:T(8,128)(2,1)} %refs_0_.1, ...), custom_call_target="tpu_custom_call" | custom-call | tf_op jit(solution)/shard_map/gather_weights/pallas_call | solution.py:474
  167.7 1.1 slice.204
  170.4 0.7 fusion.2.vecs
  171.1 19.0 %merge_qkv.1 = (bf16[1536,768]{1,0:T(8,128)(2,1)}, f32[1536,768]{1,0:T(8,128)}, bf16[1536,768]{1,0:T(8,128)(2,1)}, bf16[1536,2304]{1,0:T(8,128)(2,1)}, f32[8,768]{1,0:T(8,128)}) custom-call(bf16[1536,768]{1,0:T(8,128)(2,1)} %bitcast.105, f32[6,1,256]{2,1,0:T(1,128)} %and_convert_fusion.live_row, f32[1536,1]{1,0:T(8,128)} %fusion.1.live_col, ...), custom_call_target="tpu_custom_call" | custom-call | tf_op jit(solution)/shard_map/merge_qkv/pallas_call | solution.py:634
  190.1 1.4 slice_reduce_fusion.11
  191.5 41.3 %attention.1 = (bf16[3,512,768]{2,1,0:T(8,128)(2,1)}, f32[3,6,2,512]{3,2,1,0:T(2,128)}) custom-call(bf16[3,512,2304]{2,1,0:T(8,128)(2,1)} %bitcast.97, bf16[3,512,2304]{2,1,0:T(8,128)(2,1)} %bitcast.98, bf16[3,512,2304]{2,1,0:T(8,128)(2,1)} %bitcast.99, f32[3,512,1]{2,1,0:T(8,128)} %and_select_fusion.bias_ref), custom_call_target="tpu_custom_call" | custom-call | tf_op jit(solution)/shard_map/attention/pallas_call | solution.py:672
  232.9 53.9 %ffn.1 = (bf16[1536,768]{1,0:T(8,128)(2,1)}, bf16[1536,3072]{1,0:T(8,128)(2,1)}, bf16[1536,3072]{1,0:T(8,128)(2,1)}, bf16[1536,768]{1,0:T(8,128)(2,1)}, bf16[153...) custom-call(bf16[1536,768]{1,0:T(8,128)(2,1)} %bitcast.116, ...), custom_call_target="tpu_custom_call" | custom-call | tf_op jit(solution)/shard_map/ffn/pallas_call | solution.py:686
  286.7 5.5 %convolution_convert_fusion.3 = bf16[768,768]{1,0:T(8,128)(2,1)} fusion(bf16[1536,768]{1,0:T(8,128)(2,1)} %bitcast.117, bf16[1536,768]{1,0:T(8,128)(2,1)} %get-tuple-element.81), kind=kOutput, calls=%fused_computation.3 | convolution fusion | flops 1812529152 | bytes 5898240 | tf_op jit(solution)/shard_map/dot_general | solution.py:32
  292.2 38.7 %attention_back.1 = (bf16[3,512,768]{2,1,0:T(8,128)(2,1)}, bf16[3,512,768]{2,1,0:T(8,128)(2,1)}, bf16[3,512,768]{2,1,0:T(8,128)(2,1)}) custom-call(bf16[3,512,2304]{2,1,0:T(8,128)(2,1)} %bitcast.100, bf16[3,512,2304]{2,1,0:T(8,128)(2,1)} %bitcast.101, bf16[3,512,2304]{2,1,0:T(8,128)(2,1)} %bitcast.102, f32[3,512,1]{2,1,0:T(8,128)} %and_select_fusion.bias_ref, ...), custom_call_target="tpu_custom_call" | custom-call | tf_op jit(solution)/shard_map/attention_back/pallas_call | solution.py:730
  330.9 20.5 %merge_back.1 = (bf16[1536,768]{1,0:T(8,128)(2,1)}, bf16[1536,768]{1,0:T(8,128)(2,1)}, bf16[1536,2304]{1,0:T(8,128)(2,1)}, f32[8,768]{1,0:T(8,128)}) custom-call(bf16[1536,768]{1,0:T(8,128)(2,1)} %bitcast.118, bf16[1536,768]{1,0:T(8,128)(2,1)} %bitcast.119, bf16[1536,768]{1,0:T(8,128)(2,1)} %bitcast.120, f32[1536,768]{1,0:T(8,128)} %get-tuple-element.71.grad_two, ...), custom_call_target="tpu_custom_call" | custom-call | tf_op jit(solution)/shard_map/merge_back/pallas_call | solution.py:740
  352.1 4.0 stack.27
  356.8 0.9 fusion.11
  358.4 0.8 slice.214
  359.3 0.7 compare_select_fusion
  360.0 0.7 convert.37
  361.1 5.2 %all-gather = bf16[12,1,768]{2,1,0:T(2,128)(2,1)S(1)} all-gather(bf16[3,1,768]{2,1,0:T(2,128)(2,1)S(1)} %slice.214), channel_id=2, replica_groups=mesh['table'=8,'batch'=4] {'batch'}, dimensions={0}, use_global_device_ids=true | all-gather | bytes 23040 | tf_op jit(solution)/shard_map/all_gather | solution.py:858
  366.3 1.1 convolution_bitcast_fusion
  367.5 0.8 copy.79
  368.3 11.6 %convolution_convert_fusion.1 = bf16[768,2304]{1,0:T(8,128)(2,1)} fusion(bf16[1536,768]{1,0:T(8,128)(2,1)} %get-tuple-element.78, bf16[1536,2304]{1,0:T(8,128)(2,1)} %get-tuple-element.79), kind=kOutput, calls=%fused_computation.1 | convolution fusion | flops 5437587456 | bytes 12976128 | tf_op jit(solution)/shard_map/dot_general | solution.py:32
  379.9 3.2 convolution_convert_fusion.4
  383.1 9.3 %convolution_convert_fusion.2 = bf16[768,3072]{1,0:T(8,128)(2,1)} fusion(bf16[1536,768]{1,0:T(8,128)(2,1)S(1)} %copy-done.5, bf16[1536,3072]{1,0:T(8,128)(2,1)S(1)} %bitcast.136), kind=kOutput, calls=%fused_computation.2 | convolution fusion | flops 7250116608 | bytes 16515072 | tf_op jit(solution)/shard_map/dot_general | solution.py:32
  392.4 9.5 %convolution_convert_fusion = bf16[3072,768]{1,0:T(8,128)(2,1)} fusion(bf16[1536,3072]{1,0:T(8,128)(2,1)S(1)} %bitcast.134, bf16[1536,768]{1,0:T(8,128)(2,1)S(1)} %copy-done.4), kind=kOutput, calls=%fused_computation | convolution fusion | flops 7250116608 | bytes 16515072 | tf_op jit(solution)/shard_map/dot_general | solution.py:32
  401.9 96.6 %scatter_grads.1 = (f32[24,3072]{1,0:T(8,128)}, f32[96,768]{1,0:T(8,128)}, f32[24,2304]{1,0:T(8,128)}, f32[24,768]{1,0:T(8,128)}, f32[24,768]{1,0:T(8,128)}, /*index=5*/f32[8,768]{1,0:T(8,128)}, f32[8,128]{1,0:T(8,128)}) custom-call(bf16[4,2,2,2,24,3072]{5,4,3,2,1,0:T(8,128)(2,1)} %bitcast.112, bf16[4,2,2,2,96,768]{5,4,3,2,1,0:T(8,128)(2,1)} %bitcast.113, ...), custom_call_target="tpu_custom_call" | custom-call | tf_op jit(solution)/shard_map/scatter_grads/pallas_call | solution.py:514
  498.4 1.2 slice.203
  500.3 1.3 sqrt_reduce_fusion
  501.6 1.3 slice_bitcast_fusion.3
  502.9 1.5 slice_bitcast_fusion
  504.4 1.5 copy.96
  505.9 1.6 copy.97
  507.5 1.5 copy.98
  509.1 1.7 copy.99
  510.8 1.7 copy.100
  (93 shorter events, 7.8 us)
Async XLA Ops:
  0.7 30.3 %copy-start.3 = (s32[3]{0:T(128)S(1)}, s32[3]{0:T(128)}, u32[]{:S(2)}) copy-start(s32[3]{0:T(128)} %param.23) | copy-start | bytes 40
  19.0 13.1 %copy-start.1 = (bf16[1,768,128]{2,1,0:T(8,128)(2,1)S(1)}, bf16[1,768,128]{2,1,0:T(8,128)(2,1)}, u32[]{:S(2)}) copy-start(bf16[1,768,128]{2,1,0:T(8,128)(2,1)} %param.41) | copy-start | bytes 589828
  330.9 20.5 %copy-start.2 = (f32[16,768]{1,0:T(8,128)S(1)}, f32[16,768]{1,0:T(8,128)}, u32[]{:S(2)}) copy-start(f32[16,768]{1,0:T(8,128)} %get-tuple-element.82) | copy-start | bytes 147460
  367.4 15.6 %slice-start.3 = ((s8[9437184]{0:T(1024)(128)(4,1)}), s8[4194304]{0:T(1024)(128)(4,1)S(1)}, s32[]{:S(2)}) async-start(s8[9437184]{0:T(1024)(128)(4,1)} %bitcast.135), calls=%async_computation.3 | async-start | bytes 8388608
  368.3 11.6 %copy-start = (bf16[3,512,768]{2,1,0:T(8,128)(2,1)S(1)}, bf16[3,512,768]{2,1,0:T(8,128)(2,1)}, u32[]{:S(2)}) copy-start(bf16[3,512,768]{2,1,0:T(8,128)(2,1)} %param.22) | copy-start | bytes 7077892
  368.3 11.6 %copy-start.6 = (bf16[1536,768]{1,0:T(8,128)(2,1)S(1)}, bf16[1536,768]{1,0:T(8,128)(2,1)}, u32[]{:S(2)}) copy-start(bf16[1536,768]{1,0:T(8,128)(2,1)} %get-tuple-element.80) | copy-start | bytes 7077892
  368.3 14.8 %slice-start.4 = ((s8[9437184]{0:T(1024)(128)(4,1)}), s8[4194304]{0:T(1024)(128)(4,1)S(1)}, s32[]{:S(2)}) async-start(s8[9437184]{0:T(1024)(128)(4,1)} %bitcast.135), calls=%async_computation.4 | async-start | bytes 8388608
  368.3 14.8 %slice-start.5 = ((s8[9437184]{0:T(1024)(128)(4,1)}), s8[1048576]{0:T(1024)(128)(4,1)S(1)}, s32[]{:S(2)}) async-start(s8[9437184]{0:T(1024)(128)(4,1)} %bitcast.135), calls=%async_computation.5 | async-start | bytes 2097152
  379.9 3.2 copy-start.5
  379.9 12.5 %slice-start = ((s8[9437184]{0:T(1024)(128)(4,1)}), s8[4194304]{0:T(1024)(128)(4,1)S(1)}, s32[]{:S(2)}) async-start(s8[9437184]{0:T(1024)(128)(4,1)} %bitcast.133), calls=%async_computation | async-start | bytes 8388608
  383.1 9.3 %slice-start.1 = ((s8[9437184]{0:T(1024)(128)(4,1)}), s8[4194304]{0:T(1024)(128)(4,1)S(1)}, s32[]{:S(2)}) async-start(s8[9437184]{0:T(1024)(128)(4,1)} %bitcast.133), calls=%async_computation.1 | async-start | bytes 8388608
  383.1 9.3 %slice-start.2 = ((s8[9437184]{0:T(1024)(128)(4,1)}), s8[1048576]{0:T(1024)(128)(4,1)S(1)}, s32[]{:S(2)}) async-start(s8[9437184]{0:T(1024)(128)(4,1)} %bitcast.133), calls=%async_computation.2 | async-start | bytes 2097152
  383.1 9.3 %copy-start.4 = (bf16[1536,768]{1,0:T(8,128)(2,1)S(1)}, bf16[1536,768]{1,0:T(8,128)(2,1)}, u32[]{:S(2)}) copy-start(bf16[1536,768]{1,0:T(8,128)(2,1)} %get-tuple-element.77) | copy-start | bytes 7077892

commit v3 on v2

--- a/solution.py
+++ b/solution.py
@@ -295,100 +295,86 @@
     pl.semaphore_wait(barrier, total)
 
 
-def gather_kernel(dims, orders, *refs):
-    count = len(orders)
-    shards, fulls = refs[:count], refs[count : 2 * count]
-    local_sem, send_sem, recv_sem = refs[2 * count :]
-    spot = here(dims)
-    greet(dims, spot)
-    sent = {}
-
-    def start(item, stage):
-        axis = orders[item][stage]
-        done = orders[item][:stage]
-        where = tuple(slice(None) if a in done else spot[a] for a in range(4))
-        source = fulls[item].at[where] if stage else shards[item]
-        for offset in range(1, dims[axis]):
-            copy = pltpu.make_async_remote_copy(
-                src_ref=source,
-                dst_ref=fulls[item].at[where],
+def gather_events(dims, spot, items, shards, fulls, local_sem, send_sem, recv_sem):
+    def region(item, done):
+        array, low, size, order = items[item]
+        where = tuple(slice(None) if axis in done else spot[axis] for axis in sorted(order))
+        return fulls[array].at[(*where, slice(None), pl.ds(low, size))]
+
+    def copies(item, stage):
+        array, low, size, order = items[item]
+        place = region(item, order[:stage])
+        return [
+            pltpu.make_async_remote_copy(
+                src_ref=place if stage else shards[array].at[:, pl.ds(low, size)],
+                dst_ref=place,
                 send_sem=send_sem.at[item, stage, offset],
                 recv_sem=recv_sem.at[item, stage, offset],
-                device_id=peer(dims, spot, axis, offset)[0],
+                device_id=peer(dims, spot, order[stage], offset)[0],
                 device_id_type=MESH,
             )
-            copy.start()
-            sent[item, stage, offset] = copy
-
-    def finish(item, stage):
-        for offset in range(1, dims[orders[item][stage]]):
-            sent[item, stage, offset].wait_recv()
-
-    kept = []
-    for item in range(count):
-        copy = pltpu.make_async_copy(shards[item], fulls[item].at[tuple(spot)], local_sem.at[item])
-        copy.start()
-        kept.append(copy)
-        start(item, 0)
+            for offset in range(1, dims[order[stage]])
+        ]
+
+    def keep(item):
+        array, low, size, _ = items[item]
+        return pltpu.make_async_copy(shards[array].at[:, pl.ds(low, size)], region(item, ()), local_sem.at[item])
+
+    def begin():
+        for item in range(len(items)):
+            keep(item).start()
+            for copy in copies(item, 0):
+                copy.start()
+
+    def advance(item, stage):
+        for copy in copies(item, stage):
+            copy.wait_recv()
+        if stage == 0:
+            keep(item).wait()
+        if stage + 1 < len(items[item][3]):
+            for copy in copies(item, stage + 1):
+                copy.start()
+
+    def end():
+        for item in range(len(items)):
+            for stage in range(len(items[item][3])):
+                for copy in copies(item, stage):
+                    copy.wait_send()
+
+    return begin, slots(items, advance), end
+
+
+def slots(items, advance):
+    count = len(items)
     pairs = (count + 1) // 2
+    groups = []
     for slot in range(pairs + 3):
+        group = []
         for stage in (3, 2, 1, 0):
             pair = slot - stage
             for item in range(2 * pair, min(2 * pair + 2, count)) if 0 <= pair < pairs else ():
-                finish(item, stage)
-                if stage == 0:
-                    kept[item].wait()
-                if stage < 3:
-                    start(item, stage + 1)
-    for copy in sent.values():
-        copy.wait_send()
-
-
-def scatter_kernel(dims, items, arrays, *refs):
-    count = len(items)
-    grads, square, outs, total_out = refs[:arrays], refs[arrays], refs[arrays + 1 : 2 * arrays + 1], refs[2 * arrays + 1]
-    refs = refs[2 * arrays + 2 :]
-    buffers = [refs[i * 7 : (i + 1) * 7] for i in range(count)]
-    square_sum, square_got, local_sem, send_sem, recv_sem = refs[7 * count :]
-    spot = here(dims)
-    greet(dims, spot)
-    sent = {}
-
-    def send(key, index, source, landing, axis, offset):
-        copy = pltpu.make_async_remote_copy(
-            src_ref=source,
-            dst_ref=landing,
-            send_sem=send_sem.at[index],
-            recv_sem=recv_sem.at[index],
-            device_id=peer(dims, spot, axis, offset)[0],
-            device_id_type=MESH,
+                if stage < len(items[item][3]):
+                    group.append(functools.partial(advance, item, stage))
+        groups.append(group)
+    return groups
+
+
+def scatter_events(dims, spot, items, grads, outs, buffers, local_sem, send_sem, recv_sem):
+    buffers = [buffers[i * 7 : (i + 1) * 7] for i in range(len(items))]
+
+    def load(item):
+        array, low, size, _ = items[item]
+        return pltpu.make_async_copy(
+            grads[array].at[:, :, :, spot[3], :, pl.ds(low, size)], buffers[item][0], local_sem.at[item]
         )
-        copy.start()
-        sent.setdefault(key, []).append(copy)
-
-    def slot_of(item, stage, offset):
-        return item, stage, offset
-
-    def square_start(stage):
-        axis = 3 - stage
-        for offset in range(1, dims[axis]):
-            send(("square", stage), (count, stage, offset), square_sum.at[stage], square_got.at[stage, offset - 1], axis, offset)
-
-    def square_finish(stage):
-        for copy in sent["square", stage]:
-            copy.wait_recv()
-        value = square_sum[stage]
-        for offset in range(1, dims[3 - stage]):
-            value = value + square_got[stage, offset - 1]
-        square_sum[stage + 1] = value
-
-    def start(item, stage):
+
+    def copies(item, stage):
         array, low, size, order = items[item]
         own, first, second, got_core, got_first, got_second, got_last = buffers[item]
         axis = order[stage]
+        made = []
         for offset in range(1, dims[axis]):
-            _, other = peer(dims, spot, axis, offset)
-            index = slot_of(item, stage, offset)
+            target, other = peer(dims, spot, axis, offset)
             if stage == 0:
                 source, landing = grads[array].at[:, :, :, other, :, pl.ds(low, size)], got_core
             elif stage == 1:
@@ -398,18 +384,34 @@
                 source, landing = first.at[:, other], got_second.at[offset - 1]
             else:
                 source, landing = second.at[other], got_last.at[offset - 1]
-            send((item, stage), index, source, landing, axis, offset)
-
-    def finish(item, stage):
+            made.append(
+                pltpu.make_async_remote_copy(
+                    src_ref=source,
+                    dst_ref=landing,
+                    send_sem=send_sem.at[item, stage, offset],
+                    recv_sem=recv_sem.at[item, stage, offset],
+                    device_id=target,
+                    device_id_type=MESH,
+                )
+            )
+        return made
+
+    def begin():
+        for item in range(len(items)):
+            load(item).start()
+            for copy in copies(item, 0):
+                copy.start()
+
+    def advance(item, stage):
         array, low, size, order = items[item]
         own, first, second, got_core, got_first, got_second, got_last = buffers[item]
         axis = order[stage]
         others = range(dims[axis] - 1)
         mine = spot[axis]
-        for copy in sent[item, stage]:
+        for copy in copies(item, stage):
             copy.wait_recv()
         if stage == 0:
-            loads[item].wait()
+            load(item).wait()
 
             @pl.loop(0, dims[0] * dims[1] * dims[2])
             def _(i):
@@ -438,57 +440,61 @@
             for k in others:
                 value += got_last[k].astype(F32)
             outs[array][:, low : low + size] = value
-
-    square_sum[0] = square[...]
-    loads = []
-    for item, (array, low, size, _) in enumerate(items):
-        copy = pltpu.make_async_copy(
-            grads[array].at[:, :, :, spot[3], :, pl.ds(low, size)], buffers[item][0], local_sem.at[item]
-        )
-        copy.start()
-        loads.append(copy)
-        start(item, 0)
-    square_start(0)
-    pairs = (count + 1) // 2
-    for slot in range(pairs + 3):
-        for stage in (3, 2, 1, 0):
-            pair = slot - stage
-            for item in range(2 * pair, min(2 * pair + 2, count)) if 0 <= pair < pairs else ():
-                finish(item, stage)
-                if stage < 3:
-                    start(item, stage + 1)
-        if slot < 4:
-            square_finish(slot)
-            if slot < 3:
-                square_start(slot + 1)
-    total_out[...] = square_sum[4]
-    for group in sent.values():
-        for copy in group:
-            copy.wait_send()
-
-
-def gather_all(dims, shards, orders):
-    anywhere = pl.BlockSpec(memory_space=pl.ANY)
-    most = max(dims)
-    count = len(shards)
-    return pl.pallas_call(
-        functools.partial(gather_kernel, dims, orders),
-        in_specs=[pl.BlockSpec(memory_space=pltpu.VMEM)] * count,
-        out_specs=[anywhere] * count,
-        out_shape=[jax.ShapeDtypeStruct((*dims, *a.shape), a.dtype) for a in shards],
-        scratch_shapes=[
-            pltpu.SemaphoreType.DMA((count,)),
-            pltpu.SemaphoreType.DMA((count, 4, most)),
-            pltpu.SemaphoreType.DMA((count, 4, most)),
-        ],
-        compiler_params=params(collective_id=0, has_side_effects=True),
-        name="gather_weights",
-    )(*shards)
-
-
-def scatter_all(dims, grads, square, items):
-    most = max(dims)
-    count = len(items)
+        if stage < 3:
+            for copy in copies(item, stage + 1):
+                copy.start()
+
+    def end():
+        for item in range(len(items)):
+            for stage in range(4):
+                for copy in copies(item, stage):
+                    copy.wait_send()
+
+    return begin, slots(items, advance), end
+
+
+def square_events(dims, spot, square, total, kept, got, send_sem, recv_sem):
+    def copies(stage):
+        axis = 3 - stage
+        return [
+            pltpu.make_async_remote_copy(
+                src_ref=kept.at[stage],
+                dst_ref=got.at[stage, offset - 1],
+                send_sem=send_sem.at[stage, offset],
+                recv_sem=recv_sem.at[stage, offset],
+                device_id=peer(dims, spot, axis, offset)[0],
+                device_id_type=MESH,
+            )
+            for offset in range(1, dims[axis])
+        ]
+
+    def begin():
+        kept[0] = square[...]
+        for copy in copies(0):
+            copy.start()
+
+    def advance(stage):
+        for copy in copies(stage):
+            copy.wait_recv()
+        value = kept[stage]
+        for offset in range(1, dims[3 - stage]):
+            value = value + got[stage, offset - 1]
+        kept[stage + 1] = value
+        if stage < 3:
+            for copy in copies(stage + 1):
+                copy.start()
+        else:
+            total[...] = value
+
+    def end():
+        for stage in range(4):
+            for copy in copies(stage):
+                copy.wait_send()
+
+    return begin, [[functools.partial(advance, stage)] for stage in range(4)], end
+
+
+def scatter_scratch(dims, grads, items):
     scratch = []
     for array, _, size, order in items:
         tail = (grads[array].shape[4], size)
@@ -503,23 +509,126 @@
             (dims[0] - 1,),
         ):
             scratch.append(pltpu.VMEM((*shape, *tail), BF16))
-    vmem = pl.BlockSpec(memory_space=pltpu.VMEM)
-    scratch += [
-        pltpu.VMEM((5, *square.shape), F32),
-        pltpu.VMEM((4, most - 1, *square.shape), F32),
-        pltpu.SemaphoreType.DMA((count,)),
-        pltpu.SemaphoreType.DMA((count + 1, 4, most)),
-        pltpu.SemaphoreType.DMA((count + 1, 4, most)),
-    ]
+    return scratch
+
+
+def links(count, most):
+    return [pltpu.SemaphoreType.DMA((count, 4, most)), pltpu.SemaphoreType.DMA((count, 4, most))]
+
+
+def moving_call(dims, collective_id, name, kernel, grid, own_in, own_out, gather, scatter, square, pace=1.0):
+    most = max(dims)
+    vmem, anywhere = (lambda a: fixed(a.shape)), (lambda a: pl.BlockSpec(memory_space=pl.ANY))
+    shards, gather_items = gather
+    grads, scatter_items = scatter
+    squares = [] if square is None else [square]
+    in_specs, args = [spec for spec, _ in own_in], [arg for _, arg in own_in]
+    in_specs += [vmem(a) for a in shards] + [anywhere(a) for a in grads] + [vmem(a) for a in squares]
+    args += [*shards, *grads, *squares]
+    out_specs, out_shape = [spec for spec, _ in own_out], [shape for _, shape in own_out]
+    orders = {array: sorted(order) for array, _, _, order in gather_items}
+    for i, a in enumerate(shards):
+        out_specs.append(anywhere(a))
+        out_shape.append(jax.ShapeDtypeStruct((*(dims[axis] for axis in orders[i]), *a.shape), a.dtype))
+    for g in grads:
+        out_shape.append(jax.ShapeDtypeStruct(g.shape[4:], F32))
+        out_specs.append(vmem(out_shape[-1]))
+    for q in squares:
+        out_shape.append(jax.ShapeDtypeStruct(q.shape, F32))
+        out_specs.append(vmem(q))
+    groups = []
+    if shards:
+        groups.append([pltpu.SemaphoreType.DMA((len(gather_items),)), *links(len(gather_items), most)])
+    if grads:
+        buffers = scatter_scratch(dims, grads, scatter_items)
+        groups.append([*buffers, pltpu.SemaphoreType.DMA((len(scatter_items),)), *links(len(scatter_items), most)])
+    if squares:
+        groups.append(
+            [
+                pltpu.VMEM((5, *square.shape), F32),
+                pltpu.VMEM((4, most - 1, *square.shape), F32),
+                pltpu.SemaphoreType.DMA((4, most)),
+                pltpu.SemaphoreType.DMA((4, most)),
+            ]
+        )
+    steps = 1
+    for size in grid:
+        steps *= size
+
+    def fused(*refs):
+        refs = list(refs)
+
+        def take(n):
+            taken = refs[:n]
+            del refs[:n]
+            return taken
+
+        ins, shard_refs, grad_refs, square_refs = take(len(own_in)), take(len(shards)), take(len(grads)), take(len(squares))
+        outs, full_refs, sum_refs, total_refs = take(len(own_out)), take(len(shards)), take(len(grads)), take(len(squares))
+        step = 0
+        for axis, size in enumerate(grid):
+            step = step * size + pl.program_id(axis)
+        spot = here(dims)
+        plans = []
+        scratch = iter(groups)
+        if shards:
+            plans.append(gather_events(dims, spot, gather_items, shard_refs, full_refs, *take(len(next(scratch)))))
+        if grads:
+            held = take(len(next(scratch)))
+            plans.append(scatter_events(dims, spot, scatter_items, grad_refs, sum_refs, held[:-3], *held[-3:]))
+        if squares:
+            plans.append(square_events(dims, spot, *square_refs, *total_refs, *take(len(next(scratch)))))
+
+        def open_all():
+            greet(dims, spot)
+            for begin, _, _ in plans:
+                begin()
+
+        depth = max(len(groups_of) for _, groups_of, _ in plans)
+        merged = [[e for _, groups_of, _ in plans if i < len(groups_of) for e in groups_of[i]] for i in range(depth)]
+
+        def close_all():
+            for _, _, end in plans:
+                end()
+
+        if steps == 1:
+            open_all()
+            for group in merged:
+                for event in group:
+                    event()
+            close_all()
+            return
+        late = []
+        pl.when(step == 0)(open_all)
+        for i, group in enumerate(merged):
+            at = int((i + 1) * pace)
+
+            def run(group=group):
+                for event in group:
+                    event()
+
+            if at < steps:
+                pl.when(step == at)(run)
+            else:
+                late.append(run)
+        kernel(*ins, *outs)
+
+        @pl.when(step == steps - 1)
+        def _():
+            for run in late:
+                run()
+            close_all()
+
     return pl.pallas_call(
-        functools.partial(scatter_kernel, dims, items, len(grads)),
-        in_specs=[pl.BlockSpec(memory_space=pl.ANY)] * len(grads) + [vmem],
-        out_specs=[vmem] * (len(grads) + 1),
-        out_shape=[jax.ShapeDtypeStruct(g.shape[4:], F32) for g in grads] + [jax.ShapeDtypeStruct(square.shape, F32)],
-        scratch_shapes=scratch,
-        compiler_params=params(collective_id=1, has_side_effects=True),
-        name="scatter_grads",
-    )(*grads, square)
+        fused,
+        grid=grid,
+        in_specs=in_specs,
+        out_specs=out_specs,
+        out_shape=out_shape,
+        scratch_shapes=[piece for group in groups for piece in group],
+        compiler_params=params(collective_id=collective_id, has_side_effects=True),
+        name=name,
+    )(*args)
 
 
 def body(
@@ -567,18 +676,33 @@
     used = vec_row.shape[0]
     vec_row = jnp.pad(vec_row, (0, 8 * width - used)).reshape(8, width)
     base = (5 + wide_ff) * share
+    down_out, up_out = (0, 1, 2, 3), (0, 2, 1, 3)
+    down_in, up_in = (3, 1, 2, 0), (3, 2, 1, 0)
+    none = ((), ())
     if direct:
-        y_first, x_first = (0, 1, 2, 3), (0, 2, 1, 3)
-        qkv_full, down_full, merge_full, up_full, out_full, vec_full = gather_all(
+        qkv_full, merge_full, vec_full = moving_call(
             dims,
-            (qkv_w, down_w, merge_w, up_w, out_w, vec_row),
-            (y_first, x_first, y_first, y_first, x_first, x_first),
+            0,
+            "gather_first",
+            None,
+            (1,),
+            [],
+            [],
+            (
+                (qkv_w, merge_w, vec_row),
+                (
+                    (1, 0, width, down_out),
+                    (0, 0, width, up_out),
+                    (0, width, width, down_out),
+                    (0, 2 * width, width, up_out),
+                    (2, 0, width, down_out),
+                ),
+            ),
+            none,
+            None,
         )
         qkv_full = qkv_full.reshape(width, 3 * width)
-        down_full = down_full.reshape(ff, width)
         merge_full = merge_full.reshape(width, width)
-        up_full = up_full.reshape(width, ff)
-        out_full = out_full.reshape(width, width)
         vec_rows = vec_full.reshape(devices, 8, width)[:, 0].astype(F32)
     else:
         mine = jnp.concatenate([merge_w, out_w, *cut(qkv_w, 3), *cut(up_w, wide_ff), down_w, vec_row], axis=0)
@@ -613,22 +737,7 @@
     key_bias = jnp.where(live, 0.0, MASKED).astype(F32).reshape(rows, seq, 1)
 
     batch = lax.axis_size("batch")
-    group_rows = rows * batch
-    heads = lax.all_gather(head_w[0], "batch", axis=0)
-    counts = lax.all_gather(class_count, "batch", axis=0, tiled=True)
-    group_dlog_raw = lax.all_gather(logit_cotangent, "batch", axis=0, tiled=True)
     classes = head_w.shape[2]
-    own = lax.axis_index("batch")
-    my_table = lax.dynamic_slice(row_table, (own * rows,), (rows,))
-    class_ids = jnp.arange(classes, dtype=jnp.int32)
-    my_select = (my_table[:, None] == jnp.arange(batch, dtype=jnp.int32)[None, :]).astype(F32)
-    my_class = (class_ids[None, :] < (my_select * counts[None, :].astype(F32)).sum(1, keepdims=True)).astype(F32)
-    my_dlog = logit_cotangent * my_class
-    picked = (my_select[:, :, None] * my_dlog[:, None, :]).transpose(1, 0, 2)
-    cls_grad = jnp.sum(
-        lax.dot_general(picked, heads.astype(F32), (((2,), (2,)), ((0,), (0,))), precision=PRECISE), axis=0
-    )
-
     tok_flat = tokens.reshape(count, width)
     cot_flat = cotangent.reshape(count, width)
     merge_query, hidden, attn_in, packed, squares = pl.pallas_call(
@@ -669,18 +778,69 @@
 
     bias_block = pl.BlockSpec((1, seq, 1), lambda r, p: (r, 0, 0))
     lse_block = pl.BlockSpec((1, 1, 2, seq), lambda r, p: (r, p, 0, 0))
-    context, lse = pl.pallas_call(
-        functools.partial(attn_kernel, head**-0.5),
-        grid=(rows, pairs),
-        in_specs=[head_block(0), head_block(pairs), head_block(2 * pairs), bias_block],
-        out_specs=[head_block(0), lse_block],
-        out_shape=[
-            jax.ShapeDtypeStruct((rows, seq, width), BF16),
-            jax.ShapeDtypeStruct((rows, pairs, 2, seq), F32),
-        ],
-        compiler_params=params(),
-        name="attention",
-    )(packed_rows, packed_rows, packed_rows, key_bias)
+    attn_in_refs = [
+        (head_block(0), packed_rows),
+        (head_block(pairs), packed_rows),
+        (head_block(2 * pairs), packed_rows),
+        (bias_block, key_bias),
+    ]
+    attn_outs = [
+        (head_block(0), jax.ShapeDtypeStruct((rows, seq, width), BF16)),
+        (lse_block, jax.ShapeDtypeStruct((rows, pairs, 2, seq), F32)),
+    ]
+    attend = functools.partial(attn_kernel, head**-0.5)
+    if direct:
+        limit = jnp.broadcast_to(class_count.astype(F32)[:, None], (1, classes))
+        spare = -(rows + 1) % 8
+        small = jnp.concatenate([logit_cotangent, limit, jnp.zeros((spare, classes), F32)], axis=0)
+        third, narrow = ff // 3, width // 3
+        gather_items = [(3, 0, classes, (2, 3)), (4, 0, classes, (2, 3))]
+        for i in range(3):
+            gather_items += [(0, i * third, third, up_out), (1, i * narrow, narrow, down_out)]
+        gather_items.append((2, 0, width, down_out))
+        context, lse, up_full, down_full, out_full, heads, small = moving_call(
+            dims,
+            2,
+            "attention_gather",
+            attend,
+            (rows, pairs),
+            attn_in_refs,
+            attn_outs,
+            ((up_w, down_w, out_w, head_w[0], small), gather_items),
+            none,
+            None,
+            pace=2.2,
+        )
+        up_full = up_full.reshape(width, ff)
+        down_full = down_full.reshape(ff, width)
+        out_full = out_full.reshape(width, width)
+        heads = heads.reshape(batch, width, classes)
+        small = small.reshape(batch, -1, classes)
+        group_dlog_raw = small[:, :rows].reshape(batch * rows, classes)
+        counts = small[:, rows, 0]
+    else:
+        context, lse = pl.pallas_call(
+            attend,
+            grid=(rows, pairs),
+            in_specs=[spec for spec, _ in attn_in_refs],
+            out_specs=[spec for spec, _ in attn_outs],
+            out_shape=[shape for _, shape in attn_outs],
+            compiler_params=params(),
+            name="attention",
+        )(*(arg for _, arg in attn_in_refs))
+        heads = lax.all_gather(head_w[0], "batch", axis=0)
+        counts = lax.all_gather(class_count, "batch", axis=0, tiled=True)
+        group_dlog_raw = lax.all_gather(logit_cotangent, "batch", axis=0, tiled=True)
+    own = lax.axis_index("batch")
+    my_table = lax.dynamic_slice(row_table, (own * rows,), (rows,))
+    class_ids = jnp.arange(classes, dtype=jnp.int32)
+    my_select = (my_table[:, None] == jnp.arange(batch, dtype=jnp.int32)[None, :]).astype(F32)
+    my_class = (class_ids[None, :] < (my_select * counts[None, :].astype(F32)).sum(1, keepdims=True)).astype(F32)
+    my_dlog = logit_cotangent * my_class
+    picked = (my_select[:, :, None] * my_dlog[:, None, :]).transpose(1, 0, 2)
+    cls_grad = jnp.sum(
+        lax.dot_general(picked, heads.astype(F32), (((2,), (2,)), ((0,), (0,))), precision=PRECISE), axis=0
+    )
 
     context = context.reshape(count, width)
     (layer_out, activated, grad_up, ffn_in, grad_down, grad_attn, grad_two, grad_ctx, sums, up_sums) = pl.pallas_call(
@@ -727,15 +887,44 @@
     )(context, hidden, cot_flat, cls_grad.reshape(rows, 1, width), live_col, out_full, up_full, down_full, vecs)
 
     grad_rows = grad_ctx.reshape(rows, seq, width)
-    grad_q, grad_k, grad_v = pl.pallas_call(
-        functools.partial(attn_back_kernel, head**-0.5),
-        grid=(rows, pairs),
-        in_specs=[head_block(0), head_block(pairs), head_block(2 * pairs), bias_block, lse_block, head_block(0)],
-        out_specs=[head_block(0)] * 3,
-        out_shape=[jax.ShapeDtypeStruct((rows, seq, width), BF16)] * 3,
-        compiler_params=params(),
-        name="attention_back",
-    )(packed_rows, packed_rows, packed_rows, key_bias, lse, grad_rows)
+    cls_rows = layer_out.reshape(rows, seq, width)[:, 0, :]
+    back_refs = [*attn_in_refs, (lse_block, lse), (head_block(0), grad_rows)]
+    back_outs = [(head_block(0), jax.ShapeDtypeStruct((rows, seq, width), BF16))] * 3
+    attend_back = functools.partial(attn_back_kernel, head**-0.5)
+    grad_out_w = t_mm(context, grad_attn).astype(BF16)
+    grad_up_w = t_mm(ffn_in, grad_up).astype(BF16)
+    grad_down_w = t_mm(activated, grad_down).astype(BF16)
+    if direct:
+        ffn_items = []
+        for i in range(3):
+            ffn_items += [(0, i * third, third, up_in), (1, i * narrow, narrow, down_in)]
+        ffn_items.append((2, 0, width, down_in))
+        first_rows = jnp.pad(cls_rows, ((0, -rows % 8), (0, 0)))
+        grad_q, grad_k, grad_v, group_cls, own_up, own_down, own_out = moving_call(
+            dims,
+            3,
+            "attention_back_scatter",
+            attend_back,
+            (rows, pairs),
+            back_refs,
+            back_outs,
+            ((first_rows,), ((0, 0, width, (2, 3)),)),
+            ([g.reshape(*dims, -1, g.shape[-1]) for g in (grad_up_w, grad_down_w, grad_out_w)], ffn_items),
+            None,
+            pace=2.4,
+        )
+        group_cls = group_cls.reshape(batch, -1, width)[:, :rows].reshape(batch * rows, width)
+    else:
+        grad_q, grad_k, grad_v = pl.pallas_call(
+            attend_back,
+            grid=(rows, pairs),
+            in_specs=[spec for spec, _ in back_refs],
+            out_specs=[spec for spec, _ in back_outs],
+            out_shape=[shape for _, shape in back_outs],
+            compiler_params=params(),
+            name="attention_back",
+        )(*(arg for _, arg in back_refs))
+        group_cls = lax.all_gather(cls_rows, "batch", axis=0, tiled=True)
 
     grad_input, grad_query, grad_packed, bias_sums = pl.pallas_call(
         input_kernel,
@@ -776,9 +965,6 @@
 
     grad_merge_w = t_mm(tok_flat, grad_query).astype(BF16)
     grad_qkv_w = t_mm(attn_in, grad_packed).astype(BF16)
-    grad_out_w = t_mm(context, grad_attn).astype(BF16)
-    grad_up_w = t_mm(ffn_in, grad_up).astype(BF16)
-    grad_down_w = t_mm(activated, grad_down).astype(BF16)
 
     vec_grads = (sums[8], sums[3], sums[4], sums[2], sums[0], sums[1], bias_sums[0], bias_sums[1])
     vec_block = jnp.concatenate(
@@ -796,28 +982,27 @@
         ]
     )
     if direct:
-        y_first, x_first = (3, 1, 2, 0), (3, 2, 1, 0)
-        half_ff, half_qkv, half = ff // 2, 3 * width // 2, width // 2
-        items = (
-            (0, 0, half_ff, x_first),
-            (1, 0, half, y_first),
-            (0, half_ff, half_ff, x_first),
-            (1, half, half, y_first),
-            (2, 0, half_qkv, x_first),
-            (2, half_qkv, half_qkv, y_first),
-            (3, 0, width, x_first),
-            (4, 0, width, y_first),
-            (5, 0, width, x_first),
-        )
         square = jnp.broadcast_to(jnp.pad(partial, (0, 2))[:, None], (8, 128))
-        own_up, own_down, own_qkv, own_merge, own_out, own_vec, square = scatter_all(
+        own_qkv, own_merge, own_vec, square = moving_call(
             dims,
-            [
-                g.reshape(*dims, -1, g.shape[-1])
-                for g in (grad_up_w, grad_down_w, grad_qkv_w, grad_merge_w, grad_out_w, vec_block)
-            ],
+            1,
+            "scatter_last",
+            None,
+            (1,),
+            [],
+            [],
+            none,
+            (
+                [g.reshape(*dims, -1, g.shape[-1]) for g in (grad_qkv_w, grad_merge_w, vec_block)],
+                (
+                    (0, 0, width, up_in),
+                    (0, width, width, down_in),
+                    (0, 2 * width, width, up_in),
+                    (1, 0, width, down_in),
+                    (2, 0, width, up_in),
+                ),
+            ),
             square,
-            items,
         )
         own_vec = own_vec[0]
         totals = square[:6, 0]
@@ -850,12 +1035,10 @@
     own_up_bias = own_vec[8 * share : 8 * share + wide_ff * share]
 
     layer_rows = layer_out.reshape(rows, seq, width)
-    cls_rows = layer_rows[:, 0, :]
     my_logits = jnp.sum(
         my_select[:, :, None] * jnp.einsum("rd,kdc->rkc", cls_rows, heads, preferred_element_type=F32), axis=1
     )
     logits = my_logits * my_class
-    group_cls = lax.all_gather(cls_rows, "batch", axis=0, tiled=True)
     owner_mask = (row_table == own).astype(F32)[:, None]
     class_live = (class_ids < class_count[0]).astype(F32)[None, :]
     group_dlog = group_dlog_raw * (owner_mask * class_live)

time: 514 us -> 435 us (0.85); the launches traced: 512 us -> 427 us
  Pallas kernels: 396 us -> 334 us
  blocking collectives: 25.6 us -> 0 us
    pallas_call x4, Pallas kernels: 302 us -> 241 us  [moving_call(): pl.pallas_call(fused, grid=grid, in_specs=in_specs, out_specs=out_specs,...]
    all_gather x3 -> x0, blocking collectives: 19.2 us -> none  [the longest x1 8.69 us: body(): heads = lax.all_gather(head_w[0], 'batch', axis=0)]
    unnamed x1 -> x0, blocking collectives: 6.38 us -> none
    unnamed x40 -> x42, local copies, waits for them, and re-layouts: 11.3 us -> 6.64 us
where the time goes in v3:
time: 435 us; the launch traced here: 427 us
  Pallas kernels  334 us (77%)
  matrix products  43.9 us (10%)
  local copies, waits for them, and re-layouts  33.1 us (8%)
  other arithmetic  13.2 us (3%)
    pallas_call x4, Pallas kernels, moving_call(): pl.pallas_call(fused, grid=grid, in_specs=in_specs, out_specs=out_specs,...  241 us
    pallas_call x1, Pallas kernels, body(): pl.pallas_call(functools.partial(ffn_kernel, per_row), grid=(tiles,), in_...  54 us
    dot_general x5, matrix products, t_mm(): lax.dot_general(left, right, (((0,), (0,)), ((), ())), preferred_element_...  40.7 us
    pallas_call x1, Pallas kernels, body(): pl.pallas_call(input_kernel, grid=(tiles,), in_specs=[tiled(TILE, width),...  20.7 us
    pallas_call x1, Pallas kernels, body(): pl.pallas_call(merge_kernel, grid=(tiles,), in_specs=[tiled(TILE, width),...  18.9 us

profile of v3, /device:TPU:0, one launch (start us, length us, event | category | flops | bytes accessed | tf_op | source)
XLA Modules:
  0.0 427.5 jit_solution(10077119439909598239)
XLA Ops:
  1.3 0.7 dynamic_slice.3
  2.1 0.7 compare_convert_fusion.1
  3.0 6.1 %concatenate.19 = bf16[288]{0:T(512)(128)(2,1)S(1)} concatenate(bf16[24]{0:T(256)(128)(2,1)} %param.32, bf16[24]{0:T(256)(128)(2,1)} %param.33, bf16[24]{0:T(256)(128)(2,1)} %param.34, bf16[24]{0:T(256)(128)(2,1)} %param.38, bf16[24]{0:T(256)(128)(2,1)} %param.39, bf16[24]{0:T(256)(128)(2,1)} %param.40, bf16[24]{0:T(256)(128)(2,1)} %param.29, bf16[24]{0:T(256)(128)(2,1)} %param.30, ...), dimensions={0} | concatenate | bytes 1152 | tf_op jit(solution)/shard_map/concatenate | solution.py:675
  9.2 0.7 lt.148
  10.1 1.3 maximum_maximum_fusion.refs_8_
  11.5 0.7 compare_bitcast_fusion
  12.3 0.6 reshape.468.refs_2_
  13.0 1.4 convert_reduce_fusion
  14.4 0.8 broadcast_in_dim.24
  15.4 0.7 and_convert_fusion.live_row
  16.8 1.0 fusion.1.live_col
  18.1 1.1 and_select_fusion.refs_3_
  19.2 45.9 %gather_first.1 = (bf16[4,2,2,2,24,2304]{5,4,3,2,1,0:T(8,128)(2,1)}, bf16[4,2,2,2,24,768]{5,4,3,2,1,0:T(8,128)(2,1)}, bf16[4,2,2,2,8,768]{5,4,3,2,1,0:T(8,128)(2,1)}) custom-call(bf16[24,2304]{1,0:T(8,128)(2,1)} %refs_0_.1, bf16[24,768]{1,0:T(8,128)(2,1)} %refs_1_.1, bf16[8,768]{1,0:T(8,128)(2,1)} %reshape.468.refs_2_), custom_call_target="tpu_custom_call" | custom-call | tf_op jit(solution)/shard_map/gather_first/pallas_call | solution.py:622
  65.1 1.1 slice.216
  67.9 0.7 fusion.2.vecs
  68.6 18.9 %merge_qkv.1 = (bf16[1536,768]{1,0:T(8,128)(2,1)}, f32[1536,768]{1,0:T(8,128)}, bf16[1536,768]{1,0:T(8,128)(2,1)}, bf16[1536,2304]{1,0:T(8,128)(2,1)}, f32[8,768]{1,0:T(8,128)}) custom-call(bf16[1536,768]{1,0:T(8,128)(2,1)} %bitcast.109, f32[6,1,256]{2,1,0:T(1,128)} %and_convert_fusion.live_row, f32[1536,1]{1,0:T(8,128)} %fusion.1.live_col, ...), custom_call_target="tpu_custom_call" | custom-call | tf_op jit(solution)/shard_map/merge_qkv/pallas_call | solution.py:743
  87.5 1.4 slice_reduce_fusion.11
  88.9 76.5 %attention_gather.1 = (bf16[3,512,768]{2,1,0:T(8,128)(2,1)}, f32[3,6,2,512]{3,2,1,0:T(2,128)}, bf16[4,2,2,2,24,3072]{5,4,3,2,1,0:T(8,128)(2,1)}, bf16[4,2,2,2,96...) custom-call(bf16[3,512,2304]{2,1,0:T(8,128)(2,1)} %bitcast.101, ...), custom_call_target="tpu_custom_call" | custom-call | tf_op jit(solution)/shard_map/attention_gather/pallas_call | solution.py:622
  165.4 0.7 slice.219
  166.2 0.7 slice.238
  167.1 1.9 convolution_bitcast_fusion.1
  169.0 0.6 reshape.480.cls_grad
  169.6 54.0 %ffn.1 = (bf16[1536,768]{1,0:T(8,128)(2,1)}, bf16[1536,3072]{1,0:T(8,128)(2,1)}, bf16[1536,3072]{1,0:T(8,128)(2,1)}, bf16[1536,768]{1,0:T(8,128)(2,1)}, bf16[153...) custom-call(bf16[1536,768]{1,0:T(8,128)(2,1)} %bitcast.123, ...), custom_call_target="tpu_custom_call" | custom-call | tf_op jit(solution)/shard_map/ffn/pallas_call | solution.py:846
  223.6 4.8 %convolution_convert_fusion.4 = bf16[768,768]{1,0:T(8,128)(2,1)} fusion(bf16[1536,768]{1,0:T(8,128)(2,1)S(1)} %bitcast.124, bf16[1536,768]{1,0:T(8,128)(2,1)} %get-tuple-element.77), kind=kOutput, calls=%fused_computation.4 | convolution fusion | flops 1812529152 | bytes 5898240 | tf_op jit(solution)/shard_map/dot_general | solution.py:32
  229.1 4.0 stack.27
  233.1 0.7 broadcast_in_dim.57.refs_3_
  233.8 0.9 fusion.10
  235.4 0.8 slice.227
  236.4 0.7 compare_select_fusion
  237.6 12.6 %convolution_convert_fusion.2 = bf16[768,3072]{1,0:T(8,128)(2,1)} fusion(bf16[1536,768]{1,0:T(8,128)(2,1)} %get-tuple-element.73, bf16[1536,3072]{1,0:T(8,128)(2,1)} %get-tuple-element.74), kind=kOutput, calls=%fused_computation.2 | convolution fusion | flops 7250116608 | bytes 16515072 | tf_op jit(solution)/shard_map/dot_general | solution.py:32
  250.3 9.5 %convolution_convert_fusion = bf16[3072,768]{1,0:T(8,128)(2,1)} fusion(bf16[1536,3072]{1,0:T(8,128)(2,1)S(1)} %bitcast.145, bf16[1536,768]{1,0:T(8,128)(2,1)S(1)} %copy-done.10), kind=kOutput, calls=%fused_computation | convolution fusion | flops 7250116608 | bytes 16515072 | tf_op jit(solution)/shard_map/dot_general | solution.py:32
  259.8 73.4 %attention_back_scatter.1 = (bf16[3,512,768]{2,1,0:T(8,128)(2,1)}, bf16[3,512,768]{2,1,0:T(8,128)(2,1)}, bf16[3,512,768]{2,1,0:T(8,128)(2,1)}, bf16[2,2,8,768]{3...) custom-call(bf16[3,512,2304]{2,1,0:T(8,128)(2,1)} %bitcast.104, ...), custom_call_target="tpu_custom_call" | custom-call | tf_op jit(solution)/shard_map/attention_back_scatter/pallas_call | solution.py:622
  333.3 20.7 %merge_back.1 = (bf16[1536,768]{1,0:T(8,128)(2,1)}, bf16[1536,768]{1,0:T(8,128)(2,1)}, bf16[1536,2304]{1,0:T(8,128)(2,1)}, f32[8,768]{1,0:T(8,128)}) custom-call(bf16[1536,768]{1,0:T(8,128)(2,1)} %bitcast.125, bf16[1536,768]{1,0:T(8,128)(2,1)} %bitcast.126, bf16[1536,768]{1,0:T(8,128)(2,1)} %bitcast.127, f32[1536,768]{1,0:T(8,128)} %get-tuple-element.81.grad_two, ...), custom_call_target="tpu_custom_call" | custom-call | tf_op jit(solution)/shard_map/merge_back/pallas_call | solution.py:929
  354.0 0.7 convert.38
  355.1 1.1 convolution_bitcast_fusion
  356.3 0.8 copy.76
  357.1 10.7 %convolution_convert_fusion.1 = bf16[768,2304]{1,0:T(8,128)(2,1)} fusion(bf16[1536,768]{1,0:T(8,128)(2,1)} %get-tuple-element.84, bf16[1536,2304]{1,0:T(8,128)(2,1)} %get-tuple-element.85), kind=kOutput, calls=%fused_computation.1 | convolution fusion | flops 5437587456 | bytes 12976128 | tf_op jit(solution)/shard_map/dot_general | solution.py:32
  367.8 3.1 convolution_convert_fusion.3
  370.8 45.0 %scatter_last.1 = (f32[24,2304]{1,0:T(8,128)}, f32[24,768]{1,0:T(8,128)}, f32[8,768]{1,0:T(8,128)}, f32[8,128]{1,0:T(8,128)}) custom-call(bf16[4,2,2,2,24,2304]{5,4,3,2,1,0:T(8,128)(2,1)} %bitcast.118, bf16[4,2,2,2,24,768]{5,4,3,2,1,0:T(8,128)(2,1)} %bitcast.132, bf16[4,2,2,2,8,768]{5,4,3,2,1,0:T(8,128)(2,1)} %bitcast.128, f32[8,128]{1,0:T(8,128)} %broadcast_in_dim.57.refs_3_), custom_call_target="tpu_custom_call" | custom-call | tf_op jit(solution)/shard_map/scatter_last/pallas_call | solution.py:622
  415.9 1.2 slice.215
  417.7 1.3 sqrt_reduce_fusion
  419.0 1.3 slice_bitcast_fusion.3
  420.3 1.5 slice_bitcast_fusion
  421.8 1.5 copy.96
  423.3 1.6 copy.97
  425.0 0.6 copy.98
  425.6 0.7 copy.99
  426.3 0.7 copy.100
  (99 shorter events, 6.3 us)
Async XLA Ops:
  0.7 17.4 %copy-start.8 = (s32[3]{0:T(128)S(1)}, s32[3]{0:T(128)}, u32[]{:S(2)}) copy-start(s32[3]{0:T(128)} %param.23) | copy-start | bytes 40
  88.9 78.1 %copy-start.9 = (f32[3,128]{1,0:T(4,128)S(1)}, f32[3,128]{1,0:T(4,128)}, u32[]{:S(2)}) copy-start(f32[3,128]{1,0:T(4,128)} %param.43) | copy-start | bytes 4612
  169.6 54.0 %copy-start.2 = (bf16[3,512,768]{2,1,0:T(8,128)(2,1)S(1)}, bf16[3,512,768]{2,1,0:T(8,128)(2,1)}, u32[]{:S(2)}) copy-start(bf16[3,512,768]{2,1,0:T(8,128)(2,1)} %get-tuple-element.63) | copy-start | bytes 7077892
  223.6 4.8 %copy-start.6 = (f32[16,768]{1,0:T(8,128)S(1)}, f32[16,768]{1,0:T(8,128)}, u32[]{:S(2)}) copy-start(f32[16,768]{1,0:T(8,128)} %get-tuple-element.87) | copy-start | bytes 147460
  223.6 12.5 %copy-start.1 = (bf16[2,2,768,128]{3,2,1,0:T(8,128)(2,1)S(1)}, bf16[2,2,768,128]{3,2,1,0:T(8,128)(2,1)}, u32[]{:S(2)}) copy-start(bf16[2,2,768,128]{3,2,1,0:T(8,128)(2,1)} %get-tuple-element.66) | copy-start | bytes 2359300
  236.1 14.1 %slice-start = ((s8[9437184]{0:T(1024)(128)(4,1)}), s8[4194304]{0:T(1024)(128)(4,1)S(1)}, s32[]{:S(2)}) async-start(s8[9437184]{0:T(1024)(128)(4,1)} %bitcast.144), calls=%async_computation | async-start | bytes 8388608
  237.6 12.6 %slice-start.1 = ((s8[9437184]{0:T(1024)(128)(4,1)}), s8[4194304]{0:T(1024)(128)(4,1)S(1)}, s32[]{:S(2)}) async-start(s8[9437184]{0:T(1024)(128)(4,1)} %bitcast.144), calls=%async_computation.1 | async-start | bytes 8388608
  237.6 12.6 %slice-start.2 = ((s8[9437184]{0:T(1024)(128)(4,1)}), s8[1048576]{0:T(1024)(128)(4,1)S(1)}, s32[]{:S(2)}) async-start(s8[9437184]{0:T(1024)(128)(4,1)} %bitcast.144), calls=%async_computation.2 | async-start | bytes 2097152
  237.6 12.6 %copy-start.10 = (bf16[1536,768]{1,0:T(8,128)(2,1)S(1)}, bf16[1536,768]{1,0:T(8,128)(2,1)}, u32[]{:S(2)}) copy-start(bf16[1536,768]{1,0:T(8,128)(2,1)} %get-tuple-element.76) | copy-start | bytes 7077892
  333.3 21.8 %copy-start.7 = (bf16[2,2,8,768]{3,2,1,0:T(8,128)(2,1)S(1)}, bf16[2,2,8,768]{3,2,1,0:T(8,128)(2,1)}, u32[]{:S(2)}) copy-start(bf16[2,2,8,768]{3,2,1,0:T(8,128)(2,1)} %get-tuple-element.97) | copy-start | bytes 147460
  357.1 10.7 %copy-start = (bf16[3,512,768]{2,1,0:T(8,128)(2,1)S(1)}, bf16[3,512,768]{2,1,0:T(8,128)(2,1)}, u32[]{:S(2)}) copy-start(bf16[3,512,768]{2,1,0:T(8,128)(2,1)} %param.22) | copy-start | bytes 7077892
  357.1 10.7 %copy-start.11 = (bf16[1536,768]{1,0:T(8,128)(2,1)S(1)}, bf16[1536,768]{1,0:T(8,128)(2,1)}, u32[]{:S(2)}) copy-start(bf16[1536,768]{1,0:T(8,128)(2,1)} %get-tuple-element.86) | copy-start | bytes 7077892
  370.8 54.1 %copy-start.5 = (f32[24,768]{1,0:T(8,128)S(1)}, f32[24,768]{1,0:T(8,128)}, u32[]{:S(2)}) copy-start(f32[24,768]{1,0:T(8,128)} %get-tuple-element.177) | copy-start | bytes 221188
  370.8 54.8 %copy-start.4 = (f32[24,3072]{1,0:T(8,128)S(1)}, f32[24,3072]{1,0:T(8,128)}, u32[]{:S(2)}) copy-start(f32[24,3072]{1,0:T(8,128)} %get-tuple-element.181) | copy-start | bytes 884740
  370.8 55.5 %copy-start.3 = (f32[96,768]{1,0:T(8,128)S(1)}, f32[96,768]{1,0:T(8,128)}, u32[]{:S(2)}) copy-start(f32[96,768]{1,0:T(8,128)} %get-tuple-element.183) | copy-start | bytes 884740

commit v4 on v3

--- a/solution.py
+++ b/solution.py
@@ -114,7 +114,7 @@
         ctx_ref[0, rows, :] = jnp.concatenate(parts, axis=0).T.astype(BF16)
 
 
-def attn_back_kernel(scale, q_ref, k_ref, v_ref, bias_ref, lse_ref, grad_ref, dq_ref, dk_ref, dv_ref):
+def attn_back_kernel(scale, q_ref, k_ref, v_ref, bias_ref, lse_ref, grad_ref, out_ref):
     seq, lanes = q_ref.shape[1:]
     head = lanes // 2
     q = q_ref[0] * jnp.asarray(scale, BF16)
@@ -137,9 +137,48 @@
             grad_s = (probs * (grad_p - jnp.sum(probs * grad_p, axis=0, keepdims=True))).astype(BF16)
             grad_k += mm(grad_s, q_part)
             parts.append(mm(k_t[h * head : (h + 1) * head], grad_s))
-        dq_ref[0, rows, :] = (jnp.concatenate(parts, axis=0).T * scale).astype(BF16)
-    dk_ref[0] = grad_k.astype(BF16)
-    dv_ref[0] = grad_v.astype(BF16)
+        out_ref[0, 0, rows, :] = (jnp.concatenate(parts, axis=0).T * scale).astype(BF16)
+    out_ref[1, 0] = grad_k.astype(BF16)
+    out_ref[2, 0] = grad_v.astype(BF16)
+
+
+def share_out(low, cols, value):
+    rows = low.shape[4]
+    spots = [(a, b, c, d) for a in range(low.shape[0]) for b in range(low.shape[1]) for c in range(low.shape[2]) for d in range(low.shape[3])]
+    for i, spot in enumerate(spots):
+        low[(*spot, slice(None), cols)] = value[i * rows : (i + 1) * rows].astype(BF16)
+
+
+def attn_back_weights_kernel(
+    scale, pairs, cuts, q, k, v, bias, lse, grad, ffn_in, grad_up, ctx, grad_attn, out_ref, low_up, low_out, turned
+):
+    step = pl.program_id(0) * pairs + pl.program_id(1)
+    part = grad_up.shape[1]
+
+    @pl.when(step == 0)
+    def _():
+        turned[...] = ffn_in[...].T
+
+    @pl.when(step < cuts)
+    def _():
+        cols = pl.ds(pl.multiple_of(step * part, part), part)
+        share_out(low_up, cols, mm(turned[...], grad_up[...]))
+
+    @pl.when(step == cuts)
+    def _():
+        share_out(low_out, slice(None), mm(ctx[...].T, grad_attn[...]))
+
+    attn_back_kernel(scale, q, k, v, bias, lse, grad, out_ref)
+
+
+def qkv_grad_kernel(attn_in, grad, weight_grad, sums, turned):
+    @pl.when(pl.program_id(0) == 0)
+    def _():
+        turned[...] = attn_in[...].T
+
+    piece = grad[0]
+    weight_grad[...] = mm(turned[...], piece).astype(BF16)
+    sums[...] = jnp.broadcast_to(rowsum(piece.astype(F32)), sums.shape)
 
 
 def ffn_kernel(
@@ -223,7 +262,7 @@
 
 
 def input_kernel(
-    dq, dk, dv, grad_two, tok, query, live_row, live_col, merge_w, qkv_w, grad_input, grad_query_out, packed_out, sums
+    grad_qkv, grad_two, tok, query, live_row, live_col, merge_w, qkv_w, grad_input, merge_grad
 ):
     step = pl.program_id(0)
     width = tok.shape[1]
@@ -231,17 +270,13 @@
 
     @pl.when(step == 0)
     def _():
-        sums[...] = jnp.zeros_like(sums)
+        merge_grad[...] = jnp.zeros_like(merge_grad)
 
     x = tok[...]
-    grad_q, grad_v = dq[...], dv[...]
     grad_one = grad_two[...]
-    for i, piece in enumerate((grad_q, dk[...], grad_v)):
+    for i in range(3):
         cols = slice(i * width, (i + 1) * width)
-        packed_out[:, cols] = piece
-        grad_one += mm_t(piece, qkv_w[:, cols])
-    sums[0:1, :] += rowsum(grad_q.astype(F32))
-    sums[1:2, :] += rowsum(grad_v.astype(F32))
+        grad_one += mm_t(grad_qkv[i], qkv_w[:, cols])
     grad_merged = (grad_one * live_col[...]).astype(BF16)
     mq = query[...]
     probs, same = group_probs(mq, x, live_row[0], scale)
@@ -249,7 +284,7 @@
     grad_scores = probs * (grad_probs - jnp.sum(probs * grad_probs, axis=-1, keepdims=True))
     grad_scores = jnp.where(same & (live_row[0] > 0), grad_scores, 0.0)
     grad_query = (mm(grad_scores.astype(BF16), x) * scale).astype(BF16)
-    grad_query_out[...] = grad_query
+    merge_grad[...] += mm(x.T, grad_query)
     blocks = mm(probs.T.astype(BF16), grad_merged) + mm(grad_scores.T.astype(BF16), mq) * scale
     blocks += mm_t(grad_query, merge_w[...])
     grad_input[...] = (grad_one + blocks).astype(BF16)
@@ -270,6 +305,7 @@
 
 MESH = pl.DeviceIdType.MESH
 TABLE_MAJOR = 4
+UP_CUTS = 6
 CORES = 2
 
 
@@ -299,14 +335,14 @@
     def region(item, done):
         array, low, size, order = items[item]
         where = tuple(slice(None) if axis in done else spot[axis] for axis in sorted(order))
-        return fulls[array].at[(*where, slice(None), pl.ds(low, size))]
+        return fulls[array].at[(*where, pl.ds(low, size))]
 
     def copies(item, stage):
         array, low, size, order = items[item]
         place = region(item, order[:stage])
         return [
             pltpu.make_async_remote_copy(
-                src_ref=place if stage else shards[array].at[:, pl.ds(low, size)],
+                src_ref=place if stage else shards[array].at[pl.ds(low, size)],
                 dst_ref=place,
                 send_sem=send_sem.at[item, stage, offset],
                 recv_sem=recv_sem.at[item, stage, offset],
@@ -318,7 +354,7 @@
 
     def keep(item):
         array, low, size, _ = items[item]
-        return pltpu.make_async_copy(shards[array].at[:, pl.ds(low, size)], region(item, ()), local_sem.at[item])
+        return pltpu.make_async_copy(shards[array].at[pl.ds(low, size)], region(item, ()), local_sem.at[item])
 
     def begin():
         for item in range(len(items)):
@@ -362,10 +398,15 @@
 def scatter_events(dims, spot, items, grads, outs, buffers, local_sem, send_sem, recv_sem):
     buffers = [buffers[i * 7 : (i + 1) * 7] for i in range(len(items))]
 
+    def piece(item, core):
+        array, low, size, _ = items[item]
+        if size <= grads[array].shape[4]:
+            return grads[array].at[:, :, :, core, pl.ds(low, size)]
+        return grads[array].at[:, :, :, core, :, pl.ds(low, size)]
+
     def load(item):
-        array, low, size, _ = items[item]
         return pltpu.make_async_copy(
-            grads[array].at[:, :, :, spot[3], :, pl.ds(low, size)], buffers[item][0], local_sem.at[item]
+            piece(item, spot[3]), buffers[item][0], local_sem.at[item]
         )
 
     def copies(item, stage):
@@ -376,7 +417,7 @@
         for offset in range(1, dims[axis]):
             target, other = peer(dims, spot, axis, offset)
             if stage == 0:
-                source, landing = grads[array].at[:, :, :, other, :, pl.ds(low, size)], got_core
+                source, landing = piece(item, other), got_core
             elif stage == 1:
                 source = own.at[:, :, other] if axis == 2 else own.at[:, other]
                 landing = got_first.at[offset - 1]
@@ -396,8 +437,8 @@
             )
         return made
 
-    def begin():
-        for item in range(len(items)):
+    def begin(chosen=tuple(range(len(items)))):
+        for item in chosen:
             load(item).start()
             for copy in copies(item, 0):
                 copy.start()
@@ -439,7 +480,10 @@
             value = second[mine].astype(F32)
             for k in others:
                 value += got_last[k].astype(F32)
-            outs[array][:, low : low + size] = value
+            if size <= grads[array].shape[4]:
+                outs[array][low : low + size] = value
+            else:
+                outs[array][:, low : low + size] = value
         if stage < 3:
             for copy in copies(item, stage + 1):
                 copy.start()
@@ -497,7 +541,8 @@
 def scatter_scratch(dims, grads, items):
     scratch = []
     for array, _, size, order in items:
-        tail = (grads[array].shape[4], size)
+        rows, cols = grads[array].shape[4:]
+        tail = (size, cols) if size <= rows else (rows, size)
         inner = dims[order[2]]
         for shape in (
             dims[:3],
@@ -516,8 +561,26 @@
     return [pltpu.SemaphoreType.DMA((count, 4, most)), pltpu.SemaphoreType.DMA((count, 4, most))]
 
 
-def moving_call(dims, collective_id, name, kernel, grid, own_in, own_out, gather, scatter, square, pace=1.0):
+def split(array, size, pieces, *orders):
+    part = size // pieces
+    return [(array, i * part, part, orders[i % len(orders)]) for i in range(pieces)]
+
+
+def plain_call(kernel, grid, refs, outs, name):
+    return pl.pallas_call(
+        kernel,
+        grid=grid,
+        in_specs=[spec for spec, _ in refs],
+        out_specs=[spec for spec, _ in outs],
+        out_shape=[shape for _, shape in outs],
+        compiler_params=params(),
+        name=name,
+    )(*(arg for _, arg in refs))
+
+
+def moving_call(dims, collective_id, name, kernel, grid, own_in, own_out, gather, scatter, square, pace=1.0, made=(), early=(), after=None, extra=()):
     most = max(dims)
+    total = dims[0] * dims[1] * dims[2] * dims[3]
     vmem, anywhere = (lambda a: fixed(a.shape)), (lambda a: pl.BlockSpec(memory_space=pl.ANY))
     shards, gather_items = gather
     grads, scatter_items = scatter
@@ -530,8 +593,13 @@
     for i, a in enumerate(shards):
         out_specs.append(anywhere(a))
         out_shape.append(jax.ShapeDtypeStruct((*(dims[axis] for axis in orders[i]), *a.shape), a.dtype))
-    for g in grads:
+    whole = [*grads, *early]
+    after = after or {}
+    for g in whole:
         out_shape.append(jax.ShapeDtypeStruct(g.shape[4:], F32))
+        out_specs.append(vmem(out_shape[-1]))
+    for g in made:
+        out_shape.append(jax.ShapeDtypeStruct((g.shape[0] // total, g.shape[1]), F32))
         out_specs.append(vmem(out_shape[-1]))
     for q in squares:
         out_shape.append(jax.ShapeDtypeStruct(q.shape, F32))
@@ -540,8 +608,8 @@
     if shards:
         groups.append([pltpu.SemaphoreType.DMA((len(gather_items),)), *links(len(gather_items), most)])
     if grads:
-        buffers = scatter_scratch(dims, grads, scatter_items)
-        groups.append([*buffers, pltpu.SemaphoreType.DMA((len(scatter_items),)), *links(len(scatter_items), most)])
+        buffers = scatter_scratch(dims, whole, scatter_items)
+        groups.append([*extra, *(pltpu.VMEM(g.shape, BF16) for g in early), *buffers, pltpu.SemaphoreType.DMA((len(scatter_items),)), *links(len(scatter_items), most)])
     if squares:
         groups.append(
             [
@@ -551,6 +619,12 @@
                 pltpu.SemaphoreType.DMA((4, most)),
             ]
         )
+    if made:
+        made_shapes = [jax.ShapeDtypeStruct((*dims, g.shape[0] // total, g.shape[1]), BF16) for g in made]
+        made_items = [(i, 0, g.shape[4], (3, 2, 1, 0) if i % 2 == 0 else (3, 1, 2, 0)) for i, g in enumerate(made_shapes)]
+        buffers = [pltpu.VMEM(g.shape, F32) for g in made] + [pltpu.VMEM(g.shape, BF16) for g in made_shapes]
+        buffers += scatter_scratch(dims, made_shapes, made_items)
+        groups.append([*buffers, pltpu.SemaphoreType.DMA((len(made),)), *links(len(made), most)])
     steps = 1
     for size in grid:
         steps *= size
@@ -564,7 +638,8 @@
             return taken
 
         ins, shard_refs, grad_refs, square_refs = take(len(own_in)), take(len(shards)), take(len(grads)), take(len(squares))
-        outs, full_refs, sum_refs, total_refs = take(len(own_out)), take(len(shards)), take(len(grads)), take(len(squares))
+        outs, full_refs, sum_refs = take(len(own_out)), take(len(shards)), take(len(whole))
+        made_outs, total_refs = take(len(made)), take(len(squares))
         step = 0
         for axis, size in enumerate(grid):
             step = step * size + pl.program_id(axis)
@@ -575,9 +650,40 @@
             plans.append(gather_events(dims, spot, gather_items, shard_refs, full_refs, *take(len(next(scratch)))))
         if grads:
             held = take(len(next(scratch)))
-            plans.append(scatter_events(dims, spot, scatter_items, grad_refs, sum_refs, held[:-3], *held[-3:]))
+            turned, held = held[: len(extra)], held[len(extra) :]
+            early_refs, held = held[: len(early)], held[len(early) :]
+            begin_some, some_groups, end_some = scatter_events(
+                dims, spot, scatter_items, grad_refs + early_refs, sum_refs, held[:-3], *held[-3:]
+            )
+            ready = [item for item in range(len(scatter_items)) if item not in after]
+            plans.append((functools.partial(begin_some, ready), some_groups, end_some))
+        else:
+            turned, early_refs = [], []
         if squares:
             plans.append(square_events(dims, spot, *square_refs, *total_refs, *take(len(next(scratch)))))
+
+        if made:
+            held = take(len(next(scratch)))
+            sums, lows = held[: len(made)], held[len(made) : 2 * len(made)]
+            begin_made, made_groups, end_made = scatter_events(
+                dims, spot, made_items, lows, made_outs, held[2 * len(made) : -3], *held[-3:]
+            )
+        else:
+            sums, made_groups = [], []
+
+        def round_made():
+            for value, low in zip(sums, lows):
+                rows = low.shape[4]
+
+                @pl.loop(0, total)
+                def _(i):
+                    at = (
+                        i // (dims[1] * dims[2] * dims[3]),
+                        lax.rem(i // (dims[2] * dims[3]), dims[1]),
+                        lax.rem(i // dims[3], dims[2]),
+                        lax.rem(i, dims[3]),
+                    )
+                    low[at] = value[pl.ds(pl.multiple_of(i * rows, rows), rows), :].astype(BF16)
 
         def open_all():
             greet(dims, spot)
@@ -611,13 +717,23 @@
                 pl.when(step == at)(run)
             else:
                 late.append(run)
-        kernel(*ins, *outs)
+        kernel(*ins, *outs, *sums, *early_refs, *turned)
+        for item, at in after.items():
+            pl.when(step == at)(functools.partial(begin_some, (item,)))
 
         @pl.when(step == steps - 1)
         def _():
-            for run in late:
-                run()
+            if made:
+                round_made()
+                begin_made()
+            for i in range(max(len(late), len(made_groups))):
+                if i < len(late):
+                    late[i]()
+                for event in made_groups[i] if i < len(made_groups) else ():
+                    event()
             close_all()
+            if made:
+                end_made()
 
     return pl.pallas_call(
         fused,
@@ -691,11 +807,9 @@
             (
                 (qkv_w, merge_w, vec_row),
                 (
-                    (1, 0, width, down_out),
-                    (0, 0, width, up_out),
-                    (0, width, width, down_out),
-                    (0, 2 * width, width, up_out),
-                    (2, 0, width, down_out),
+                    (1, 0, share, down_out),
+                    *split(0, share, 3, up_out, down_out),
+                    (2, 0, 8, up_out),
                 ),
             ),
             none,
@@ -793,11 +907,11 @@
         limit = jnp.broadcast_to(class_count.astype(F32)[:, None], (1, classes))
         spare = -(rows + 1) % 8
         small = jnp.concatenate([logit_cotangent, limit, jnp.zeros((spare, classes), F32)], axis=0)
-        third, narrow = ff // 3, width // 3
-        gather_items = [(3, 0, classes, (2, 3)), (4, 0, classes, (2, 3))]
-        for i in range(3):
-            gather_items += [(0, i * third, third, up_out), (1, i * narrow, narrow, down_out)]
-        gather_items.append((2, 0, width, down_out))
+        gather_items = [(3, 0, width, (2, 3)), (4, 0, small.shape[0], (2, 3))]
+        up_items, down_items = split(0, share, 3, up_out), split(1, wide_ff * share, 3, down_out)
+        for pair in zip(up_items, down_items):
+            gather_items += pair
+        gather_items.append((2, 0, share, down_out))
         context, lse, up_full, down_full, out_full, heads, small = moving_call(
             dims,
             2,
@@ -889,82 +1003,73 @@
     grad_rows = grad_ctx.reshape(rows, seq, width)
     cls_rows = layer_out.reshape(rows, seq, width)[:, 0, :]
     back_refs = [*attn_in_refs, (lse_block, lse), (head_block(0), grad_rows)]
-    back_outs = [(head_block(0), jax.ShapeDtypeStruct((rows, seq, width), BF16))] * 3
-    attend_back = functools.partial(attn_back_kernel, head**-0.5)
-    grad_out_w = t_mm(context, grad_attn).astype(BF16)
-    grad_up_w = t_mm(ffn_in, grad_up).astype(BF16)
+    back_outs = [
+        (
+            pl.BlockSpec((3, 1, seq, lanes), lambda r, p: (0, r, 0, p)),
+            jax.ShapeDtypeStruct((3, rows, seq, width), BF16),
+        )
+    ]
     grad_down_w = t_mm(activated, grad_down).astype(BF16)
     if direct:
-        ffn_items = []
-        for i in range(3):
-            ffn_items += [(0, i * third, third, up_in), (1, i * narrow, narrow, down_in)]
-        ffn_items.append((2, 0, width, down_in))
+        part = ff // UP_CUTS
+        back_refs += [
+            (fixed((count, width)), ffn_in),
+            (pl.BlockSpec((count, part), lambda r, p: (0, jnp.minimum(r * pairs + p, UP_CUTS - 1))), grad_up),
+            (fixed((count, width)), context),
+            (fixed((count, width)), grad_attn),
+        ]
+        ffn_items = [
+            *split(0, wide_ff * share, 3, up_in, down_in),
+            *split(1, ff, 3, down_in, up_in),
+            (2, 0, share, up_in),
+        ]
         first_rows = jnp.pad(cls_rows, ((0, -rows % 8), (0, 0)))
-        grad_q, grad_k, grad_v, group_cls, own_up, own_down, own_out = moving_call(
+        grad_qkv, group_cls, own_down, own_up, own_out = moving_call(
             dims,
             3,
             "attention_back_scatter",
-            attend_back,
+            functools.partial(attn_back_weights_kernel, head**-0.5, pairs, UP_CUTS),
             (rows, pairs),
             back_refs,
             back_outs,
-            ((first_rows,), ((0, 0, width, (2, 3)),)),
-            ([g.reshape(*dims, -1, g.shape[-1]) for g in (grad_up_w, grad_down_w, grad_out_w)], ffn_items),
+            ((first_rows,), ((0, 0, first_rows.shape[0], (2, 3)),)),
+            ([grad_down_w.reshape(*dims, -1, width)], ffn_items),
             None,
             pace=2.4,
+            early=(jax.ShapeDtypeStruct((*dims, share, ff), BF16), jax.ShapeDtypeStruct((*dims, share, width), BF16)),
+            after={3: UP_CUTS // 3 - 1, 4: 2 * UP_CUTS // 3 - 1, 5: UP_CUTS - 1, 6: UP_CUTS},
+            extra=(pltpu.VMEM((width, count), BF16),),
         )
         group_cls = group_cls.reshape(batch, -1, width)[:, :rows].reshape(batch * rows, width)
     else:
-        grad_q, grad_k, grad_v = pl.pallas_call(
-            attend_back,
-            grid=(rows, pairs),
-            in_specs=[spec for spec, _ in back_refs],
-            out_specs=[spec for spec, _ in back_outs],
-            out_shape=[shape for _, shape in back_outs],
-            compiler_params=params(),
-            name="attention_back",
-        )(*(arg for _, arg in back_refs))
+        grad_out_w = t_mm(context, grad_attn).astype(BF16)
+        grad_up_w = t_mm(ffn_in, grad_up).astype(BF16)
+        attend_back = functools.partial(attn_back_kernel, head**-0.5)
+        (grad_qkv,) = plain_call(attend_back, (rows, pairs), back_refs, back_outs, "attention_back")
         group_cls = lax.all_gather(cls_rows, "batch", axis=0, tiled=True)
 
-    grad_input, grad_query, grad_packed, bias_sums = pl.pallas_call(
-        input_kernel,
-        grid=(tiles,),
-        in_specs=[
-            tiled(TILE, width),
-            tiled(TILE, width),
-            tiled(TILE, width),
-            tiled(TILE, width),
-            tiled(TILE, width),
-            tiled(TILE, width),
-            pl.BlockSpec((1, 1, TILE), lambda i: (i, 0, 0)),
-            tiled(TILE, 1),
-            fixed((width, width)),
-            fixed((width, 3 * width)),
-        ],
-        out_specs=[tiled(TILE, width), tiled(TILE, width), tiled(TILE, 3 * width), fixed((8, width))],
-        out_shape=[
-            jax.ShapeDtypeStruct((count, width), BF16),
-            jax.ShapeDtypeStruct((count, width), BF16),
-            jax.ShapeDtypeStruct((count, 3 * width), BF16),
-            jax.ShapeDtypeStruct((8, width), F32),
-        ],
+    grad_qkv = grad_qkv.reshape(3, count, width)
+    grad_qkv_w, qkv_sums = pl.pallas_call(
+        qkv_grad_kernel,
+        grid=(3,),
+        in_specs=[fixed((count, width)), pl.BlockSpec((1, count, width), lambda i: (i, 0, 0))],
+        out_specs=[pl.BlockSpec((width, width), lambda i: (0, i)), pl.BlockSpec((8, width), lambda i: (0, i))],
+        out_shape=[jax.ShapeDtypeStruct((width, 3 * width), BF16), jax.ShapeDtypeStruct((8, 3 * width), F32)],
+        scratch_shapes=[pltpu.VMEM((width, count), BF16)],
         compiler_params=params(),
-        name="merge_back",
-    )(
-        grad_q.reshape(count, width),
-        grad_k.reshape(count, width),
-        grad_v.reshape(count, width),
-        grad_two,
-        tok_flat,
-        merge_query,
-        live_row,
-        live_col,
-        merge_full,
-        qkv_full,
-    )
-
-    grad_merge_w = t_mm(tok_flat, grad_query).astype(BF16)
-    grad_qkv_w = t_mm(attn_in, grad_packed).astype(BF16)
+        name="qkv_grad",
+    )(attn_in, grad_qkv)
+    bias_sums = [qkv_sums[0, :width], qkv_sums[0, 2 * width :]]
+    input_refs = [
+        (pl.BlockSpec((3, TILE, width), lambda i: (0, i, 0)), grad_qkv),
+        *((tiled(TILE, width), a) for a in (grad_two, tok_flat, merge_query)),
+        (pl.BlockSpec((1, 1, TILE), lambda i: (i, 0, 0)), live_row),
+        (tiled(TILE, 1), live_col),
+        (fixed((width, width)), merge_full),
+        (fixed((width, 3 * width)), qkv_full),
+    ]
+    input_outs = [(tiled(TILE, width), jax.ShapeDtypeStruct((count, width), BF16))]
+    merge_grad = jax.ShapeDtypeStruct((width, width), F32)
 
     vec_grads = (sums[8], sums[3], sums[4], sums[2], sums[0], sums[1], bias_sums[0], bias_sums[1])
     vec_block = jnp.concatenate(
@@ -983,30 +1088,29 @@
     )
     if direct:
         square = jnp.broadcast_to(jnp.pad(partial, (0, 2))[:, None], (8, 128))
-        own_qkv, own_merge, own_vec, square = moving_call(
+        grad_input, own_qkv, own_vec, own_merge, square = moving_call(
             dims,
             1,
-            "scatter_last",
-            None,
-            (1,),
-            [],
-            [],
+            "merge_back_scatter",
+            input_kernel,
+            (tiles,),
+            input_refs,
+            input_outs,
             none,
             (
-                [g.reshape(*dims, -1, g.shape[-1]) for g in (grad_qkv_w, grad_merge_w, vec_block)],
-                (
-                    (0, 0, width, up_in),
-                    (0, width, width, down_in),
-                    (0, 2 * width, width, up_in),
-                    (1, 0, width, down_in),
-                    (2, 0, width, up_in),
-                ),
+                [g.reshape(*dims, -1, g.shape[-1]) for g in (grad_qkv_w, vec_block)],
+                (*split(0, share, 3, up_in, down_in), (1, 0, 8, down_in)),
             ),
             square,
+            made=(merge_grad,),
         )
         own_vec = own_vec[0]
         totals = square[:6, 0]
     else:
+        input_outs.append((fixed((width, width)), merge_grad))
+        grad_input, grad_merge_w = plain_call(input_kernel, (tiles,), input_refs, input_outs, "merge_back")
+        grad_merge_w = grad_merge_w.astype(BF16)
+
         def owners(mat, n):
             return mat.reshape(devices, share, n, width).transpose(0, 2, 1, 3).reshape(devices, n * share, width)
 

time: 435 us -> 417 us (0.959); the launches traced: 427 us -> 416 us
  matrix products: 43.9 us -> 15.5 us
  Pallas kernels: 334 us -> 348 us
    dot_general x5 -> x1, matrix products: 40.7 us -> 12.3 us  [t_mm(): lax.dot_general(left, right, (((0,), (0,)), ((), ())), preferred_element_...]
    pallas_call x4, Pallas kernels: 241 us -> 265 us  [moving_call(): pl.pallas_call(fused, grid=grid, in_specs=in_specs, out_specs=out_specs,...]
    pallas_call x1, Pallas kernels: 20.7 us -> 10.2 us  [body(): pl.pallas_call(qkv_grad_kernel, grid=(3,), in_specs=[fixed((count, width)...]
where the time goes in v4:
time: 417 us; the launch traced here: 416 us
  Pallas kernels  348 us (83%)
  local copies, waits for them, and re-layouts  35.3 us (8%)
  matrix products  15.5 us (4%)
  other arithmetic  15 us (4%)
    pallas_call x4, Pallas kernels, moving_call(): pl.pallas_call(fused, grid=grid, in_specs=in_specs, out_specs=out_specs,...  265 us
    pallas_call x1, Pallas kernels, body(): pl.pallas_call(functools.partial(ffn_kernel, per_row), grid=(tiles,), in_...  53.9 us
    pallas_call x1, Pallas kernels, body(): pl.pallas_call(merge_kernel, grid=(tiles,), in_specs=[tiled(TILE, width),...  19 us
    dot_general x1, matrix products, t_mm(): lax.dot_general(left, right, (((0,), (0,)), ((), ())), preferred_element_...  12.3 us
    pallas_call x1, Pallas kernels, body(): pl.pallas_call(qkv_grad_kernel, grid=(3,), in_specs=[fixed((count, width)...  10.2 us

profile of v4, /device:TPU:0, one launch (start us, length us, event | category | flops | bytes accessed | tf_op | source)
XLA Modules:
  0.0 416.0 jit_solution(2714032612728249239)
XLA Ops:
  1.3 0.7 dynamic_slice.3
  2.1 0.7 compare_convert_fusion.1
  3.0 6.1 %concatenate.19 = bf16[288]{0:T(512)(128)(2,1)S(1)} concatenate(bf16[24]{0:T(256)(128)(2,1)} %param.32, bf16[24]{0:T(256)(128)(2,1)} %param.33, bf16[24]{0:T(256)(128)(2,1)} %param.34, bf16[24]{0:T(256)(128)(2,1)} %param.38, bf16[24]{0:T(256)(128)(2,1)} %param.39, bf16[24]{0:T(256)(128)(2,1)} %param.40, bf16[24]{0:T(256)(128)(2,1)} %param.29, bf16[24]{0:T(256)(128)(2,1)} %param.30, ...), dimensions={0} | concatenate | bytes 1152 | tf_op jit(solution)/shard_map/concatenate | solution.py:791
  9.2 0.7 lt.148
  10.1 1.3 maximum_maximum_fusion.refs_8_
  11.5 0.7 compare_bitcast_fusion
  12.3 0.6 reshape.453.refs_2_
  13.0 1.4 convert_reduce_fusion
  14.4 0.8 broadcast_in_dim.24
  15.4 0.7 and_convert_fusion.live_row.refs_4_
  16.8 1.0 fusion.1.live_col.refs_5_
  18.1 1.1 and_select_fusion.refs_3_
  19.2 45.9 %gather_first.1 = (bf16[4,2,2,2,24,2304]{5,4,3,2,1,0:T(8,128)(2,1)}, bf16[4,2,2,2,24,768]{5,4,3,2,1,0:T(8,128)(2,1)}, bf16[4,2,2,2,8,768]{5,4,3,2,1,0:T(8,128)(2,1)}) custom-call(bf16[24,2304]{1,0:T(8,128)(2,1)} %refs_0_.1, bf16[24,768]{1,0:T(8,128)(2,1)} %refs_1_.1, bf16[8,768]{1,0:T(8,128)(2,1)} %reshape.453.refs_2_), custom_call_target="tpu_custom_call" | custom-call | tf_op jit(solution)/shard_map/gather_first/pallas_call | solution.py:738
  65.1 1.1 slice.216
  67.8 0.7 fusion.2.vecs
  68.5 19.0 %merge_qkv.1 = (bf16[1536,768]{1,0:T(8,128)(2,1)}, f32[1536,768]{1,0:T(8,128)}, bf16[1536,768]{1,0:T(8,128)(2,1)}, bf16[1536,2304]{1,0:T(8,128)(2,1)}, f32[8,768]{1,0:T(8,128)}) custom-call(bf16[1536,768]{1,0:T(8,128)(2,1)} %bitcast.98, f32[6,1,256]{2,1,0:T(1,128)} %and_convert_fusion.live_row.refs_4_, f32[1536,1]{1,0:T(8,128)} %fusion.1.live_col.refs_5_, ...), custom_call_target="tpu_custom_call" | custom-call | tf_op jit(solution)/shard_map/merge_qkv/pallas_call | solution.py:857
  87.5 1.4 slice_reduce_fusion.11
  88.9 76.4 %attention_gather.1 = (bf16[3,512,768]{2,1,0:T(8,128)(2,1)}, f32[3,6,2,512]{3,2,1,0:T(2,128)}, bf16[4,2,2,2,24,3072]{5,4,3,2,1,0:T(8,128)(2,1)}, bf16[4,2,2,2,96...) custom-call(bf16[3,512,2304]{2,1,0:T(8,128)(2,1)} %bitcast.86, ...), custom_call_target="tpu_custom_call" | custom-call | tf_op jit(solution)/shard_map/attention_gather/pallas_call | solution.py:738
  165.3 0.7 slice.219
  166.1 0.7 slice.238
  167.0 1.9 convolution_bitcast_fusion.1
  168.9 0.6 reshape.465.cls_grad
  169.5 53.9 %ffn.1 = (bf16[1536,768]{1,0:T(8,128)(2,1)}, bf16[1536,3072]{1,0:T(8,128)(2,1)}, bf16[1536,3072]{1,0:T(8,128)(2,1)}, bf16[1536,768]{1,0:T(8,128)(2,1)}, bf16[153...) custom-call(bf16[1536,768]{1,0:T(8,128)(2,1)} %bitcast.96, ...), custom_call_target="tpu_custom_call" | custom-call | tf_op jit(solution)/shard_map/ffn/pallas_call | solution.py:960
  223.4 1.5 slice_reduce_fusion.8
  224.9 0.8 convert.37
  225.8 4.0 stack.27
  229.7 0.7 broadcast_in_dim.57.refs_10_
  230.5 0.9 fusion.10
  232.0 0.8 slice.227
  233.0 0.7 compare_select_fusion
  234.3 12.3 %convolution_convert_fusion = bf16[3072,768]{1,0:T(8,128)(2,1)} fusion(bf16[1536,3072]{1,0:T(8,128)(2,1)} %get-tuple-element.73, bf16[1536,768]{1,0:T(8,128)(2,1)} %get-tuple-element.74), kind=kOutput, calls=%fused_computation | convolution fusion | flops 7250116608 | bytes 16515072 | tf_op jit(solution)/shard_map/dot_general | solution.py:32
  246.6 80.1 %attention_back_scatter.1 = (bf16[3,3,512,768]{3,2,1,0:T(8,128)(2,1)}, bf16[2,2,8,768]{3,2,1,0:T(8,128)(2,1)}, f32[96,768]{1,0:T(8,128)}, f32[24,3072]{1,0:T(8,128)}, f32[24,768]{1,0:T(8,128)}) custom-call(bf16[3,512,2304]{2,1,0:T(8,128)(2,1)} %bitcast.89, bf16[3,512,2304]{2,1,0:T(8,128)(2,1)} %bitcast.90, bf16[3,512,2304]{2,1,0:T(8,128)(2,1)} %bitcast.91, ...), custom_call_target="tpu_custom_call" | custom-call | tf_op jit(solution)/shard_map/attention_back_scatter/pallas_call | solution.py:738
  326.7 0.8 slice.237
  327.5 1.1 convolution_bitcast_fusion
  328.6 10.2 %qkv_grad.1 = (bf16[768,2304]{1,0:T(8,128)(2,1)}, f32[8,2304]{1,0:T(8,128)}) custom-call(bf16[1536,768]{1,0:T(8,128)(2,1)} %get-tuple-element.78.attn_in, bf16[3,1536,768]{2,1,0:T(8,128)(2,1)} %bitcast.92), custom_call_target="tpu_custom_call" | custom-call | tf_op jit(solution)/shard_map/qkv_grad/pallas_call | solution.py:1052
  338.8 0.9 convert.38
  340.1 0.8 copy.76
  340.9 62.4 %merge_back_scatter.1 = (bf16[1536,768]{1,0:T(8,128)(2,1)}, f32[24,2304]{1,0:T(8,128)}, f32[8,768]{1,0:T(8,128)}, f32[24,768]{1,0:T(8,128)}, f32[8,128]{1,0:T(8,128)}) custom-call(bf16[3,1536,768]{2,1,0:T(8,128)(2,1)} %bitcast.93, f32[1536,768]{1,0:T(8,128)} %get-tuple-element.76.refs_1_, bf16[1536,768]{1,0:T(8,128)(2,1)} %bitcast.99, ...), custom_call_target="tpu_custom_call" | custom-call | tf_op jit(solution)/shard_map/merge_back_scatter/pallas_call | solution.py:738
  403.3 1.2 slice.215
  405.2 1.3 sqrt_reduce_fusion
  406.5 1.3 slice_bitcast_fusion.3
  407.8 1.5 slice_bitcast_fusion
  409.3 3.3 copy.97
  412.6 0.6 copy.98
  413.3 0.7 copy.99
  414.0 0.6 copy.100
  414.6 0.7 copy.101
  415.3 0.7 copy.102
  (81 shorter events, 5.7 us)
Async XLA Ops:
  0.7 17.4 %copy-start.6 = (s32[3]{0:T(128)S(1)}, s32[3]{0:T(128)}, u32[]{:S(2)}) copy-start(s32[3]{0:T(128)} %param.23) | copy-start | bytes 40
  88.9 78.0 %copy-start.7 = (f32[3,128]{1,0:T(4,128)S(1)}, f32[3,128]{1,0:T(4,128)}, u32[]{:S(2)}) copy-start(f32[3,128]{1,0:T(4,128)} %param.43) | copy-start | bytes 4612
  169.5 63.3 %copy-start = (bf16[2,2,768,128]{3,2,1,0:T(8,128)(2,1)S(1)}, bf16[2,2,768,128]{3,2,1,0:T(8,128)(2,1)}, u32[]{:S(2)}) copy-start(bf16[2,2,768,128]{3,2,1,0:T(8,128)(2,1)} %get-tuple-element.63) | copy-start | bytes 2359300
  409.3 3.3 copy-start.5
  409.3 4.0 copy-start.3
  409.3 4.7 %copy-start.4 = (f32[24,768]{1,0:T(8,128)S(1)}, f32[24,768]{1,0:T(8,128)}, u32[]{:S(2)}) copy-start(f32[24,768]{1,0:T(8,128)} %get-tuple-element.171) | copy-start | bytes 221188
  409.3 5.3 %copy-start.2 = (f32[24,3072]{1,0:T(8,128)S(1)}, f32[24,3072]{1,0:T(8,128)}, u32[]{:S(2)}) copy-start(f32[24,3072]{1,0:T(8,128)} %get-tuple-element.175) | copy-start | bytes 884740
  409.3 6.0 %copy-start.1 = (f32[96,768]{1,0:T(8,128)S(1)}, f32[96,768]{1,0:T(8,128)}, u32[]{:S(2)}) copy-start(f32[96,768]{1,0:T(8,128)} %get-tuple-element.177) | copy-start | bytes 884740

commit v5 on v4

--- a/solution.py
+++ b/solution.py
@@ -306,6 +306,7 @@
 MESH = pl.DeviceIdType.MESH
 TABLE_MAJOR = 4
 UP_CUTS = 6
+ATTN_PACE, BACK_PACE, LAST_PACE = 3.0, 2.4, 2.5
 CORES = 2
 
 
@@ -788,9 +789,10 @@
     dims = (TABLE_MAJOR, table_size // TABLE_MAJOR, batch_size // CORES, CORES)
     direct = share % BLOCK == 0
     vec_list = (out_bias, gain_one, shift_one, down_bias, gain_two, shift_two, query_bias, value_bias)
-    vec_row = jnp.concatenate([*vec_list, up_bias])
-    used = vec_row.shape[0]
-    vec_row = jnp.pad(vec_row, (0, 8 * width - used)).reshape(8, width)
+    used = 8 * share + up_bias.shape[0]
+    spare = jnp.zeros((8 * width - used,), F32)
+    vec_row = jnp.concatenate([*(v.astype(F32) for v in (*vec_list, up_bias)), spare])
+    vec_row = vec_row.reshape(8, width).astype(BF16)
     base = (5 + wide_ff) * share
     down_out, up_out = (0, 1, 2, 3), (0, 2, 1, 3)
     down_in, up_in = (3, 1, 2, 0), (3, 2, 1, 0)
@@ -907,11 +909,14 @@
         limit = jnp.broadcast_to(class_count.astype(F32)[:, None], (1, classes))
         spare = -(rows + 1) % 8
         small = jnp.concatenate([logit_cotangent, limit, jnp.zeros((spare, classes), F32)], axis=0)
-        gather_items = [(3, 0, width, (2, 3)), (4, 0, small.shape[0], (2, 3))]
         up_items, down_items = split(0, share, 3, up_out), split(1, wide_ff * share, 3, down_out)
-        for pair in zip(up_items, down_items):
-            gather_items += pair
-        gather_items.append((2, 0, share, down_out))
+        gather_items = [
+            *(up_items[0], down_items[0], up_items[1], down_items[1]),
+            (2, 0, share, (2, 1, 0, 3)),
+            (3, 0, width, (2, 3)),
+            *(up_items[2], down_items[2]),
+            (4, 0, small.shape[0], (2, 3)),
+        ]
         context, lse, up_full, down_full, out_full, heads, small = moving_call(
             dims,
             2,
@@ -923,7 +928,7 @@
             ((up_w, down_w, out_w, head_w[0], small), gather_items),
             none,
             None,
-            pace=2.2,
+            pace=ATTN_PACE,
         )
         up_full = up_full.reshape(width, ff)
         down_full = down_full.reshape(ff, width)
@@ -1035,7 +1040,7 @@
             ((first_rows,), ((0, 0, first_rows.shape[0], (2, 3)),)),
             ([grad_down_w.reshape(*dims, -1, width)], ffn_items),
             None,
-            pace=2.4,
+            pace=BACK_PACE,
             early=(jax.ShapeDtypeStruct((*dims, share, ff), BF16), jax.ShapeDtypeStruct((*dims, share, width), BF16)),
             after={3: UP_CUTS // 3 - 1, 4: 2 * UP_CUTS // 3 - 1, 5: UP_CUTS - 1, 6: UP_CUTS},
             extra=(pltpu.VMEM((width, count), BF16),),
@@ -1076,18 +1081,9 @@
         [v.reshape(devices, share) for v in vec_grads] + [up_sums[0].reshape(devices, wide_ff * share)], axis=1
     )
     vec_block = jnp.pad(vec_block, ((0, 0), (0, 8 * width - used))).astype(BF16).reshape(devices, 8, width)
-    partial = jnp.stack(
-        [
-            jnp.sum(squares[0]),
-            jnp.sum(squares[1]),
-            jnp.sum(sums[5]),
-            jnp.sum(sums[6]),
-            jnp.sum(sums[7]),
-            jnp.sum(live_mask),
-        ]
-    )
+    live_sums = jnp.sum(live_mask.reshape(-1, width), axis=0, keepdims=True)
+    square = jnp.concatenate([squares[:2], sums[5:8], live_sums, jnp.zeros((2, width), F32)], axis=0)
     if direct:
-        square = jnp.broadcast_to(jnp.pad(partial, (0, 2))[:, None], (8, 128))
         grad_input, own_qkv, own_vec, own_merge, square = moving_call(
             dims,
             1,
@@ -1102,10 +1098,10 @@
                 (*split(0, share, 3, up_in, down_in), (1, 0, 8, down_in)),
             ),
             square,
+            pace=LAST_PACE,
             made=(merge_grad,),
         )
         own_vec = own_vec[0]
-        totals = square[:6, 0]
     else:
         input_outs.append((fixed((width, width)), merge_grad))
         grad_input, grad_merge_w = plain_call(input_kernel, (tiles,), input_refs, input_outs, "merge_back")
@@ -1134,7 +1130,7 @@
         own_vec = owned[base + wide_ff * share]
         own_merge, own_qkv, own_out, own_up = joined(0, 1), joined(2 * share, 3), joined(share, 1), joined(5 * share, wide_ff)
         own_down = owned[base : base + wide_ff * share]
-        totals = lax.psum(partial, BOTH)
+        square = lax.psum(square, BOTH)
     own_vecs = [own_vec[i * share : (i + 1) * share] for i in range(8)]
     own_up_bias = own_vec[8 * share : 8 * share + wide_ff * share]
 
@@ -1149,6 +1145,7 @@
     grad_head = lax.dot_general(
         group_cls.astype(F32), group_dlog, (((0,), (0,)), ((), ())), precision=PRECISE, preferred_element_type=F32
     )[None]
+    totals = jnp.sum(square[:6], axis=1)
     root_squares = jnp.sqrt(totals[:5] / (totals[5] * width))
     return (
         layer_rows,

time: 417 us -> 401 us (0.962)
  Pallas kernels: 348 us -> 338 us
    pallas_call x4, Pallas kernels: 265 us -> 255 us  [moving_call(): pl.pallas_call(fused, grid=grid, in_specs=in_specs, out_specs=out_specs,...]
where the time goes in v5:
time: 401 us; the launch traced here: 399 us
  Pallas kernels  338 us (84%)
  local copies, waits for them, and re-layouts  31.8 us (8%)
  matrix products  15.5 us (4%)
  other arithmetic  12.2 us (3%)
    pallas_call x4, Pallas kernels, moving_call(): pl.pallas_call(fused, grid=grid, in_specs=in_specs, out_specs=out_specs,...  255 us
    pallas_call x1, Pallas kernels, body(): pl.pallas_call(functools.partial(ffn_kernel, per_row), grid=(tiles,), in_...  53.9 us
    pallas_call x1, Pallas kernels, body(): pl.pallas_call(merge_kernel, grid=(tiles,), in_specs=[tiled(TILE, width),...  19 us
    dot_general x1, matrix products, t_mm(): lax.dot_general(left, right, (((0,), (0,)), ((), ())), preferred_element_...  12.3 us
    pallas_call x1, Pallas kernels, body(): pl.pallas_call(qkv_grad_kernel, grid=(3,), in_specs=[fixed((count, width)...  10.2 us
    unnamed x29, local copies, waits for them, and re-layouts  8.09 us

profile of v5, /device:TPU:0, one launch (start us, length us, event | category | flops | bytes accessed | tf_op | source)
XLA Modules:
  0.0 399.5 jit_solution(12073108710668057123)
XLA Ops:
  1.3 0.7 dynamic_slice.3
  2.1 0.7 compare_convert_fusion.1
  3.2 0.7 lt.147
  4.1 1.3 maximum_maximum_fusion.1.refs_8_
  5.5 0.7 fusion.32
  6.2 0.7 broadcast_compare_fusion
  7.1 6.1 %concatenate.23 = bf16[6144]{0:T(1024)(128)(2,1)S(1)} concatenate(bf16[24]{0:T(256)(128)(2,1)} %param.32, bf16[24]{0:T(256)(128)(2,1)} %param.33, bf16[24]{0:T(256)(128)(2,1)} %param.34, bf16[24]{0:T(256)(128)(2,1)} %param.38, bf16[24]{0:T(256)(128)(2,1)} %param.39, bf16[24]{0:T(256)(128)(2,1)} %param.40, bf16[24]{0:T(256)(128)(2,1)} %param.29, bf16[24]{0:T(256)(128)(2,1)} %param.30, ...), dimensions={0} | concatenate | bytes 24576 | tf_op jit(solution)/shard_map/concatenate | solution.py:794
  13.2 0.6 convert_element_type.84.refs_2_
  13.8 0.8 broadcast_in_dim.52
  15.0 0.7 and_convert_fusion.live_row.refs_4_
  16.4 1.0 fusion.1.live_col.refs_5_
  17.7 1.1 and_select_fusion.refs_3_
  18.8 45.9 %gather_first.1 = (bf16[4,2,2,2,24,2304]{5,4,3,2,1,0:T(8,128)(2,1)}, bf16[4,2,2,2,24,768]{5,4,3,2,1,0:T(8,128)(2,1)}, bf16[4,2,2,2,8,768]{5,4,3,2,1,0:T(8,128)(2,1)}) custom-call(bf16[24,2304]{1,0:T(8,128)(2,1)} %refs_0_.1, bf16[24,768]{1,0:T(8,128)(2,1)} %refs_1_.1, bf16[8,768]{1,0:T(8,128)(2,1)} %convert_element_type.84.refs_2_), custom_call_target="tpu_custom_call" | custom-call | tf_op jit(solution)/shard_map/gather_first/pallas_call | solution.py:739
  64.7 1.1 slice.203
  66.8 0.6 fusion.6.qkv_bias
  67.4 0.7 fusion.2.vecs
  68.1 19.0 %merge_qkv.1 = (bf16[1536,768]{1,0:T(8,128)(2,1)}, f32[1536,768]{1,0:T(8,128)}, bf16[1536,768]{1,0:T(8,128)(2,1)}, bf16[1536,2304]{1,0:T(8,128)(2,1)}, f32[8,768]{1,0:T(8,128)}) custom-call(bf16[1536,768]{1,0:T(8,128)(2,1)} %bitcast.92, f32[6,1,256]{2,1,0:T(1,128)} %and_convert_fusion.live_row.refs_4_, f32[1536,1]{1,0:T(8,128)} %fusion.1.live_col.refs_5_, ...), custom_call_target="tpu_custom_call" | custom-call | tf_op jit(solution)/shard_map/merge_qkv/pallas_call | solution.py:859
  87.1 0.7 slice.178
  87.9 70.3 %attention_gather.1 = (bf16[3,512,768]{2,1,0:T(8,128)(2,1)}, f32[3,6,2,512]{3,2,1,0:T(2,128)}, bf16[4,2,2,2,24,3072]{5,4,3,2,1,0:T(8,128)(2,1)}, bf16[4,2,2,2,96...) custom-call(bf16[3,512,2304]{2,1,0:T(8,128)(2,1)} %bitcast.80, ...), custom_call_target="tpu_custom_call" | custom-call | tf_op jit(solution)/shard_map/attention_gather/pallas_call | solution.py:739
  158.2 0.7 slice.206
  158.9 0.7 slice.225
  159.9 1.9 convolution_bitcast_fusion.1
  161.7 0.6 reshape.446.cls_grad
  162.3 53.9 %ffn.1 = (bf16[1536,768]{1,0:T(8,128)(2,1)}, bf16[1536,3072]{1,0:T(8,128)(2,1)}, bf16[1536,3072]{1,0:T(8,128)(2,1)}, bf16[1536,768]{1,0:T(8,128)(2,1)}, bf16[153...) custom-call(bf16[1536,768]{1,0:T(8,128)(2,1)} %bitcast.90, ...), custom_call_target="tpu_custom_call" | custom-call | tf_op jit(solution)/shard_map/ffn/pallas_call | solution.py:965
  216.3 0.9 fusion.5
  217.3 0.8 slice.214
  218.3 0.7 compare_select_fusion
  218.9 0.6 pad.14.refs_10_
  219.6 0.7 slice.179
  220.3 0.8 convert.48
  221.2 0.7 maximum_maximum_fusion.refs_10_
  222.4 12.3 %convolution_convert_fusion = bf16[3072,768]{1,0:T(8,128)(2,1)} fusion(bf16[1536,3072]{1,0:T(8,128)(2,1)} %get-tuple-element.73, bf16[1536,768]{1,0:T(8,128)(2,1)} %get-tuple-element.74), kind=kOutput, calls=%fused_computation | convolution fusion | flops 7250116608 | bytes 16515072 | tf_op jit(solution)/shard_map/dot_general | solution.py:32
  234.7 87.4 %attention_back_scatter.1 = (bf16[3,3,512,768]{3,2,1,0:T(8,128)(2,1)}, bf16[2,2,8,768]{3,2,1,0:T(8,128)(2,1)}, f32[96,768]{1,0:T(8,128)}, f32[24,3072]{1,0:T(8,128)}, f32[24,768]{1,0:T(8,128)}) custom-call(bf16[3,512,2304]{2,1,0:T(8,128)(2,1)} %bitcast.83, bf16[3,512,2304]{2,1,0:T(8,128)(2,1)} %bitcast.84, bf16[3,512,2304]{2,1,0:T(8,128)(2,1)} %bitcast.85, ...), custom_call_target="tpu_custom_call" | custom-call | tf_op jit(solution)/shard_map/attention_back_scatter/pallas_call | solution.py:739
  322.1 0.8 slice.224
  322.9 1.1 convolution_bitcast_fusion
  324.1 10.2 %qkv_grad.1 = (bf16[768,2304]{1,0:T(8,128)(2,1)}, f32[8,2304]{1,0:T(8,128)}) custom-call(bf16[1536,768]{1,0:T(8,128)(2,1)} %get-tuple-element.78.attn_in, bf16[3,1536,768]{2,1,0:T(8,128)(2,1)} %bitcast.86), custom_call_target="tpu_custom_call" | custom-call | tf_op jit(solution)/shard_map/qkv_grad/pallas_call | solution.py:1057
  334.3 0.9 convert.49
  335.6 0.8 copy.76
  336.4 50.9 %merge_back_scatter.1 = (bf16[1536,768]{1,0:T(8,128)(2,1)}, f32[24,2304]{1,0:T(8,128)}, f32[8,768]{1,0:T(8,128)}, f32[24,768]{1,0:T(8,128)}, f32[8,768]{1,0:T(8,128)}) custom-call(bf16[3,1536,768]{2,1,0:T(8,128)(2,1)} %bitcast.87, f32[1536,768]{1,0:T(8,128)} %get-tuple-element.76.refs_1_, bf16[1536,768]{1,0:T(8,128)(2,1)} %bitcast.93, ...), custom_call_target="tpu_custom_call" | custom-call | tf_op jit(solution)/shard_map/merge_back_scatter/pallas_call | solution.py:739
  387.3 0.9 slice_reduce_fusion
  390.0 1.3 slice_bitcast_fusion.3
  391.2 1.5 slice_bitcast_fusion
  392.8 3.3 copy.97
  396.1 0.6 copy.98
  396.7 0.7 copy.99
  397.4 0.6 copy.100
  398.1 0.7 copy.101
  398.8 0.7 copy.102
  (87 shorter events, 5.8 us)
Async XLA Ops:
  0.7 17.0 %copy-start.6 = (s32[3]{0:T(128)S(1)}, s32[3]{0:T(128)}, u32[]{:S(2)}) copy-start(s32[3]{0:T(128)} %param.23) | copy-start | bytes 40
  87.9 71.9 %copy-start.7 = (f32[3,128]{1,0:T(4,128)S(1)}, f32[3,128]{1,0:T(4,128)}, u32[]{:S(2)}) copy-start(f32[3,128]{1,0:T(4,128)} %param.43) | copy-start | bytes 4612
  162.3 55.7 %copy-start = (bf16[2,2,768,128]{3,2,1,0:T(8,128)(2,1)S(1)}, bf16[2,2,768,128]{3,2,1,0:T(8,128)(2,1)}, u32[]{:S(2)}) copy-start(bf16[2,2,768,128]{3,2,1,0:T(8,128)(2,1)} %get-tuple-element.63) | copy-start | bytes 2359300
  392.7 3.3 copy-start.5
  392.8 4.0 copy-start.3
  392.8 4.7 %copy-start.4 = (f32[24,768]{1,0:T(8,128)S(1)}, f32[24,768]{1,0:T(8,128)}, u32[]{:S(2)}) copy-start(f32[24,768]{1,0:T(8,128)} %get-tuple-element.164) | copy-start | bytes 221188
  392.8 5.3 %copy-start.2 = (f32[24,3072]{1,0:T(8,128)S(1)}, f32[24,3072]{1,0:T(8,128)}, u32[]{:S(2)}) copy-start(f32[24,3072]{1,0:T(8,128)} %get-tuple-element.168) | copy-start | bytes 884740
  392.8 6.0 %copy-start.1 = (f32[96,768]{1,0:T(8,128)S(1)}, f32[96,768]{1,0:T(8,128)}, u32[]{:S(2)}) copy-start(f32[96,768]{1,0:T(8,128)} %get-tuple-element.170) | copy-start | bytes 884740

commit v6 on v5

--- a/solution.py
+++ b/solution.py
@@ -306,7 +306,7 @@
 MESH = pl.DeviceIdType.MESH
 TABLE_MAJOR = 4
 UP_CUTS = 6
-ATTN_PACE, BACK_PACE, LAST_PACE = 3.0, 2.4, 2.5
+ATTN_PACE, BACK_PACE, LAST_PACE = 3.0, 2.7, 2.5
 CORES = 2
 
 

time: 401 us -> 400 us (level)
  no operation moved by 1% of the time
where the time goes in v6:
time: 400 us; the launch traced here: 399 us
  Pallas kernels  337 us (84%)
  local copies, waits for them, and re-layouts  31.8 us (8%)
  matrix products  15.5 us (4%)
  other arithmetic  12.2 us (3%)
    pallas_call x4, Pallas kernels, moving_call(): pl.pallas_call(fused, grid=grid, in_specs=in_specs, out_specs=out_specs,...  254 us
    pallas_call x1, Pallas kernels, body(): pl.pallas_call(functools.partial(ffn_kernel, per_row), grid=(tiles,), in_...  53.9 us
    pallas_call x1, Pallas kernels, body(): pl.pallas_call(merge_kernel, grid=(tiles,), in_specs=[tiled(TILE, width),...  19 us
    dot_general x1, matrix products, t_mm(): lax.dot_general(left, right, (((0,), (0,)), ((), ())), preferred_element_...  12.3 us
    pallas_call x1, Pallas kernels, body(): pl.pallas_call(qkv_grad_kernel, grid=(3,), in_specs=[fixed((count, width)...  10.2 us
    unnamed x29, local copies, waits for them, and re-layouts  8.09 us

profile of v6, /device:TPU:0, one launch (start us, length us, event | category | flops | bytes accessed | tf_op | source)
XLA Modules:
  0.0 398.9 jit_solution(3741919251470378757)
XLA Ops:
  1.3 0.7 dynamic_slice.3
  2.1 0.7 compare_convert_fusion.1
  3.2 0.7 lt.147
  4.1 1.3 maximum_maximum_fusion.1.refs_8_
  5.5 0.7 fusion.32
  6.2 0.7 broadcast_compare_fusion
  7.1 6.1 %concatenate.23 = bf16[6144]{0:T(1024)(128)(2,1)S(1)} concatenate(bf16[24]{0:T(256)(128)(2,1)} %param.32, bf16[24]{0:T(256)(128)(2,1)} %param.33, bf16[24]{0:T(256)(128)(2,1)} %param.34, bf16[24]{0:T(256)(128)(2,1)} %param.38, bf16[24]{0:T(256)(128)(2,1)} %param.39, bf16[24]{0:T(256)(128)(2,1)} %param.40, bf16[24]{0:T(256)(128)(2,1)} %param.29, bf16[24]{0:T(256)(128)(2,1)} %param.30, ...), dimensions={0} | concatenate | bytes 24576 | tf_op jit(solution)/shard_map/concatenate | solution.py:794
  13.2 0.6 convert_element_type.84.refs_2_
  13.8 0.8 broadcast_in_dim.52
  15.0 0.7 and_convert_fusion.live_row.refs_4_
  16.4 1.0 fusion.1.live_col.refs_5_
  17.7 1.1 and_select_fusion.refs_3_
  18.8 45.9 %gather_first.1 = (bf16[4,2,2,2,24,2304]{5,4,3,2,1,0:T(8,128)(2,1)}, bf16[4,2,2,2,24,768]{5,4,3,2,1,0:T(8,128)(2,1)}, bf16[4,2,2,2,8,768]{5,4,3,2,1,0:T(8,128)(2,1)}) custom-call(bf16[24,2304]{1,0:T(8,128)(2,1)} %refs_0_.1, bf16[24,768]{1,0:T(8,128)(2,1)} %refs_1_.1, bf16[8,768]{1,0:T(8,128)(2,1)} %convert_element_type.84.refs_2_), custom_call_target="tpu_custom_call" | custom-call | tf_op jit(solution)/shard_map/gather_first/pallas_call | solution.py:739
  64.7 1.1 slice.203
  66.8 0.6 fusion.6.qkv_bias
  67.4 0.7 fusion.2.vecs
  68.1 19.0 %merge_qkv.1 = (bf16[1536,768]{1,0:T(8,128)(2,1)}, f32[1536,768]{1,0:T(8,128)}, bf16[1536,768]{1,0:T(8,128)(2,1)}, bf16[1536,2304]{1,0:T(8,128)(2,1)}, f32[8,768]{1,0:T(8,128)}) custom-call(bf16[1536,768]{1,0:T(8,128)(2,1)} %bitcast.92, f32[6,1,256]{2,1,0:T(1,128)} %and_convert_fusion.live_row.refs_4_, f32[1536,1]{1,0:T(8,128)} %fusion.1.live_col.refs_5_, ...), custom_call_target="tpu_custom_call" | custom-call | tf_op jit(solution)/shard_map/merge_qkv/pallas_call | solution.py:859
  87.1 0.7 slice.178
  87.9 70.3 %attention_gather.1 = (bf16[3,512,768]{2,1,0:T(8,128)(2,1)}, f32[3,6,2,512]{3,2,1,0:T(2,128)}, bf16[4,2,2,2,24,3072]{5,4,3,2,1,0:T(8,128)(2,1)}, bf16[4,2,2,2,96...) custom-call(bf16[3,512,2304]{2,1,0:T(8,128)(2,1)} %bitcast.80, ...), custom_call_target="tpu_custom_call" | custom-call | tf_op jit(solution)/shard_map/attention_gather/pallas_call | solution.py:739
  158.2 0.7 slice.206
  158.9 0.7 slice.225
  159.9 1.9 convolution_bitcast_fusion.1
  161.7 0.6 reshape.446.cls_grad
  162.3 53.9 %ffn.1 = (bf16[1536,768]{1,0:T(8,128)(2,1)}, bf16[1536,3072]{1,0:T(8,128)(2,1)}, bf16[1536,3072]{1,0:T(8,128)(2,1)}, bf16[1536,768]{1,0:T(8,128)(2,1)}, bf16[153...) custom-call(bf16[1536,768]{1,0:T(8,128)(2,1)} %bitcast.90, ...), custom_call_target="tpu_custom_call" | custom-call | tf_op jit(solution)/shard_map/ffn/pallas_call | solution.py:965
  216.3 0.9 fusion.5
  217.3 0.8 slice.214
  218.3 0.7 compare_select_fusion
  218.9 0.6 pad.14.refs_10_
  219.6 0.7 slice.179
  220.3 0.8 convert.48
  221.2 0.7 maximum_maximum_fusion.refs_10_
  222.4 12.3 %convolution_convert_fusion = bf16[3072,768]{1,0:T(8,128)(2,1)} fusion(bf16[1536,3072]{1,0:T(8,128)(2,1)} %get-tuple-element.73, bf16[1536,768]{1,0:T(8,128)(2,1)} %get-tuple-element.74), kind=kOutput, calls=%fused_computation | convolution fusion | flops 7250116608 | bytes 16515072 | tf_op jit(solution)/shard_map/dot_general | solution.py:32
  234.7 86.9 %attention_back_scatter.1 = (bf16[3,3,512,768]{3,2,1,0:T(8,128)(2,1)}, bf16[2,2,8,768]{3,2,1,0:T(8,128)(2,1)}, f32[96,768]{1,0:T(8,128)}, f32[24,3072]{1,0:T(8,128)}, f32[24,768]{1,0:T(8,128)}) custom-call(bf16[3,512,2304]{2,1,0:T(8,128)(2,1)} %bitcast.83, bf16[3,512,2304]{2,1,0:T(8,128)(2,1)} %bitcast.84, bf16[3,512,2304]{2,1,0:T(8,128)(2,1)} %bitcast.85, ...), custom_call_target="tpu_custom_call" | custom-call | tf_op jit(solution)/shard_map/attention_back_scatter/pallas_call | solution.py:739
  321.7 0.8 slice.224
  322.5 1.1 convolution_bitcast_fusion
  323.6 10.2 %qkv_grad.1 = (bf16[768,2304]{1,0:T(8,128)(2,1)}, f32[8,2304]{1,0:T(8,128)}) custom-call(bf16[1536,768]{1,0:T(8,128)(2,1)} %get-tuple-element.78.attn_in, bf16[3,1536,768]{2,1,0:T(8,128)(2,1)} %bitcast.86), custom_call_target="tpu_custom_call" | custom-call | tf_op jit(solution)/shard_map/qkv_grad/pallas_call | solution.py:1057
  333.9 0.9 convert.49
  335.1 0.8 copy.76
  336.0 50.8 %merge_back_scatter.1 = (bf16[1536,768]{1,0:T(8,128)(2,1)}, f32[24,2304]{1,0:T(8,128)}, f32[8,768]{1,0:T(8,128)}, f32[24,768]{1,0:T(8,128)}, f32[8,768]{1,0:T(8,128)}) custom-call(bf16[3,1536,768]{2,1,0:T(8,128)(2,1)} %bitcast.87, f32[1536,768]{1,0:T(8,128)} %get-tuple-element.76.refs_1_, bf16[1536,768]{1,0:T(8,128)(2,1)} %bitcast.93, ...), custom_call_target="tpu_custom_call" | custom-call | tf_op jit(solution)/shard_map/merge_back_scatter/pallas_call | solution.py:739
  386.7 0.9 slice_reduce_fusion
  389.4 1.3 slice_bitcast_fusion.3
  390.6 1.5 slice_bitcast_fusion
  392.2 3.3 copy.97
  395.5 0.6 copy.98
  396.1 0.7 copy.99
  396.8 0.6 copy.100
  397.4 0.7 copy.101
  398.2 0.7 copy.102
  (87 shorter events, 5.8 us)
Async XLA Ops:
  0.7 17.0 %copy-start.6 = (s32[3]{0:T(128)S(1)}, s32[3]{0:T(128)}, u32[]{:S(2)}) copy-start(s32[3]{0:T(128)} %param.23) | copy-start | bytes 40
  87.9 71.9 %copy-start.7 = (f32[3,128]{1,0:T(4,128)S(1)}, f32[3,128]{1,0:T(4,128)}, u32[]{:S(2)}) copy-start(f32[3,128]{1,0:T(4,128)} %param.43) | copy-start | bytes 4612
  162.3 55.7 %copy-start = (bf16[2,2,768,128]{3,2,1,0:T(8,128)(2,1)S(1)}, bf16[2,2,768,128]{3,2,1,0:T(8,128)(2,1)}, u32[]{:S(2)}) copy-start(bf16[2,2,768,128]{3,2,1,0:T(8,128)(2,1)} %get-tuple-element.63) | copy-start | bytes 2359300
  392.1 3.3 copy-start.5
  392.1 4.0 copy-start.3
  392.1 4.7 %copy-start.4 = (f32[24,768]{1,0:T(8,128)S(1)}, f32[24,768]{1,0:T(8,128)}, u32[]{:S(2)}) copy-start(f32[24,768]{1,0:T(8,128)} %get-tuple-element.164) | copy-start | bytes 221188
  392.2 5.3 %copy-start.2 = (f32[24,3072]{1,0:T(8,128)S(1)}, f32[24,3072]{1,0:T(8,128)}, u32[]{:S(2)}) copy-start(f32[24,3072]{1,0:T(8,128)} %get-tuple-element.168) | copy-start | bytes 884740
  392.2 6.0 %copy-start.1 = (f32[96,768]{1,0:T(8,128)S(1)}, f32[96,768]{1,0:T(8,128)}, u32[]{:S(2)}) copy-start(f32[96,768]{1,0:T(8,128)} %get-tuple-element.170) | copy-start | bytes 884740
